TPU v7x, 32 devices: a whole 2x2x4 slice. The times are simulated.
32 devices in a mesh: page: 16 (over z, y, core), win: 2 (over x).
Axes of the slice: x: 2, y: 2, z: 4, core: 2. Of those that a mesh axis runs over, the one named last changes fastest.
Arguments:
- visual_in: bfloat16 [16, 24, 48, 768], P('page', 'win'), may hold values from -6 to 6
- text_in: bfloat16 [16, 400, 768], P('page'), may hold values from -6 to 6
- highlight: int32 [16, 24, 48], P('page', 'win'), may hold values from 0 to 1, as said below
- text_mask: int32 [16, 400], P('page'), may hold values 0 or 1
- window_proj: bfloat16 [768, 2304], replicated, may hold values from -0.21875 to 0.21875
- window_out: bfloat16 [768, 768], replicated, may hold values from -1.5 to 1.5
- visual_up: bfloat16 [768, 3072], replicated, may hold values from -0.21875 to 0.21875
- visual_down: bfloat16 [3072, 768], replicated, may hold values from -0.109375 to 0.109375
- text_query: bfloat16 [768, 768], replicated, may hold values from -0.21875 to 0.21875
- keyval_proj: bfloat16 [768, 1536], replicated, may hold values from -0.21875 to 0.21875
- cross_out: bfloat16 [768, 768], replicated, may hold values from -6 to 6
- text_up: bfloat16 [768, 3072], replicated, may hold values from -0.21875 to 0.21875
- text_down: bfloat16 [3072, 768], replicated, may hold values from -0.109375 to 0.109375
- norm_window: float32 [768], replicated, may hold values from 0.1 to 1.9
- norm_visual: float32 [768], replicated, may hold values from 0.1 to 1.9
- norm_text: float32 [768], replicated, may hold values from 0.1 to 1.9
- norm_pages: float32 [768], replicated, may hold values from 0.1 to 1.9
- norm_reply: float32 [768], replicated, may hold values from 0.1 to 1.9
- highlight_embed: float32 [768], replicated, may hold values from -6 to 6
- visual_upstream: bfloat16 [16, 24, 48, 768], P('page', 'win'), may hold values from -6 to 6
- text_upstream: bfloat16 [16, 400, 768], P('page', 'win'), may hold values from -6 to 6
Outputs:
- visual_out: bfloat16 [16, 24, 48, 768], P('page', 'win')
- text_out: bfloat16 [16, 400, 768], P('page', 'win')
- visual_grad: float32 [16, 24, 48, 768], P('page', 'win')
- text_grad: float32 [16, 400, 768], P('page', 'win')
- window_proj_grad: float32 [768, 2304], P('page')
- window_out_grad: float32 [768, 768], P('page')
- visual_up_grad: float32 [768, 3072], P('page')
- visual_down_grad: float32 [3072, 768], P('page')
- text_query_grad: float32 [768, 768], P('page')
- keyval_grad: float32 [768, 1536], P('page')
- cross_out_grad: float32 [768, 768], P('page')
- text_up_grad: float32 [768, 3072], P('page')
- text_down_grad: float32 [3072, 768], P('page')
- norm_window_grad: float32 [768], P('page')
- norm_visual_grad: float32 [768], P('page')
- norm_text_grad: float32 [768], P('page')
- norm_pages_grad: float32 [768], P('page')
- norm_reply_grad: float32 [768], P('page')
- highlight_embed_grad: float32 [768], P('page')
Inputs may be any that keep to these rules, and one draw needn't show every extreme that they name: `highlight`: each page's mask is either all zeros or marks some of its patches.
All inputs are finite; a program needn't handle non-finite values. No bound on the sum of `text_mask` on one device may be relied on, other than what follows from the above.
Results may differ from a plain program's by a relative error of at most 0.019.
Values may be sent and summed in bfloat16 or wider, within the bound.
No kernel may reach another device: no remote copies, remote signals or barrier semaphores. Data moves between devices by JAX's collectives and lax.ppermute only.
A program may use at most 256 MiB of HBM per device.

v0:
```python
import jax
import jax.numpy as jnp
from jax import lax
from jax.sharding import PartitionSpec as P

D = 768
HEADS = 12
HEAD_DIM = 64
WIN = 12
SHIFT = 6
WIN_ROW = 4
PAGE_QUERY_COUNT = 400


epsilon = 1e-05
masked_score = -1e30


def shifted_2(shard, axis, by):
    count = lax.axis_size(axis)
    return lax.ppermute(shard, axis, [(i, (i + by) % count) for i in range(count)])


def layer_norm(stream, norm_gain):
    center = stream - jnp.mean(stream, -1, keepdims=True)
    spread = jnp.mean(center * center, -1, keepdims=True)
    return center * lax.rsqrt(spread + epsilon) * norm_gain


def norm_back(stream, norm_gain, upstream):
    _, pullback = jax.vjp(lambda inner_part: layer_norm(inner_part, norm_gain), stream)
    center = stream - jnp.mean(stream, -1, keepdims=True)
    spread = jnp.mean(center * center, -1, keepdims=True)
    return (pullback(upstream)[0], upstream * center * lax.rsqrt(spread + epsilon))


def column_total(gain_terms):
    return jnp.sum(gain_terms.reshape(-1, gain_terms.shape[-1]), 0)


def matmul(left_side, right_side):
    flattened = left_side.reshape(-1, left_side.shape[-1])
    result = jnp.dot(flattened, right_side, preferred_element_type=jnp.float32)
    return result.reshape(left_side.shape[:-1] + (right_side.shape[-1],))


def matmul_back(gradient, right_side):
    flattened = gradient.reshape(-1, gradient.shape[-1])
    result = lax.dot_general(
        flattened, right_side, (((1,), (1,)), ((), ())), preferred_element_type=jnp.float32
    )
    return result.reshape(gradient.shape[:-1] + (right_side.shape[0],))


def weight_grad(left_side, gradient):
    return lax.dot_general(
        left_side.reshape(-1, left_side.shape[-1]),
        gradient.reshape(-1, gradient.shape[-1]),
        (((0,), (0,)), ((), ())),
        preferred_element_type=jnp.float32,
    )


def gelu_exact(hidden):
    return jax.nn.gelu(hidden, approximate=False)


def unchanged(tensor):
    return tensor


def feed_forward(stream, norm_gain, upward, downward):
    normed = layer_norm(stream, norm_gain).astype(jnp.bfloat16)
    hidden = matmul(normed, upward)
    active = gelu_exact(hidden).astype(jnp.bfloat16)
    return (stream + matmul(active, downward), (normed, hidden, active))


def feed_back(stream, norm_gain, upward, downward, saved, upstream, keep_rows):
    normed, hidden, active = saved
    out_grad = upstream.astype(jnp.bfloat16)
    down_grad = weight_grad(keep_rows(active), keep_rows(out_grad))
    _, pullback = jax.vjp(gelu_exact, hidden)
    hidden_grad = pullback(matmul_back(out_grad, downward))[0].astype(jnp.bfloat16)
    up_grad = weight_grad(keep_rows(normed), keep_rows(hidden_grad))
    stream_grad, gain_terms = norm_back(stream, norm_gain, matmul_back(hidden_grad, upward))
    return (upstream + stream_grad, column_total(keep_rows(gain_terms)), up_grad, down_grad)


def windows_of(tensor):
    page_count, channels = (tensor.shape[0], tensor.shape[-1])
    tensor = tensor.reshape(page_count, WIN, WIN_ROW, WIN, channels).transpose(0, 2, 1, 3, 4)
    return tensor.reshape(page_count, WIN_ROW, WIN * WIN, channels)


def windows_back(tensor):
    page_count, channels = (tensor.shape[0], tensor.shape[-1])
    tensor = tensor.reshape(page_count, WIN_ROW, WIN, WIN, channels).transpose(0, 2, 1, 3, 4)
    return tensor.reshape(page_count, WIN, WIN * WIN_ROW, channels)


def window_scores(win_queries, win_keys):
    score_scale = HEAD_DIM ** (-0.5)
    return (
        jnp.einsum("pwqhe,pwkhe->pwhqk", win_queries, win_keys, preferred_element_type=jnp.float32)
        * score_scale
    )


def split_heads(key_value):
    key_heads = key_value[:, :D].reshape(-1, HEADS, HEAD_DIM)
    value_heads = key_value[:, D:].reshape(-1, HEADS, HEAD_DIM)
    return (key_heads, value_heads)


def cross_scores(queries, page_kv, text_kv, permitted_mask):
    score_scale = HEAD_DIM ** (-0.5)
    page_keys, _ = split_heads(page_kv)
    text_keys, _ = split_heads(text_kv)
    page_part = (
        jnp.einsum("qhe,khe->hqk", queries, page_keys, preferred_element_type=jnp.float32)
        * score_scale
    )
    text_part = (
        jnp.einsum("qhe,khe->hqk", queries, text_keys, preferred_element_type=jnp.float32)
        * score_scale
    )
    return (page_part, jnp.where(permitted_mask[None], text_part, masked_score))


def cross_stats(inputs):
    queries, page_kv, text_kv, permitted_mask = inputs
    page_part, text_part = cross_scores(queries, page_kv, text_kv, permitted_mask)
    row_peak = jnp.maximum(
        jnp.max(page_part, -1, keepdims=True), jnp.max(text_part, -1, keepdims=True)
    )
    row_total = jnp.sum(jnp.exp(page_part - row_peak), -1, keepdims=True) + jnp.sum(
        jnp.exp(text_part - row_peak), -1, keepdims=True
    )
    return (row_peak, row_total, page_part, text_part)


def cross_weighted(inputs):
    page_part, text_part, cross_log, page_kv, text_kv = inputs
    _, page_values = split_heads(page_kv)
    _, text_values = split_heads(text_kv)
    page_attend = jnp.exp(page_part - cross_log).astype(jnp.bfloat16)
    text_attend = jnp.exp(text_part - cross_log).astype(jnp.bfloat16)
    context = jnp.einsum(
        "hqk,khe->qhe", page_attend, page_values, preferred_element_type=jnp.float32
    )
    return context + jnp.einsum(
        "hqk,khe->qhe", text_attend, text_values, preferred_element_type=jnp.float32
    )


def cross_forward(inputs):
    queries, page_kv, text_kv, permitted_mask = inputs
    row_peak, row_total, page_part, text_part = cross_stats(inputs)
    cross_log = row_peak + jnp.log(row_total)
    context = cross_weighted((page_part, text_part, cross_log, page_kv, text_kv))
    return (cross_log, context.astype(jnp.bfloat16))


def cross_terms(queries, page_kv, text_kv, permitted_mask, cross_log, context_grad):
    page_part, text_part = cross_scores(queries, page_kv, text_kv, permitted_mask)
    _, page_values = split_heads(page_kv)
    _, text_values = split_heads(text_kv)
    page_exact = jnp.exp(page_part - cross_log)
    text_exact = jnp.exp(text_part - cross_log)
    page_dprob = jnp.einsum(
        "qhe,khe->hqk", context_grad, page_values, preferred_element_type=jnp.float32
    )
    text_dprob = jnp.einsum(
        "qhe,khe->hqk", context_grad, text_values, preferred_element_type=jnp.float32
    )
    return (page_exact, text_exact, page_dprob, text_dprob)


def cross_row_dot(inputs):
    page_exact, text_exact, page_dprob, text_dprob = cross_terms(*inputs)
    return jnp.sum(page_dprob * page_exact, -1, keepdims=True) + jnp.sum(
        text_dprob * text_exact, -1, keepdims=True
    )


def cross_grads(inputs):
    queries, page_kv, text_kv, permitted_mask, cross_log, context_grad, row_dot = inputs
    score_scale = HEAD_DIM ** (-0.5)
    page_exact, text_exact, page_dprob, text_dprob = cross_terms(
        queries, page_kv, text_kv, permitted_mask, cross_log, context_grad
    )
    page_keys, _ = split_heads(page_kv)
    text_keys, _ = split_heads(text_kv)
    page_dscore = (page_exact * (page_dprob - row_dot)).astype(jnp.bfloat16)
    text_dscore = (text_exact * (text_dprob - row_dot)).astype(jnp.bfloat16)
    query_grad = jnp.einsum(
        "hqk,khe->qhe", page_dscore, page_keys, preferred_element_type=jnp.float32
    )
    query_grad = (
        query_grad
        + jnp.einsum("hqk,khe->qhe", text_dscore, text_keys, preferred_element_type=jnp.float32)
    ) * score_scale
    page_key_grad = (
        jnp.einsum("hqk,qhe->khe", page_dscore, queries, preferred_element_type=jnp.float32)
        * score_scale
    )
    page_value_grad = jnp.einsum(
        "hqk,qhe->khe",
        page_exact.astype(jnp.bfloat16),
        context_grad,
        preferred_element_type=jnp.float32,
    )
    text_key_grad = (
        jnp.einsum("hqk,qhe->khe", text_dscore, queries, preferred_element_type=jnp.float32)
        * score_scale
    )
    text_value_gradient = jnp.einsum(
        "hqk,qhe->khe",
        text_exact.astype(jnp.bfloat16),
        context_grad,
        preferred_element_type=jnp.float32,
    )
    page_grad = jnp.concatenate([page_key_grad.reshape(-1, D), page_value_grad.reshape(-1, D)], -1)
    text_grad = jnp.concatenate(
        [text_key_grad.reshape(-1, D), text_value_gradient.reshape(-1, D)], -1
    )
    return (query_grad, page_grad, text_grad)


def cross_backward(inputs):
    row_dot = cross_row_dot(inputs)
    return cross_grads(tuple(inputs) + (row_dot,))


def shards(
    visual_in,
    text_in,
    highlight,
    text_mask,
    window_proj,
    window_out,
    visual_up,
    visual_down,
    text_query,
    keyval_proj,
    cross_out,
    text_up,
    text_down,
    norm_window,
    norm_visual,
    norm_text,
    norm_pages,
    norm_reply,
    highlight_embed,
    visual_upstream,
    text_upstream,
):
    page_count = visual_in.shape[0]
    score_scale = HEAD_DIM ** (-0.5)
    win_index = lax.axis_index("win")
    own_count = text_upstream.shape[1]

    def own_rows(tensor):
        return lax.dynamic_slice_in_dim(tensor, win_index * own_count, own_count, 1)

    stream = (
        visual_in.astype(jnp.float32) + highlight[..., None].astype(jnp.float32) * highlight_embed
    )
    normed = layer_norm(stream, norm_window).astype(jnp.bfloat16)
    rows_ahead = shifted_2(normed[:, :SHIFT], "win", -1)
    shifted = jnp.roll(jnp.concatenate([normed[:, SHIFT:], rows_ahead], 1), -SHIFT, 2)
    packed = windows_of(matmul(shifted, window_proj).astype(jnp.bfloat16))
    heads_shape = packed.shape[:3] + (HEADS, HEAD_DIM)
    win_queries = packed[..., :D].reshape(heads_shape)
    win_keys = packed[..., D : 2 * D].reshape(heads_shape)
    win_values = packed[..., 2 * D :].reshape(heads_shape)
    first_scores = window_scores(win_queries, win_keys)
    win_log = jax.nn.logsumexp(first_scores, -1, keepdims=True)
    win_attend = jnp.exp(first_scores - win_log).astype(jnp.bfloat16)
    win_context = jnp.einsum(
        "pwhqk,pwkhe->pwqhe", win_attend, win_values, preferred_element_type=jnp.float32
    ).astype(jnp.bfloat16)
    rolled = jnp.roll(windows_back(win_context.reshape(packed.shape[:3] + (D,))), SHIFT, 2)
    rows_behind = shifted_2(rolled[:, SHIFT:], "win", 1)
    unshifted = jnp.concatenate([rows_behind, rolled[:, :SHIFT]], 1)
    visual_mid = stream + matmul(unshifted, window_out)
    visual_final, visual_saved = feed_forward(visual_mid, norm_visual, visual_up, visual_down)
    pages_normed = layer_norm(visual_final, norm_pages).astype(jnp.bfloat16)
    local_kv = matmul(pages_normed, keyval_proj).astype(jnp.bfloat16).reshape(page_count, -1, 2 * D)
    text_stream = text_in.astype(jnp.float32)
    text_normed = layer_norm(text_stream, norm_text).astype(jnp.bfloat16)
    text_kv = matmul(text_normed, keyval_proj).astype(jnp.bfloat16)
    first_row = win_index * own_count
    work_upstream = text_upstream.astype(jnp.float32)
    rows_stream = own_rows(text_stream)
    rows_normed = own_rows(text_normed)
    text_queries = matmul(rows_normed, text_query).astype(jnp.bfloat16)
    row_count = text_queries.shape[1]
    row_ids = first_row + jnp.arange(row_count)[:, None]
    key_ids = jnp.arange(PAGE_QUERY_COUNT)[None, :]
    permitted_mask = (key_ids <= row_ids)[None] & (text_mask[:, None, :] == 1)
    query_heads = text_queries.reshape(page_count, row_count, HEADS, HEAD_DIM)
    page_kv = lax.all_gather(local_kv, "win", axis=1, tiled=True)
    cross_log, cross_context = lax.map(
        cross_forward, (query_heads, page_kv, text_kv, permitted_mask)
    )
    cross_flat = cross_context.reshape(page_count, row_count, D)
    text_mid = rows_stream + matmul(cross_flat, cross_out)
    text_final, text_saved = feed_forward(text_mid, norm_reply, text_up, text_down)
    text_mid_grad, reply_gain, text_up_grad, text_down_grad = feed_back(
        text_mid, norm_reply, text_up, text_down, text_saved, work_upstream, unchanged
    )
    cross_branch = text_mid_grad.astype(jnp.bfloat16)
    cross_out_grad = weight_grad(unchanged(cross_flat), unchanged(cross_branch))
    context_grad = (
        matmul_back(cross_branch, cross_out)
        .astype(jnp.bfloat16)
        .reshape(page_count, row_count, HEADS, HEAD_DIM)
    )
    query_grad, page_kv_grad, text_keyvalue_gradient = lax.map(
        cross_backward, (query_heads, page_kv, text_kv, permitted_mask, cross_log, context_grad)
    )
    query_own = query_grad.reshape(page_count, row_count, D).astype(jnp.bfloat16)
    page_kv_own, text_kv_own = (
        lax.psum_scatter(
            page_kv_grad.astype(jnp.bfloat16), "win", scatter_dimension=1, tiled=True
        ).astype(jnp.float32),
        lax.psum_scatter(
            text_keyvalue_gradient.astype(jnp.bfloat16), "win", scatter_dimension=1, tiled=True
        ).astype(jnp.float32),
    )
    page_kv_own = page_kv_own.astype(jnp.bfloat16)
    text_kv_own = text_kv_own.astype(jnp.bfloat16)
    text_query_grad = weight_grad(own_rows(text_normed), query_own)
    keyval_grad = weight_grad(own_rows(text_normed), text_kv_own) + weight_grad(
        pages_normed, page_kv_own
    )
    text_normed_grad = matmul_back(query_own, text_query) + matmul_back(text_kv_own, keyval_proj)
    text_in_grad, text_terms = norm_back(own_rows(text_stream), norm_text, text_normed_grad)
    text_grad = unchanged(text_mid_grad) + text_in_grad
    text_gain = column_total(text_terms)
    pages_grad = matmul_back(page_kv_own, keyval_proj).reshape(visual_final.shape)
    final_extra, pages_terms = norm_back(visual_final, norm_pages, pages_grad)
    pages_gain = column_total(pages_terms)
    visual_mid_grad, visual_gain, visual_up_grad, visual_down_grad = feed_back(
        visual_mid,
        norm_visual,
        visual_up,
        visual_down,
        visual_saved,
        visual_upstream.astype(jnp.float32) + final_extra,
        unchanged,
    )
    window_branch = visual_mid_grad.astype(jnp.bfloat16)
    window_out_grad = weight_grad(unshifted, window_branch)
    unshifted_grad = matmul_back(window_branch, window_out).astype(jnp.bfloat16)
    grad_later = shifted_2(unshifted_grad[:, :SHIFT], "win", -1)
    rolled_grad = jnp.concatenate([unshifted_grad[:, SHIFT:], grad_later], 1)
    win_context_grad = windows_of(jnp.roll(rolled_grad, -SHIFT, 2)).reshape(heads_shape)
    win_exact = jnp.exp(window_scores(win_queries, win_keys) - win_log)
    win_dprob = jnp.einsum(
        "pwqhe,pwkhe->pwhqk", win_context_grad, win_values, preferred_element_type=jnp.float32
    )
    row_sums = jnp.sum(win_dprob * win_exact, -1, keepdims=True)
    win_dscore = (win_exact * (win_dprob - row_sums)).astype(jnp.bfloat16)
    query_part = (
        jnp.einsum("pwhqk,pwkhe->pwqhe", win_dscore, win_keys, preferred_element_type=jnp.float32)
        * score_scale
    )
    key_part = (
        jnp.einsum(
            "pwhqk,pwqhe->pwkhe", win_dscore, win_queries, preferred_element_type=jnp.float32
        )
        * score_scale
    )
    value_part = jnp.einsum(
        "pwhqk,pwqhe->pwkhe",
        win_exact.astype(jnp.bfloat16),
        win_context_grad,
        preferred_element_type=jnp.float32,
    )
    flat_shape = packed.shape[:3] + (D,)
    packed_grad = jnp.concatenate(
        [
            query_part.reshape(flat_shape),
            key_part.reshape(flat_shape),
            value_part.reshape(flat_shape),
        ],
        -1,
    ).astype(jnp.bfloat16)
    projected_grad = windows_back(packed_grad)
    window_proj_grad = weight_grad(shifted, projected_grad)
    shifted_grad = jnp.roll(matmul_back(projected_grad, window_proj).astype(jnp.bfloat16), SHIFT, 2)
    grad_earlier = shifted_2(shifted_grad[:, SHIFT:], "win", 1)
    normed_grad = jnp.concatenate([grad_earlier, shifted_grad[:, :SHIFT]], 1)
    stream_extra, window_terms = norm_back(stream, norm_window, normed_grad.astype(jnp.float32))
    visual_grad = visual_mid_grad + stream_extra
    window_gain = column_total(window_terms)
    embed_grad = column_total(highlight[..., None].astype(jnp.float32) * visual_grad)
    all_summed = (
        lax.psum_scatter(
            window_proj_grad.astype(jnp.bfloat16), "page", scatter_dimension=0, tiled=True
        ).astype(jnp.float32),
        lax.psum_scatter(
            window_out_grad.astype(jnp.bfloat16), "page", scatter_dimension=0, tiled=True
        ).astype(jnp.float32),
        lax.psum_scatter(
            visual_up_grad.astype(jnp.bfloat16), "page", scatter_dimension=0, tiled=True
        ).astype(jnp.float32),
        lax.psum_scatter(
            visual_down_grad.astype(jnp.bfloat16), "page", scatter_dimension=0, tiled=True
        ).astype(jnp.float32),
        lax.psum_scatter(
            text_query_grad.astype(jnp.bfloat16), "page", scatter_dimension=0, tiled=True
        ).astype(jnp.float32),
        lax.psum_scatter(
            keyval_grad.astype(jnp.bfloat16), "page", scatter_dimension=0, tiled=True
        ).astype(jnp.float32),
        lax.psum_scatter(
            cross_out_grad.astype(jnp.bfloat16), "page", scatter_dimension=0, tiled=True
        ).astype(jnp.float32),
        lax.psum_scatter(
            text_up_grad.astype(jnp.bfloat16), "page", scatter_dimension=0, tiled=True
        ).astype(jnp.float32),
        lax.psum_scatter(
            text_down_grad.astype(jnp.bfloat16), "page", scatter_dimension=0, tiled=True
        ).astype(jnp.float32),
        lax.psum_scatter(
            window_gain.astype(jnp.bfloat16), "page", scatter_dimension=0, tiled=True
        ).astype(jnp.float32),
        lax.psum_scatter(
            visual_gain.astype(jnp.bfloat16), "page", scatter_dimension=0, tiled=True
        ).astype(jnp.float32),
        lax.psum_scatter(
            text_gain.astype(jnp.bfloat16), "page", scatter_dimension=0, tiled=True
        ).astype(jnp.float32),
        lax.psum_scatter(
            pages_gain.astype(jnp.bfloat16), "page", scatter_dimension=0, tiled=True
        ).astype(jnp.float32),
        lax.psum_scatter(
            reply_gain.astype(jnp.bfloat16), "page", scatter_dimension=0, tiled=True
        ).astype(jnp.float32),
        lax.psum_scatter(
            embed_grad.astype(jnp.bfloat16), "page", scatter_dimension=0, tiled=True
        ).astype(jnp.float32),
    )
    (
        window_proj_sum,
        window_out_sum,
        visual_up_sum,
        visual_down_sum,
        text_query_sum,
        keyval_sum,
        cross_out_sum,
        text_up_sum,
        text_down_sum,
        window_gain_sum,
        visual_gain_sum,
        text_gain_sum,
        pages_gain_sum,
        reply_gain_sum,
        embed_sum,
    ) = (
        lax.psum(all_summed[0].astype(jnp.bfloat16), "win").astype(jnp.float32),
        lax.psum(all_summed[1].astype(jnp.bfloat16), "win").astype(jnp.float32),
        lax.psum(all_summed[2].astype(jnp.bfloat16), "win").astype(jnp.float32),
        lax.psum(all_summed[3].astype(jnp.bfloat16), "win").astype(jnp.float32),
        lax.psum(all_summed[4].astype(jnp.bfloat16), "win").astype(jnp.float32),
        lax.psum(all_summed[5].astype(jnp.bfloat16), "win").astype(jnp.float32),
        lax.psum(all_summed[6].astype(jnp.bfloat16), "win").astype(jnp.float32),
        lax.psum(all_summed[7].astype(jnp.bfloat16), "win").astype(jnp.float32),
        lax.psum(all_summed[8].astype(jnp.bfloat16), "win").astype(jnp.float32),
        lax.psum(all_summed[9].astype(jnp.bfloat16), "win").astype(jnp.float32),
        lax.psum(all_summed[10].astype(jnp.bfloat16), "win").astype(jnp.float32),
        lax.psum(all_summed[11].astype(jnp.bfloat16), "win").astype(jnp.float32),
        lax.psum(all_summed[12].astype(jnp.bfloat16), "win").astype(jnp.float32),
        lax.psum(all_summed[13].astype(jnp.bfloat16), "win").astype(jnp.float32),
        lax.psum(all_summed[14].astype(jnp.bfloat16), "win").astype(jnp.float32),
    )
    return (
        visual_final.astype(jnp.bfloat16),
        unchanged(text_final).astype(jnp.bfloat16),
        visual_grad,
        text_grad,
        window_proj_sum,
        window_out_sum,
        visual_up_sum,
        visual_down_sum,
        text_query_sum,
        keyval_sum,
        cross_out_sum,
        text_up_sum,
        text_down_sum,
        window_gain_sum,
        visual_gain_sum,
        text_gain_sum,
        pages_gain_sum,
        reply_gain_sum,
        embed_sum,
    )


def solution(mesh):
    return jax.shard_map(
        shards,
        mesh=mesh,
        in_specs=(
            P("page", "win", None, None),
            P("page", None, None),
            P("page", "win", None),
            P("page", None),
            P(),
            P(),
            P(),
            P(),
            P(),
            P(),
            P(),
            P(),
            P(),
            P(),
            P(),
            P(),
            P(),
            P(),
            P(),
            P("page", "win", None, None),
            P("page", "win", None),
        ),
        out_specs=(
            P("page", "win", None, None),
            P("page", "win", None),
            P("page", "win", None, None),
            P("page", "win", None),
            P("page", None),
            P("page", None),
            P("page", None),
            P("page", None),
            P("page", None),
            P("page", None),
            P("page", None),
            P("page", None),
            P("page", None),
            P("page"),
            P("page"),
            P("page"),
            P("page"),
            P("page"),
            P("page"),
        ),
        check_vma=False,
    )
```

profile of v0, /device:TPU:0, one launch (start us, length us, event | category | flops | bytes accessed | tf_op | source)
XLA Modules:
  0.0 1089.7 jit_solution(15791098336963758596)
XLA Ops:
  16.4 10.2 collective-permute-done
  59.2 6.1 fusion.36
  83.0 9.6 collective-permute-done.1
  96.2 20.5 %multiply_convert_fusion.2 = (bf16[576,3072]{1,0:T(8,128)(2,1)S(1)}, f32[576,3072]{1,0:T(8,128)}, f32[576,3072]{1,0:T(8,128)}) fusion(bf16[576,768]{1,0:T(8,128)(2,1)S(1)} %bitcast.348, bf16[768,3072]{1,0:T(8,128)(2,1)S(1)} %bitcast.365), kind=kOutput, calls=%fused_computation.13 | convolution fusion | flops 2832924672 | bytes 23298048 | tf_op jit(solution)/shard_map/dot_general | solution.py:43
  149.2 26.3 %all-gather.2.cloned.1.call-done = bf16[1,1152,1536]{2,1,0:T(8,128)(2,1)} async-done(((bf16[1,576,1536]{2,1,0:T(8,128)(2,1)}), bf16[1,1152,1536]{2,1,0:T(8,128)(2,1)}) %all-gather.2.cloned.1.call-update) | async-done | bytes 3538960 | tf_op jit(solution)/shard_map/all_gather | solution.py:304
  198.0 6.9 fusion.69
  209.8 8.9 multiply_convert_fusion.6
  228.4 6.8 multiply_reduce_fusion.4
  235.2 8.9 multiply_reduce_fusion
  247.0 6.0 multiply_convert_fusion
  257.5 16.5 %copy.113 = bf16[1,1152,1536]{2,0,1:T(2,128)(2,1)} copy(bf16[1,1152,1536]{1,2,0:T(8,128)(2,1)} %pad_maximum_fusion) | data formatting | bytes 7077888
  274.0 5.7 copy.123
  291.9 8.4 copy.115
  327.5 7.7 reshape_bitcast_fusion
  335.2 8.6 copy.114
  351.3 8.2 add_convert_fusion
  359.6 6.7 fusion.140
  387.9 7.2 collective-permute-done.2
  411.8 8.7 multiply_reduce_fusion.2
  420.6 7.6 multiply_convert_fusion.1
  454.8 6.1 fusion.37
  480.7 7.0 convolution_convert_fusion.2
  487.7 8.6 bitcast_convert_fusion
  496.6 8.4 bitcast_convert_fusion.1
  530.7 21.9 %reduce-scatter.30.cloned.1.call-done = bf16[48,3072]{1,0:T(8,128)(2,1)} async-done(((bf16[768,3072]{1,0:T(8,128)(2,1)}), bf16[48,3072]{1,0:T(8,128)(2,1)}) %reduce-scatter.30.cloned.1.call-update) | async-done | bytes 294928 | tf_op jit(solution)/shard_map/reduce_scatter | solution.py:423
  552.6 79.0 %reduce-scatter.32.cloned.1.call-done = bf16[192,768]{1,0:T(8,128)(2,1)} async-done(((bf16[3072,768]{1,0:T(8,128)(2,1)}), bf16[192,768]{1,0:T(8,128)(2,1)}) %reduce-scatter.32.cloned.1.call-update) | async-done | bytes 294928 | tf_op jit(solution)/shard_map/reduce_scatter | solution.py:426
  631.6 60.8 %reduce-scatter.18.cloned.1.call-done = bf16[48,768]{1,0:T(8,128)(2,1)} async-done(((bf16[768,768]{1,0:T(8,128)(2,1)}), bf16[48,768]{1,0:T(8,128)(2,1)}) %reduce-scatter.18.cloned.1.call-update) | async-done | bytes 73744 | tf_op jit(solution)/shard_map/reduce_scatter | solution.py:405
  692.4 65.7 %reduce-scatter.26.cloned.1.call-done = bf16[48,1536]{1,0:T(8,128)(2,1)} async-done(((bf16[768,1536]{1,0:T(8,128)(2,1)}), bf16[48,1536]{1,0:T(8,128)(2,1)}) %reduce-scatter.26.cloned.1.call-update) | async-done | bytes 147472 | tf_op jit(solution)/shard_map/reduce_scatter | solution.py:417
  758.1 71.3 %reduce-scatter.16.cloned.1.call-done = bf16[48,2304]{1,0:T(8,128)(2,1)} async-done(((bf16[768,2304]{1,0:T(8,128)(2,1)}), bf16[48,2304]{1,0:T(8,128)(2,1)}) %reduce-scatter.16.cloned.1.call-update) | async-done | bytes 221200 | tf_op jit(solution)/shard_map/reduce_scatter | solution.py:402
  829.5 78.7 %reduce-scatter.22.cloned.1.call-done = bf16[192,768]{1,0:T(8,128)(2,1)} async-done(((bf16[3072,768]{1,0:T(8,128)(2,1)}), bf16[192,768]{1,0:T(8,128)(2,1)}) %reduce-scatter.22.cloned.1.call-update) | async-done | bytes 294928 | tf_op jit(solution)/shard_map/reduce_scatter | solution.py:411
  908.2 78.3 %reduce-scatter.20.cloned.1.call-done = bf16[48,3072]{1,0:T(8,128)(2,1)} async-done(((bf16[768,3072]{1,0:T(8,128)(2,1)}), bf16[48,3072]{1,0:T(8,128)(2,1)}) %reduce-scatter.20.cloned.1.call-update) | async-done | bytes 294928 | tf_op jit(solution)/shard_map/reduce_scatter | solution.py:408
  998.6 58.0 %all-reduce.6 = (bf16[768]{0:T(1024)(128)(2,1)S(1)}, bf16[768]{0:T(1024)(128)(2,1)}, bf16[768]{0:T(1024)(128)(2,1)}, bf16[768]{0:T(1024)(128)(2,1)}, bf16[768]{0...) all-reduce(bf16[768]{0:T(1024)(128)(2,1)} %get-tuple-element.74, ...), channel_id=13, replica_groups=mesh['page'=16,'win'=2] {'page'}, use_global_device_ids=true, to_apply=%region_52.53.clone | all-reduce | flops 4608 | bytes 18432
  (465 shorter events, 333.6 us)
Async XLA Ops:
  7.2 20.6 %copy-start = (bf16[768,2304]{1,0:T(8,128)(2,1)S(1)}, bf16[768,2304]{1,0:T(8,128)(2,1)}, u32[]{:S(2)}) copy-start(bf16[768,2304]{1,0:T(8,128)(2,1)} %param.25) | copy-start | bytes 10616836
  7.2 168.3 %all-gather.2.cloned.1.call-start = ((), (), s32[]{:S(2)}) async-start(), calls=%async_computation.11 | async-start | bytes 5308416 | tf_op jit(solution)/shard_map/all_gather | solution.py:304
  8.1 84.5 %copy-start.62 = (f32[1,12,48]{2,1,0:T(8,128)}, f32[1,12,48]{2,1,0:T(8,128)S(1)}, u32[]{:S(2)}) copy-start(f32[1,12,48]{2,1,0:T(8,128)S(1)} %copy.125) | copy-start | bytes 6916
  9.8 16.7 %copy-start.64 = (f32[12,48]{1,0:T(8,128)}, f32[12,48]{1,0:T(8,128)S(1)}, u32[]{:S(2)}) copy-start(f32[12,48]{1,0:T(8,128)S(1)} %broadcast_multiply_fusion.2) | copy-start | bytes 6916
  13.4 13.2 %collective-permute-start = (bf16[1,6,48,768]{3,2,1,0:T(8,128)(2,1)S(1)}, bf16[1,6,48,768]{3,2,1,0:T(8,128)(2,1)S(1)}, u32[]{:S(2)}, u32[]{:S(2)}) collective-permute-start(bf16[1,6,48,768]{3,2,1,0:T(8,128)(2,1)S(1)} %get-tuple-element.124), channel_id=1, source_target_pairs={{0,1},{1,0},{2,3},{3,2},{4,5},{5,4},{6,7},{7,6},{8,9},{9,8},{10,11... | collective-permute-start | bytes 1327112 | tf_op jit(solution)/shard_map/ppermute | solution.py:21
  74.4 18.2 %copy-start.74 = (f32[768]{0:T(1024)S(1)}, f32[768]{0:T(1024)}, u32[]{:S(2)}) copy-start(f32[768]{0:T(1024)} %param.39) | copy-start | bytes 9220
  79.8 16.3 %slice-start.11 = ((s8[4718592]{0:T(1024)(128)(4,1)}), s8[4194304]{0:T(1024)(128)(4,1)S(1)}, s32[]{:S(2)}) async-start(s8[4718592]{0:T(1024)(128)(4,1)} %bitcast.364), calls=%async_computation.35 | async-start | bytes 8388608
  81.2 11.4 %collective-permute-start.1 = (bf16[1,6,48,768]{3,2,1,0:T(8,128)(2,1)S(1)}, bf16[1,6,48,768]{3,2,1,0:T(8,128)(2,1)S(1)}, u32[]{:S(2)}, u32[]{:S(2)}) collective-permute-start(bf16[1,6,48,768]{3,2,1,0:T(8,128)(2,1)S(1)} %fusion.83), channel_id=1, source_target_pairs={{0,1},{1,0},{2,3},{3,2},{4,5},{5,4},{6,7},{7,6},{8,9},{9,8},{10,11... | collective-permute-start | bytes 1327112 | tf_op jit(solution)/shard_map/ppermute | solution.py:21
  95.4 21.3 %copy-start.4 = (f32[1,12,48,768]{3,2,1,0:T(8,128)}, f32[1,12,48,768]{3,2,1,0:T(8,128)S(1)}, u32[]{:S(2)}) copy-start(f32[1,12,48,768]{3,2,1,0:T(8,128)S(1)} %get-tuple-element.128) | copy-start | bytes 5308420
  95.4 21.2 %copy-start.67 = (f32[12,48]{1,0:T(8,128)}, f32[12,48]{1,0:T(8,128)S(1)}, u32[]{:S(2)}) copy-start(f32[12,48]{1,0:T(8,128)S(1)} %broadcast_multiply_fusion.1) | copy-start | bytes 6916
  95.4 21.2 %slice-start.7 = ((s8[4718592]{0:T(1024)(128)(4,1)}), s8[4194304]{0:T(1024)(128)(4,1)S(1)}, s32[]{:S(2)}) async-start(s8[4718592]{0:T(1024)(128)(4,1)} %bitcast.360), calls=%async_computation.31 | async-start | bytes 8388608
  95.8 20.9 %copy-start.87 = (f32[12,48]{1,0:T(8,128)}, f32[12,48]{1,0:T(8,128)S(1)}, u32[]{:S(2)}) copy-start(f32[12,48]{1,0:T(8,128)S(1)} %multiply_reduce_fusion.11) | copy-start | bytes 6916
  95.8 20.8 %copy-start.81 = (f32[12,48]{1,0:T(8,128)}, f32[12,48]{1,0:T(8,128)S(1)}, u32[]{:S(2)}) copy-start(f32[12,48]{1,0:T(8,128)S(1)} %fusion.105) | copy-start | bytes 6916
  96.1 20.5 %copy-start.57 = (bf16[1,12,48,768]{3,2,1,0:T(8,128)(2,1)}, bf16[1,12,48,768]{3,2,1,0:T(8,128)(2,1)S(1)}, u32[]{:S(2)}) copy-start(bf16[1,12,48,768]{3,2,1,0:T(8,128)(2,1)S(1)} %multiply_convert_fusion.8) | copy-start | bytes 2654212
  96.1 20.5 %slice-start.8 = ((s8[4718592]{0:T(1024)(128)(4,1)}), s8[524288]{0:T(1024)(128)(4,1)S(1)}, s32[]{:S(2)}) async-start(s8[4718592]{0:T(1024)(128)(4,1)} %bitcast.360), calls=%async_computation.32 | async-start | bytes 1048576
  124.8 202.7 %reduce-scatter.34.cloned.1.call-start = ((), (), s32[]{:S(2)}) async-start(), calls=%async_computation.21 | async-start | bytes 5308416
  205.0 15.8 %slice-start.5 = ((s8[4718592]{0:T(1024)(128)(4,1)}), s8[524288]{0:T(1024)(128)(4,1)S(1)}, s32[]{:S(2)}) async-start(s8[4718592]{0:T(1024)(128)(4,1)} %bitcast.358), calls=%async_computation.29 | async-start | bytes 1048576
  279.7 92.9 %reduce-scatter.36.cloned.1.call-start = ((), (), s32[]{:S(2)}) async-start(), calls=%async_computation.22 | async-start | bytes 1843200
  303.2 227.5 %reduce-scatter.24.cloned.1.call-start = ((), (), s32[]{:S(2)}) async-start(), calls=%async_computation.16 | async-start | bytes 1253376 | tf_op jit(solution)/shard_map/reduce_scatter | solution.py:414
  311.8 218.9 %reduce-scatter.28.cloned.1.call-start = ((), (), s32[]{:S(2)}) async-start(), calls=%async_computation.18 | async-start | bytes 1253376 | tf_op jit(solution)/shard_map/reduce_scatter | solution.py:420
  314.4 238.2 %reduce-scatter.30.cloned.1.call-start = ((), (), s32[]{:S(2)}) async-start(), calls=%async_computation.19 | async-start | bytes 5013504 | tf_op jit(solution)/shard_map/reduce_scatter | solution.py:423
  319.7 311.9 %reduce-scatter.32.cloned.1.call-start = ((), (), s32[]{:S(2)}) async-start(), calls=%async_computation.20 | async-start | bytes 5013504 | tf_op jit(solution)/shard_map/reduce_scatter | solution.py:426
  324.7 367.7 %reduce-scatter.18.cloned.1.call-start = ((), (), s32[]{:S(2)}) async-start(), calls=%async_computation.13 | async-start | bytes 1253376 | tf_op jit(solution)/shard_map/reduce_scatter | solution.py:405
  372.6 385.5 %reduce-scatter.26.cloned.1.call-start = ((), (), s32[]{:S(2)}) async-start(), calls=%async_computation.17 | async-start | bytes 2506752 | tf_op jit(solution)/shard_map/reduce_scatter | solution.py:417
  382.9 12.2 %collective-permute-start.2 = (bf16[1,6,48,768]{3,2,1,0:T(8,128)(2,1)}, bf16[1,6,48,768]{3,2,1,0:T(8,128)(2,1)}, u32[]{:S(2)}, u32[]{:S(2)}) collective-permute-start(bf16[1,6,48,768]{3,2,1,0:T(8,128)(2,1)} %get-tuple-element.122), channel_id=1, source_target_pairs={{0,1},{1,0},{2,3},{3,2},{4,5},{5,4},{6,7},{7,6},{8,9},{9,8},{10,11... | collective-permute-start | bytes 1327112 | tf_op jit(solution)/shard_map/ppermute | solution.py:21
  387.7 441.8 %reduce-scatter.16.cloned.1.call-start = ((), (), s32[]{:S(2)}) async-start(), calls=%async_computation.12 | async-start | bytes 3760128 | tf_op jit(solution)/shard_map/reduce_scatter | solution.py:402
  487.7 420.5 %reduce-scatter.22.cloned.1.call-start = ((), (), s32[]{:S(2)}) async-start(), calls=%async_computation.15 | async-start | bytes 5013504 | tf_op jit(solution)/shard_map/reduce_scatter | solution.py:411
  496.3 490.2 %reduce-scatter.20.cloned.1.call-start = ((), (), s32[]{:S(2)}) async-start(), calls=%async_computation.14 | async-start | bytes 5013504 | tf_op jit(solution)/shard_map/reduce_scatter | solution.py:408
  505.0 567.7 %all-reduce.11.cloned.1.call-start = ((), (), s32[]{:S(2)}) async-start(), calls=%async_computation.23 | async-start | bytes 3538944 | tf_op jit(solution)/shard_map/psum | solution.py:465
  529.3 460.5 %copy-start.63 = (f32[1,12,48]{2,1,0:T(8,128)S(1)}, f32[1,12,48]{2,1,0:T(8,128)}, u32[]{:S(2)}) copy-start(f32[1,12,48]{2,1,0:T(8,128)} %copy-done.62) | copy-start | bytes 6916
  529.3 460.5 %copy-start.65 = (f32[12,48]{1,0:T(8,128)S(1)}, f32[12,48]{1,0:T(8,128)}, u32[]{:S(2)}) copy-start(f32[12,48]{1,0:T(8,128)} %copy-done.64) | copy-start | bytes 6916
  530.2 459.6 %collective-permute-start.3 = (bf16[1,6,48,768]{3,2,1,0:T(8,128)(2,1)}, bf16[1,6,48,768]{3,2,1,0:T(8,128)(2,1)}, u32[]{:S(2)}, u32[]{:S(2)}) collective-permute-start(bf16[1,6,48,768]{3,2,1,0:T(8,128)(2,1)} %fusion.82), channel_id=1, source_target_pairs={{0,1},{1,0},{2,3},{3,2},{4,5},{5,4},{6,7},{7,6},{8,9},{9,8},{10,11... | collective-permute-start | bytes 1327112 | tf_op jit(solution)/shard_map/ppermute | solution.py:21
  (112 other events, 560.5 us)
Sparse Core Ops, SparseCore 0:
  125.0 50.5 all-gather.1
  279.8 47.6 reduce-scatter.33
  329.9 22.2 reduce-scatter.35
  355.7 58.0 reduce-scatter.23
  417.3 56.9 reduce-scatter.27
  478.0 74.5 reduce-scatter.29
  557.0 74.5 reduce-scatter.31
  635.2 57.1 reduce-scatter.17
  696.2 61.9 reduce-scatter.25
  762.3 67.0 reduce-scatter.15
  833.8 74.3 reduce-scatter.21
  911.9 74.5 reduce-scatter.19
  989.6 56.2 all-reduce.10
where the time goes:
time: 1100 us; the launch traced here: 1090 us
  waiting for transfers between devices  512 us (47%)
  matrix products  211 us (19%)
  local copies, waits for them, and re-layouts  187 us (17%)
  other arithmetic  92.1 us (8%)
  blocking collectives  63.6 us (6%)
  between operations  16.8 us (2%)
    reduce_scatter x1, waiting for transfers between devices, shards(): lax.psum_scatter(text_down_grad.astype(jnp.bfloat16), 'page', scatter_dim...  79 us
    reduce_scatter x1, waiting for transfers between devices, shards(): lax.psum_scatter(visual_down_grad.astype(jnp.bfloat16), 'page', scatter_d...  78.7 us
    reduce_scatter x1, waiting for transfers between devices, shards(): lax.psum_scatter(visual_up_grad.astype(jnp.bfloat16), 'page', scatter_dim...  78.3 us
    unnamed x270, local copies, waits for them, and re-layouts  75.5 us
    reduce_scatter x1, waiting for transfers between devices, shards(): lax.psum_scatter(window_proj_grad.astype(jnp.bfloat16), 'page', scatter_d...  71.3 us
    reduce_scatter x1, waiting for transfers between devices, shards(): lax.psum_scatter(keyval_grad.astype(jnp.bfloat16), 'page', scatter_dimens...  65.7 us
    reduce_scatter x1, waiting for transfers between devices, shards(): lax.psum_scatter(window_out_grad.astype(jnp.bfloat16), 'page', scatter_di...  60.8 us
    unnamed x1, blocking collectives  58 us
  transfers between devices with their start and end apart: 17, of which 12 were waited for; matrix products, arithmetic and copies ran while one was open for 25% of the time, Pallas kernels for 0%

commit v1 on v0

--- a/solution.py
+++ b/solution.py
@@ -1,15 +1,1193 @@
+import functools
+
 import jax
 import jax.numpy as jnp
+import numpy as np
 from jax import lax
+from jax.experimental import pallas as pl
+from jax.experimental.pallas import tpu as pltpu
 from jax.sharding import PartitionSpec as P
 
 D = 768
 HEADS = 12
 HEAD_DIM = 64
+FF = 3072
 WIN = 12
 SHIFT = 6
 WIN_ROW = 4
-PAGE_QUERY_COUNT = 400
+QUAD = 256
+PAIR = 128
+EPSILON = 1e-05
+MASKED = -1e30
+SCALE = HEAD_DIM ** (-0.5)
+F32 = jnp.float32
+BF16 = jnp.bfloat16
+
+
+def dot(left, right):
+    return jnp.dot(left, right, preferred_element_type=F32)
+
+
+def dot_t(left, right):
+    return lax.dot_general(left, right, (((1,), (1,)), ((), ())), preferred_element_type=F32)
+
+
+def t_dot(left, right):
+    return lax.dot_general(left, right, (((0,), (0,)), ((), ())), preferred_element_type=F32)
+
+
+def norm_parts(x):
+    center = x - jnp.mean(x, -1, keepdims=True)
+    inverse = lax.rsqrt(jnp.mean(center * center, -1, keepdims=True) + EPSILON)
+    return center * inverse, inverse
+
+
+def norm_back(hat, inverse, gain, grad):
+    scaled = grad * gain
+    mean = jnp.mean(scaled, -1, keepdims=True)
+    along = jnp.mean(scaled * hat, -1, keepdims=True)
+    return inverse * (scaled - mean - hat * along)
+
+
+def poly(x, terms):
+    total = jnp.full_like(x, terms[0])
+    for term in terms[1:]:
+        total = total * x + term
+    return total
+
+
+ERF_TOP = (
+    0.00022905065861350646,
+    0.0034082910107109506,
+    0.050955695062380861,
+    0.18520832239976145,
+    1.128379143519084,
+)
+ERF_BOTTOM = (
+    -1.1791602954361697e-7,
+    0.000023547966471313185,
+    0.0010179625278914885,
+    0.014070470171167667,
+    0.11098505178285362,
+    0.49746925110067538,
+    1.0,
+)
+ERF_EDGE = 3.7439211627767994
+
+
+def gelu_parts(hidden):
+    z = hidden * (0.5**0.5)
+    edge = jnp.clip(z, -ERF_EDGE, ERF_EDGE)
+    square = edge * edge
+    half = (0.5 * edge) * poly(square, ERF_TOP) / poly(square, ERF_BOTTOM)
+    share = 0.5 + half
+    slope = share + hidden * (jnp.exp(-(z * z)) * ((2 * np.pi) ** -0.5))
+    return hidden * share, slope
+
+
+def lanes_of(rows, width=PAIR):
+    return lax.broadcasted_iota(jnp.int32, (rows, width), 1)
+
+
+def head_masks():
+    first = (lanes_of(1) < HEAD_DIM).astype(F32).astype(BF16)
+    second = (lanes_of(1) >= HEAD_DIM).astype(F32).astype(BF16)
+    return first, second
+
+
+def one_hot(column, count):
+    return (lanes_of(column.shape[0], count) == column).astype(F32).astype(BF16)
+
+
+def split3(x):
+    high = x.astype(BF16).astype(F32)
+    rest = x - high
+    middle = rest.astype(BF16).astype(F32)
+    return high, middle, rest - middle
+
+
+def pack_stat(x, start):
+    high, middle, low = split3(x)
+    total = high + pltpu.roll(middle, 16, 1) + pltpu.roll(low, 32, 1)
+    return total if start == 0 else pltpu.roll(total, start, 1)
+
+
+def unpack_stat(x, start):
+    base = x if start == 0 else pltpu.roll(x, PAIR - start, 1)
+    return base + pltpu.roll(base, PAIR - 16, 1) + pltpu.roll(base, PAIR - 32, 1)
+
+
+def whole(*shape):
+    return pl.BlockSpec(shape, lambda *_: (0,) * len(shape))
+
+
+def call(kernel, name, out_shape, args, flops, **options):
+    size = sum(int(np.prod(a.shape)) * a.dtype.itemsize for a in args)
+    outs = jax.tree.leaves(out_shape)
+    size += sum(int(np.prod(o.shape)) * o.dtype.itemsize for o in outs)
+    return pl.pallas_call(
+        kernel,
+        out_shape=out_shape,
+        name=name,
+        cost_estimate=pl.CostEstimate(flops=int(flops), bytes_accessed=size, transcendentals=0),
+        **options,
+    )(*args)
+
+
+def shape_of(dtype, *shape):
+    return jax.ShapeDtypeStruct(shape, dtype)
+
+
+def window_take(rows, cols):
+    half, k, r, c = np.meshgrid(
+        np.arange(2), np.arange(WIN_ROW), np.arange(SHIFT), np.arange(WIN), indexing="ij"
+    )
+    row = half * SHIFT + r
+    col = (k * WIN + SHIFT + c) % cols
+    take = (row * cols + col).reshape(-1)
+    back = np.argsort(take)
+    return np.stack([take, row.reshape(-1), col.reshape(-1), back], 1).astype(np.int32)
+
+
+def visual_pre(visual, highlight, embed, gain, orders):
+    rows, width = visual.shape
+    page_rows, cols = highlight.shape
+
+    half = rows // 2
+
+    def kernel(v_ref, hl_ref, e_ref, g_ref, t_ref, stream_ref, first_ref, second_ref, mark_ref):
+        table = t_ref[...]
+        moved = dot(one_hot(table[:, 0:1], rows), v_ref[...])
+        marks = dot(one_hot(table[:, 1:2], page_rows), hl_ref[...].astype(F32).astype(BF16))
+        mark = jnp.sum(
+            jnp.where(lanes_of(rows, cols) == table[:, 2:3], marks, 0.0), 1, keepdims=True
+        )
+        stream = moved + mark * e_ref[...]
+        stream_ref[...] = stream
+        mark_ref[...] = jnp.broadcast_to(mark, (rows, PAIR))
+        hat, _ = norm_parts(stream)
+        normed = (hat * g_ref[...]).astype(BF16)
+        first_ref[...] = normed[:half]
+        second_ref[...] = normed[half:]
+
+    return call(
+        kernel,
+        "visual_pre",
+        (
+            shape_of(F32, rows, width),
+            shape_of(BF16, half, width),
+            shape_of(BF16, half, width),
+            shape_of(F32, rows, PAIR),
+        ),
+        (visual, highlight, embed, gain, orders),
+        2 * rows * rows * width,
+    )
+
+
+def text_pre(own_index, text, gain, query_proj, keyval_proj, own_count):
+    rows, width = text.shape
+
+    def kernel(w_ref, t_ref, o_ref, g_ref, q_ref, kv_ref, queries_ref, normed_ref, own_kv_ref):
+        hat, _ = norm_parts(t_ref[...].astype(F32))
+        normed = (hat * g_ref[...]).astype(BF16)
+        queries_ref[...] = (dot(normed, q_ref[...]).astype(BF16).astype(F32) * SCALE).astype(BF16)
+        hat, _ = norm_parts(o_ref[...].astype(F32))
+        normed = (hat * g_ref[...]).astype(BF16)
+        normed_ref[...] = normed
+        own_kv_ref[...] = dot(normed, kv_ref[...]).astype(BF16)
+
+    grid_spec = pltpu.PrefetchScalarGridSpec(
+        num_scalar_prefetch=1,
+        grid=(1,),
+        in_specs=[
+            whole(rows, width),
+            pl.BlockSpec((own_count, width), lambda i, w: (w[0], 0)),
+            whole(1, width),
+            whole(*query_proj.shape),
+            whole(*keyval_proj.shape),
+        ],
+        out_specs=[whole(rows, width), whole(own_count, width), whole(own_count, 2 * width)],
+    )
+    return call(
+        kernel,
+        "text_pre",
+        (
+            shape_of(BF16, rows, width),
+            shape_of(BF16, own_count, width),
+            shape_of(BF16, own_count, 2 * width),
+        ),
+        (own_index, text, text, gain, query_proj, keyval_proj),
+        2 * width * width * (rows + 2 * own_count),
+        grid_spec=grid_spec,
+    )
+
+
+def window_forward(normed, received, window_proj):
+    half, width = normed.shape
+    rows = 2 * half
+    part = half // WIN_ROW
+    size = 2 * part
+
+    def kernel(n_ref, r_ref, wq_ref, wk_ref, wv_ref, x_ref, q_ref, k_ref, v_ref, lse_ref, top_ref, low_ref, t_sc, l_sc):
+        step = pl.program_id(0)
+
+        @pl.when(step == 0)
+        def _():
+            top = n_ref[...].astype(F32)
+            low = r_ref[...].astype(F32)
+            pieces = []
+            for k in range(WIN_ROW):
+                pieces += [top[k * part : (k + 1) * part], low[k * part : (k + 1) * part]]
+            x_ref[...] = jnp.concatenate(pieces, 0).astype(BF16)
+            lse_ref[...] = jnp.zeros_like(lse_ref)
+
+        x = x_ref[...]
+        queries = (dot(x, wq_ref[...]).astype(BF16).astype(F32) * SCALE).astype(BF16)
+        q_ref[...] = queries
+        k_ref[...] = dot(x, wk_ref[...]).astype(BF16)
+        v_ref[...] = dot(x, wv_ref[...]).astype(BF16)
+        masks = head_masks()
+        lane = lanes_of(size)
+        for k in range(WIN_ROW):
+            at = slice(k * size, (k + 1) * size)
+            stat = lse_ref[at, :]
+            for pair in range(QUAD // PAIR):
+                cols = slice(pair * PAIR, (pair + 1) * PAIR)
+                q2, k2, v2 = q_ref[at, cols], k_ref[at, cols], v_ref[at, cols]
+                outs = []
+                for t in range(2):
+                    scores = dot_t(q2, k2 * masks[t])
+                    peak = jnp.max(scores, -1, keepdims=True)
+                    attend = jnp.exp(scores - peak).astype(BF16)
+                    out = dot(attend, v2 * masks[t] + masks[1 - t])
+                    outs.append(out)
+                    total = out[:, HEAD_DIM * (1 - t) : HEAD_DIM * (1 - t) + 1]
+                    stat = jnp.where(
+                        lane == step * (QUAD // HEAD_DIM) + 2 * pair + t, peak + jnp.log(total), stat
+                    )
+                low_lane = lane < HEAD_DIM
+                value = jnp.where(low_lane, outs[0], outs[1])
+                total = pltpu.roll(jnp.where(low_lane, outs[1], outs[0]), HEAD_DIM, 1)
+                context = value / total
+                t_sc[k * part : (k + 1) * part, cols] = context[:part]
+                l_sc[k * part : (k + 1) * part, cols] = context[part:]
+            lse_ref[at, :] = stat
+        top_ref[...] = t_sc[...].astype(BF16)
+        low_ref[...] = l_sc[...].astype(BF16)
+
+    steps = width // QUAD
+    grid_spec = pltpu.PrefetchScalarGridSpec(
+        num_scalar_prefetch=0,
+        grid=(steps,),
+        in_specs=[whole(half, width), whole(half, width)]
+        + [pl.BlockSpec((width, QUAD), lambda j, n=n: (0, n * steps + j)) for n in range(3)],
+        out_specs=[whole(rows, width)]
+        + [pl.BlockSpec((rows, QUAD), lambda j: (0, j))] * 3
+        + [whole(rows, PAIR)]
+        + [pl.BlockSpec((half, QUAD), lambda j: (0, j))] * 2,
+        scratch_shapes=[pltpu.VMEM((half, QUAD), F32)] * 2,
+    )
+    return call(
+        kernel,
+        "window_forward",
+        (shape_of(BF16, rows, width),)
+        + (shape_of(BF16, rows, width),) * 3
+        + (shape_of(F32, rows, PAIR),)
+        + (shape_of(BF16, half, width),) * 2,
+        (normed, received, window_proj, window_proj, window_proj),
+        2 * rows * width * (3 * width + 2 * size),
+        grid_spec=grid_spec,
+    )
+
+
+FF_CHUNK = 512
+ROW_BLOCK = 144
+
+
+def visual_forward(received, top, stream, window_out, gain, up, down, pages_gain, keyval_proj, orders):
+    rows, width = stream.shape
+    half = rows // 2
+    steps = up.shape[1] // FF_CHUNK
+
+    def kernel(
+        r_ref, t_ref, s_ref, wo_ref, g_ref, up_ref, down_ref, pg_ref, kv_ref, o_ref,
+        unshifted_ref, mid_ref, normed_ref, active_ref, slope_ref, final_ref, pages_ref, page_kv_ref, out_ref,
+    ):
+        step = pl.program_id(0)
+
+        @pl.when(step == 0)
+        def _():
+            unshifted_ref[:half, :] = r_ref[...]
+            unshifted_ref[half:, :] = t_ref[...]
+            mid = s_ref[...] + dot(unshifted_ref[...], wo_ref[...])
+            mid_ref[...] = mid
+            final_ref[...] = mid
+            hat, _ = norm_parts(mid)
+            normed_ref[...] = (hat * g_ref[...]).astype(BF16)
+
+        for block in range(rows // ROW_BLOCK):
+            at = slice(block * ROW_BLOCK, (block + 1) * ROW_BLOCK)
+            hidden = dot(normed_ref[at, :], up_ref[...])
+            active, slope = gelu_parts(hidden)
+            active = active.astype(BF16)
+            active_ref[at, :] = active
+            slope_ref[at, :] = slope.astype(BF16)
+            final_ref[at, :] += dot(active, down_ref[...])
+
+        @pl.when(step == steps - 1)
+        def _():
+            final = final_ref[...]
+            hat, _ = norm_parts(final)
+            pages = (hat * pg_ref[...]).astype(BF16)
+            pages_ref[...] = pages
+            page_kv_ref[...] = dot(pages, kv_ref[...]).astype(BF16)
+            out_ref[...] = dot(one_hot(o_ref[:, 3:4], rows), final.astype(BF16)).astype(BF16)
+
+    grid_spec = pltpu.PrefetchScalarGridSpec(
+        num_scalar_prefetch=0,
+        grid=(steps,),
+        in_specs=[
+            whole(half, width), whole(half, width), whole(rows, width), whole(*window_out.shape), whole(1, width),
+            pl.BlockSpec((width, FF_CHUNK), lambda j: (0, j)), pl.BlockSpec((FF_CHUNK, width), lambda j: (j, 0)),
+            whole(1, width), whole(*keyval_proj.shape), whole(*orders.shape),
+        ],
+        out_specs=[
+            whole(rows, width), whole(rows, width), whole(rows, width),
+            pl.BlockSpec((rows, FF_CHUNK), lambda j: (0, j)), pl.BlockSpec((rows, FF_CHUNK), lambda j: (0, j)),
+            whole(rows, width), whole(rows, width), whole(rows, 2 * width), whole(rows, width),
+        ],
+    )
+    return call(
+        kernel,
+        "visual_forward",
+        (
+            shape_of(BF16, rows, width), shape_of(F32, rows, width), shape_of(BF16, rows, width),
+            shape_of(BF16, rows, up.shape[1]), shape_of(BF16, rows, up.shape[1]),
+            shape_of(F32, rows, width), shape_of(BF16, rows, width), shape_of(BF16, rows, 2 * width), shape_of(BF16, rows, width),
+        ),
+        (received, top, stream, window_out, gain, up, down, pages_gain, keyval_proj, orders),
+        2 * rows * width * (width + 2 * up.shape[1] + 2 * width + rows),
+        grid_spec=grid_spec,
+    )
+
+
+STAT = PAIR
+
+
+def visible_bias(query_start, key_start, key_mask, shape, query_axis):
+    query = query_start + lax.broadcasted_iota(jnp.int32, shape, query_axis)
+    key = key_start + lax.broadcasted_iota(jnp.int32, shape, 1 - query_axis)
+    return jnp.where((key <= query) & (key_mask > 0.5), 0.0, MASKED)
+
+
+def own_mask(mask_ref, own, count):
+    mask = mask_ref[...].astype(F32)
+    picked = mask[:, :count]
+    for other in range(1, mask.shape[1] // count):
+        picked = jnp.where(own == other, mask[:, other * count : (other + 1) * count], picked)
+    return picked
+
+
+def cross_forward(index, queries, page_kv, text_kv, text_mask):
+    keys = page_kv.shape[0]
+    own_count = text_kv.shape[0]
+    width = queries.shape[1]
+    steps = width // QUAD
+
+    def kernel(i_ref, q_ref, pk_ref, pv_ref, tk_ref, tv_ref, m_ref, pack_ref, bias_sc, stat_sc):
+        step = pl.program_id(0)
+
+        @pl.when(step == 0)
+        def _():
+            own = i_ref[0]
+            bias_sc[...] = visible_bias(
+                i_ref[1] * own_count, own * own_count, own_mask(m_ref, own, own_count), (own_count, own_count), 0
+            )
+            stat_sc[...] = jnp.zeros_like(stat_sc)
+
+        masks = head_masks()
+        lane = lanes_of(own_count)
+        bias = bias_sc[...]
+        stat = stat_sc[...]
+        for pair in range(QUAD // PAIR):
+            cols = slice(pair * PAIR, (pair + 1) * PAIR)
+            q2 = q_ref[:, cols]
+            outs = []
+            for t in range(2):
+                page = dot_t(q2, pk_ref[:, cols] * masks[t])
+                text = dot_t(q2, tk_ref[:, cols] * masks[t]) + bias
+                peak = jnp.maximum(jnp.max(page, -1, keepdims=True), jnp.max(text, -1, keepdims=True))
+                out = dot(jnp.exp(page - peak).astype(BF16), pv_ref[:, cols] * masks[t] + masks[1 - t])
+                out += dot(jnp.exp(text - peak).astype(BF16), tv_ref[:, cols] * masks[t] + masks[1 - t])
+                outs.append(out)
+                total = out[:, HEAD_DIM * (1 - t) : HEAD_DIM * (1 - t) + 1]
+                stat = jnp.where(
+                    lane == step * (QUAD // HEAD_DIM) + 2 * pair + t, peak + jnp.log(total), stat
+                )
+            low_lane = lane < HEAD_DIM
+            value = jnp.where(low_lane, outs[0], outs[1])
+            total = pltpu.roll(jnp.where(low_lane, outs[1], outs[0]), HEAD_DIM, 1)
+            pack_ref[:, pl.ds(pl.multiple_of(step * QUAD + pair * PAIR, PAIR), PAIR)] = (value / total).astype(BF16)
+        stat_sc[...] = stat
+
+        @pl.when(step == steps - 1)
+        def _():
+            pack_ref[:, width:] = pack_stat(stat, 0).astype(BF16)
+
+    grid_spec = pltpu.PrefetchScalarGridSpec(
+        num_scalar_prefetch=1,
+        grid=(steps,),
+        in_specs=[
+            pl.BlockSpec((own_count, QUAD), lambda j, i: (i[1], j)),
+            pl.BlockSpec((keys, QUAD), lambda j, i: (0, j)),
+            pl.BlockSpec((keys, QUAD), lambda j, i: (0, steps + j)),
+            pl.BlockSpec((own_count, QUAD), lambda j, i: (0, j)),
+            pl.BlockSpec((own_count, QUAD), lambda j, i: (0, steps + j)),
+            whole(*text_mask.shape),
+        ],
+        out_specs=whole(own_count, width + STAT),
+        scratch_shapes=[pltpu.VMEM((own_count, own_count), F32), pltpu.VMEM((own_count, PAIR), F32)],
+    )
+    return call(
+        kernel,
+        "cross_forward",
+        shape_of(BF16, own_count, width + STAT),
+        (index, queries, page_kv, page_kv, text_kv, text_kv, text_mask),
+        8 * own_count * width * (keys + own_count),
+        grid_spec=grid_spec,
+    )
+
+
+def text_block(own_index, mine, theirs, text, cross_out, gain, up, down, upstream):
+    own_count, width = upstream.shape
+    steps = up.shape[1] // FF_CHUNK
+
+    def kernel(
+        w_ref, a_ref, b_ref, t_ref, co_ref, g_ref, up_ref, down_ref, u_ref,
+        out_ref, context_ref, normed_ref, active_ref, grad_ref, mid_grad_ref, branch_ref, pack_ref, gain_ref,
+        mid_sc, context_sc, stat_sc, up_sc,
+    ):
+        step = pl.program_id(0)
+        lane = lanes_of(own_count)
+        low_lane = lane < HEAD_DIM
+
+        @pl.when(step == 0)
+        def _():
+            first = unpack_stat(a_ref[:, width:].astype(F32), 0)
+            second = unpack_stat(b_ref[:, width:].astype(F32), 0)
+            peak = jnp.maximum(first, second)
+            total = peak + jnp.log(jnp.exp(first - peak) + jnp.exp(second - peak))
+            stat_sc[...] = total
+            first = jnp.exp(first - total)
+            second = jnp.exp(second - total)
+            for pair in range(HEADS // 2):
+                cols = slice(pair * PAIR, (pair + 1) * PAIR)
+                one = jnp.where(low_lane, first[:, 2 * pair : 2 * pair + 1], first[:, 2 * pair + 1 : 2 * pair + 2])
+                two = jnp.where(low_lane, second[:, 2 * pair : 2 * pair + 1], second[:, 2 * pair + 1 : 2 * pair + 2])
+                context_sc[:, cols] = one * a_ref[:, cols].astype(F32) + two * b_ref[:, cols].astype(F32)
+            context = context_sc[...].astype(BF16)
+            context_ref[...] = context
+            mid = t_ref[...].astype(F32) + dot(context, co_ref[...])
+            mid_sc[...] = mid
+            up_sc[...] = jnp.zeros_like(up_sc)
+            mid_grad_ref[...] = jnp.zeros_like(mid_grad_ref)
+            hat, _ = norm_parts(mid)
+            normed_ref[...] = (hat * g_ref[...]).astype(BF16)
+
+        hidden = dot(normed_ref[...], up_ref[...])
+        active, slope = gelu_parts(hidden)
+        active = active.astype(BF16)
+        active_ref[...] = active
+        up_sc[...] += dot(active, down_ref[...])
+        grad = (dot_t(u_ref[...], down_ref[...]) * slope).astype(BF16)
+        grad_ref[...] = grad
+        mid_grad_ref[...] += dot_t(grad, up_ref[...])
+
+        @pl.when(step == steps - 1)
+        def _():
+            mid = mid_sc[...]
+            out_ref[...] = (mid + up_sc[...]).astype(BF16)
+            hat, inverse = norm_parts(mid)
+            grad = mid_grad_ref[...]
+            gain_ref[...] = jnp.sum(grad * hat, 0, keepdims=True)
+            mid_grad = u_ref[...].astype(F32) + norm_back(hat, inverse, g_ref[...], grad)
+            mid_grad_ref[...] = mid_grad
+            branch = mid_grad.astype(BF16)
+            branch_ref[...] = branch
+            context_grad = dot_t(branch, co_ref[...]).astype(BF16)
+            pack_ref[:, :width] = context_grad
+            products = context_grad.astype(F32) * context_sc[...]
+            along = jnp.zeros((own_count, PAIR), F32)
+            for pair in range(HEADS // 2):
+                product = products[:, pair * PAIR : (pair + 1) * PAIR]
+                one = jnp.sum(jnp.where(low_lane, product, 0.0), -1, keepdims=True)
+                two = jnp.sum(jnp.where(low_lane, 0.0, product), -1, keepdims=True)
+                along = jnp.where(lane == 2 * pair, one, along)
+                along = jnp.where(lane == 2 * pair + 1, two, along)
+            kept = jnp.where(lane < HEADS, stat_sc[...], 0.0)
+            pack_ref[:, width:] = (pack_stat(kept, 0) + pack_stat(along, 48)).astype(BF16)
+
+    grid_spec = pltpu.PrefetchScalarGridSpec(
+        num_scalar_prefetch=1,
+        grid=(steps,),
+        in_specs=[
+            whole(own_count, width + STAT), whole(own_count, width + STAT),
+            pl.BlockSpec((own_count, width), lambda j, w: (w[0], 0)),
+            whole(*cross_out.shape), whole(1, width),
+            pl.BlockSpec((width, FF_CHUNK), lambda j, w: (0, j)), pl.BlockSpec((FF_CHUNK, width), lambda j, w: (j, 0)),
+            whole(own_count, width),
+        ],
+        out_specs=[
+            whole(own_count, width), whole(own_count, width), whole(own_count, width),
+            pl.BlockSpec((own_count, FF_CHUNK), lambda j, w: (0, j)), pl.BlockSpec((own_count, FF_CHUNK), lambda j, w: (0, j)),
+            whole(own_count, width), whole(own_count, width), whole(own_count, width + STAT), whole(1, width),
+        ],
+        scratch_shapes=[
+            pltpu.VMEM((own_count, width), F32), pltpu.VMEM((own_count, width), F32),
+            pltpu.VMEM((own_count, PAIR), F32), pltpu.VMEM((own_count, width), F32),
+        ],
+    )
+    return call(
+        kernel,
+        "text_block",
+        (
+            shape_of(BF16, own_count, width), shape_of(BF16, own_count, width), shape_of(BF16, own_count, width),
+            shape_of(BF16, own_count, up.shape[1]), shape_of(BF16, own_count, up.shape[1]),
+            shape_of(F32, own_count, width), shape_of(BF16, own_count, width), shape_of(BF16, own_count, width + STAT),
+            shape_of(F32, 1, width),
+        ),
+        (own_index, mine, theirs, text, cross_out, gain, up, down, upstream),
+        2 * own_count * width * (2 * width + 4 * up.shape[1]),
+        grid_spec=grid_spec,
+    )
+
+
+def cross_backward(index, queries, page_kv, text_kv, text_mask, mine, theirs):
+    keys = page_kv.shape[0]
+    own_count = text_kv.shape[0]
+    width = queries.shape[1]
+    steps = width // QUAD
+    padded = 256
+
+    def kernel(
+        i_ref, q0_ref, q1_ref, pk_ref, pv_ref, tk_ref, tv_ref, m_ref, a_ref, b_ref,
+        dp_ref, dt_ref, dq0_ref, dq1_ref, bias_sc, stat_sc, pad_sc,
+    ):
+        step = pl.program_id(0)
+
+        @pl.when(step == 0)
+        def _():
+            own = i_ref[0]
+            row_mask = own_mask(m_ref, own, own_count)
+            same = lax.broadcasted_iota(jnp.int32, (own_count, own_count), 0) == lax.broadcasted_iota(
+                jnp.int32, (own_count, own_count), 1
+            )
+            key_mask = jnp.sum(jnp.where(same, row_mask, 0.0), 1, keepdims=True)
+            pad_sc[...] = jnp.zeros_like(pad_sc)
+            for g, pack in enumerate((a_ref, b_ref)):
+                bias_sc[g] = visible_bias(
+                    i_ref[g] * own_count, own * own_count, key_mask, (own_count, own_count), 1
+                )
+                stats = pack[:, width:].astype(F32)
+                pad_sc[:own_count, :] = unpack_stat(stats, 0)
+                stat_sc[2 * g] = pad_sc[...].T
+                pad_sc[:own_count, :] = unpack_stat(stats, 48)
+                stat_sc[2 * g + 1] = pad_sc[...].T
+
+        masks = head_masks()
+        low_key = lanes_of(keys) < HEAD_DIM
+        low_text = lanes_of(own_count) < HEAD_DIM
+        for pair in range(QUAD // PAIR):
+            cols = slice(pair * PAIR, (pair + 1) * PAIR)
+            wide = pl.ds(pl.multiple_of(step * QUAD + pair * PAIR, PAIR), PAIR)
+            grads = [[None] * 4 for _ in range(2)]
+            query_grads = [None, None]
+            for t in range(2):
+                page_k, page_v = pk_ref[:, cols] * masks[t], pv_ref[:, cols] * masks[t]
+                text_k, text_v = tk_ref[:, cols] * masks[t], tv_ref[:, cols] * masks[t]
+                head = step * (QUAD // HEAD_DIM) + 2 * pair + t
+                for g, (q_ref, pack) in enumerate(((q0_ref, a_ref), (q1_ref, b_ref))):
+                    q2 = q_ref[:, cols]
+                    out_grad = pack[:, wide]
+                    log = stat_sc[2 * g, pl.ds(head, 1), :own_count]
+                    along = stat_sc[2 * g + 1, pl.ds(head, 1), :own_count]
+                    found = []
+                    query_grad = None
+                    for k, v, bias in ((page_k, page_v, None), (text_k, text_v, bias_sc[g])):
+                        scores = dot_t(k, q2)
+                        if bias is not None:
+                            scores = scores + bias
+                        share = jnp.exp(scores - log)
+                        score_grad = (share * (dot_t(v, out_grad) - along)).astype(BF16)
+                        found += [dot(score_grad, q2), dot(share.astype(BF16), out_grad)]
+                        part = t_dot(score_grad, k)
+                        query_grad = part if query_grad is None else query_grad + part
+                    grads[t] = [x if y is None else x + y for x, y in zip(found, grads[t])]
+                    query_grads[g] = query_grad if query_grads[g] is None else query_grads[g] + query_grad
+            second = pl.ds(pl.multiple_of(width + step * QUAD + pair * PAIR, PAIR), PAIR)
+            dp_ref[:, wide] = jnp.where(low_key, grads[0][0], grads[1][0]).astype(BF16)
+            dp_ref[:, second] = jnp.where(low_key, grads[0][1], grads[1][1]).astype(BF16)
+            dt_ref[:, wide] = jnp.where(low_text, grads[0][2], grads[1][2]).astype(BF16)
+            dt_ref[:, second] = jnp.where(low_text, grads[0][3], grads[1][3]).astype(BF16)
+            dq0_ref[:, cols] = query_grads[0] * SCALE
+            dq1_ref[:, cols] = (query_grads[1] * SCALE).astype(BF16)
+
+    grid_spec = pltpu.PrefetchScalarGridSpec(
+        num_scalar_prefetch=1,
+        grid=(steps,),
+        in_specs=[
+            pl.BlockSpec((own_count, QUAD), lambda j, i: (i[0], j)),
+            pl.BlockSpec((own_count, QUAD), lambda j, i: (i[1], j)),
+            pl.BlockSpec((keys, QUAD), lambda j, i: (0, j)),
+            pl.BlockSpec((keys, QUAD), lambda j, i: (0, steps + j)),
+            pl.BlockSpec((own_count, QUAD), lambda j, i: (0, j)),
+            pl.BlockSpec((own_count, QUAD), lambda j, i: (0, steps + j)),
+            whole(*text_mask.shape),
+            whole(own_count, width + STAT),
+            whole(own_count, width + STAT),
+        ],
+        out_specs=[whole(keys, 2 * width), whole(own_count, 2 * width)]
+        + [pl.BlockSpec((own_count, QUAD), lambda j, i: (0, j))] * 2,
+        scratch_shapes=[
+            pltpu.VMEM((2, own_count, own_count), F32),
+            pltpu.VMEM((4, PAIR, padded), F32),
+            pltpu.VMEM((padded, PAIR), F32),
+        ],
+    )
+    return call(
+        kernel,
+        "cross_backward",
+        (
+            shape_of(BF16, keys, 2 * width),
+            shape_of(BF16, own_count, 2 * width),
+            shape_of(F32, own_count, width),
+            shape_of(BF16, own_count, width),
+        ),
+        (index, queries, queries, page_kv, page_kv, text_kv, text_kv, text_mask, mine, theirs),
+        40 * own_count * width * (keys + own_count),
+        grid_spec=grid_spec,
+    )
+
+
+def text_tail(own_index, mine, theirs, kv_grad, text, mid_grad, gain, query_proj, keyval_proj):
+    own_count, width = mid_grad.shape
+
+    def kernel(w_ref, a_ref, b_ref, kv_ref, t_ref, m_ref, g_ref, q_ref, kp_ref, grad_ref, query_ref, gain_ref):
+        query = (a_ref[...] + b_ref[...].astype(F32)).astype(BF16)
+        query_ref[...] = query
+        grad = dot_t(query, q_ref[...]) + dot_t(kv_ref[...], kp_ref[...])
+        hat, inverse = norm_parts(t_ref[...].astype(F32))
+        gain_ref[...] = jnp.sum(grad * hat, 0, keepdims=True)
+        grad_ref[...] = m_ref[...] + norm_back(hat, inverse, g_ref[...], grad)
+
+    grid_spec = pltpu.PrefetchScalarGridSpec(
+        num_scalar_prefetch=1,
+        grid=(1,),
+        in_specs=[whole(own_count, width)] * 2
+        + [whole(own_count, 2 * width), pl.BlockSpec((own_count, width), lambda j, w: (w[0], 0)), whole(own_count, width)]
+        + [whole(1, width), whole(width, width), whole(width, 2 * width)],
+        out_specs=[whole(own_count, width), whole(own_count, width), whole(1, width)],
+    )
+    return call(
+        kernel,
+        "text_tail",
+        (shape_of(F32, own_count, width), shape_of(BF16, own_count, width), shape_of(F32, 1, width)),
+        (own_index, mine, theirs, kv_grad, text, mid_grad, gain, query_proj, keyval_proj),
+        6 * own_count * width * width,
+        grid_spec=grid_spec,
+    )
+
+
+def visual_backward(kv_grad, keyval_proj, final, upstream, orders, pages_gain, mid, gain, window_out, up, down, slope):
+    rows, width = final.shape
+    half = rows // 2
+    steps = up.shape[1] // FF_CHUNK
+
+    def kernel(
+        kv_ref, kp_ref, f_ref, u_ref, o_ref, pg_ref, m_ref, g_ref, wo_ref, up_ref, down_ref, s_ref,
+        out_grad_ref, grad_ref, mid_grad_ref, branch_ref, first_ref, second_ref, pages_gain_ref, gain_ref, acc_sc,
+    ):
+        step = pl.program_id(0)
+
+        @pl.when(step == 0)
+        def _():
+            pages = dot_t(kv_ref[...], kp_ref[...])
+            hat, inverse = norm_parts(f_ref[...])
+            pages_gain_ref[...] = jnp.sum(pages * hat, 0, keepdims=True)
+            upstream_rows = dot(one_hot(o_ref[:, 0:1], rows), u_ref[...])
+            final_grad = upstream_rows + norm_back(hat, inverse, pg_ref[...], pages)
+            mid_grad_ref[...] = final_grad
+            out_grad_ref[...] = final_grad.astype(BF16)
+            acc_sc[...] = jnp.zeros_like(acc_sc)
+
+        for block in range(rows // ROW_BLOCK):
+            at = slice(block * ROW_BLOCK, (block + 1) * ROW_BLOCK)
+            grad = (dot_t(out_grad_ref[at, :], down_ref[...]) * s_ref[at, :].astype(F32)).astype(BF16)
+            grad_ref[at, :] = grad
+            acc_sc[at, :] += dot_t(grad, up_ref[...])
+
+        @pl.when(step == steps - 1)
+        def _():
+            grad = acc_sc[...]
+            hat, inverse = norm_parts(m_ref[...])
+            gain_ref[...] = jnp.sum(grad * hat, 0, keepdims=True)
+            mid_grad = mid_grad_ref[...] + norm_back(hat, inverse, g_ref[...], grad)
+            mid_grad_ref[...] = mid_grad
+            branch = mid_grad.astype(BF16)
+            branch_ref[...] = branch
+            context = dot_t(branch, wo_ref[...]).astype(BF16)
+            first_ref[...] = context[:half]
+            second_ref[...] = context[half:]
+
+    grid_spec = pltpu.PrefetchScalarGridSpec(
+        num_scalar_prefetch=0,
+        grid=(steps,),
+        in_specs=[
+            whole(rows, 2 * width), whole(*keyval_proj.shape), whole(rows, width), whole(rows, width),
+            whole(*orders.shape), whole(1, width), whole(rows, width), whole(1, width), whole(*window_out.shape),
+            pl.BlockSpec((width, FF_CHUNK), lambda j: (0, j)), pl.BlockSpec((FF_CHUNK, width), lambda j: (j, 0)),
+            pl.BlockSpec((rows, FF_CHUNK), lambda j: (0, j)),
+        ],
+        out_specs=[
+            whole(rows, width), pl.BlockSpec((rows, FF_CHUNK), lambda j: (0, j)), whole(rows, width), whole(rows, width),
+            whole(half, width), whole(half, width), whole(1, width), whole(1, width),
+        ],
+        scratch_shapes=[pltpu.VMEM((rows, width), F32)],
+    )
+    return call(
+        kernel,
+        "visual_backward",
+        (
+            shape_of(BF16, rows, width), shape_of(BF16, rows, up.shape[1]), shape_of(F32, rows, width), shape_of(BF16, rows, width),
+            shape_of(BF16, half, width), shape_of(BF16, half, width), shape_of(F32, 1, width), shape_of(F32, 1, width),
+        ),
+        (kv_grad, keyval_proj, final, upstream, orders, pages_gain, mid, gain, window_out, up, down, slope),
+        2 * rows * width * (3 * width + 2 * up.shape[1] + rows),
+        grid_spec=grid_spec,
+    )
+
+
+def window_backward(queries, keys, values, logs, top, received, window_proj):
+    rows, width = queries.shape
+    half = rows // 2
+    part = half // WIN_ROW
+    size = 2 * part
+    steps = width // QUAD
+
+    def kernel(
+        q_ref, k_ref, v_ref, lse_ref, t_ref, r_ref, wq_ref, wk_ref, wv_ref,
+        packed_ref, top_ref, low_ref, acc_sc, dq_ref, dk_ref, dv_ref,
+    ):
+        step = pl.program_id(0)
+
+        @pl.when(step == 0)
+        def _():
+            acc_sc[...] = jnp.zeros_like(acc_sc)
+
+        masks = head_masks()
+        lane = lanes_of(size)
+        low_lane = lane < HEAD_DIM
+        top = t_ref[...].astype(F32)
+        low = r_ref[...].astype(F32)
+        for k in range(WIN_ROW):
+            at = slice(k * size, (k + 1) * size)
+            grads = jnp.concatenate([top[k * part : (k + 1) * part], low[k * part : (k + 1) * part]], 0).astype(BF16)
+            stat = lse_ref[at, :]
+            for pair in range(QUAD // PAIR):
+                cols = slice(pair * PAIR, (pair + 1) * PAIR)
+                q2, k2, v2, g2 = q_ref[at, cols], k_ref[at, cols], v_ref[at, cols], grads[:, cols]
+                query_grad = None
+                key_grads, value_grads = [], []
+                for t in range(2):
+                    head = step * (QUAD // HEAD_DIM) + 2 * pair + t
+                    log = jnp.sum(jnp.where(lane == head, stat, 0.0), 1, keepdims=True)
+                    key = k2 * masks[t]
+                    share = jnp.exp(dot_t(q2, key) - log)
+                    share_grad = dot_t(g2, v2 * masks[t])
+                    along = jnp.sum(share * share_grad, -1, keepdims=True)
+                    score_grad = (share * (share_grad - along)).astype(BF16)
+                    part_grad = dot(score_grad, key)
+                    query_grad = part_grad if query_grad is None else query_grad + part_grad
+                    key_grads.append(t_dot(score_grad, q2))
+                    value_grads.append(t_dot(share.astype(BF16), g2))
+                dq_ref[at, cols] = (query_grad * SCALE).astype(BF16)
+                dk_ref[at, cols] = jnp.where(low_lane, key_grads[0], key_grads[1]).astype(BF16)
+                dv_ref[at, cols] = jnp.where(low_lane, value_grads[0], value_grads[1]).astype(BF16)
+        acc_sc[...] += dot_t(dq_ref[...], wq_ref[...]) + dot_t(dk_ref[...], wk_ref[...]) + dot_t(dv_ref[...], wv_ref[...])
+        for n, ref in enumerate((dq_ref, dk_ref, dv_ref)):
+            packed_ref[:, pl.ds(pl.multiple_of(n * width + step * QUAD, QUAD), QUAD)] = ref[...]
+
+        @pl.when(step == steps - 1)
+        def _():
+            for k in range(WIN_ROW):
+                at = k * size
+                top_piece, low_piece = acc_sc[at : at + part, :], acc_sc[at + part : at + size, :]
+                if k == 0:
+                    tops, lows = [top_piece], [low_piece]
+                else:
+                    tops.append(top_piece)
+                    lows.append(low_piece)
+            top_ref[...] = jnp.concatenate(tops, 0).astype(BF16)
+            low_ref[...] = jnp.concatenate(lows, 0).astype(BF16)
+
+    block = pl.BlockSpec((rows, QUAD), lambda j: (0, j))
+    half_block = pl.BlockSpec((half, QUAD), lambda j: (0, j))
+    grid_spec = pltpu.PrefetchScalarGridSpec(
+        num_scalar_prefetch=0,
+        grid=(steps,),
+        in_specs=[block, block, block, whole(rows, PAIR), half_block, half_block]
+        + [pl.BlockSpec((width, QUAD), lambda j, n=n: (0, n * steps + j)) for n in range(3)],
+        out_specs=[whole(rows, 3 * width), whole(half, width), whole(half, width)],
+        scratch_shapes=[pltpu.VMEM((rows, width), F32)] + [pltpu.VMEM((rows, QUAD), BF16)] * 3,
+    )
+    return call(
+        kernel,
+        "window_backward",
+        (shape_of(BF16, rows, 3 * width),) + (shape_of(BF16, half, width),) * 2,
+        (queries, keys, values, logs, top, received, window_proj, window_proj, window_proj),
+        2 * rows * width * (3 * width + 5 * size),
+        grid_spec=grid_spec,
+    )
+
+
+def visual_tail(received, top, stream, mid_grad, mark, gain, orders):
+    rows, width = stream.shape
+    half = rows // 2
+
+    def kernel(r_ref, t_ref, s_ref, m_ref, mark_ref, g_ref, o_ref, out_ref, gain_ref, embed_ref, grad_sc):
+        grad_sc[:half, :] = r_ref[...].astype(F32)
+        grad_sc[half:, :] = t_ref[...].astype(F32)
+        grad = grad_sc[...]
+        hat, inverse = norm_parts(s_ref[...])
+        gain_ref[...] = jnp.sum(grad * hat, 0, keepdims=True)
+        result = m_ref[...] + norm_back(hat, inverse, g_ref[...], grad)
+        embed_ref[...] = jnp.sum(mark_ref[:, 0:1] * result, 0, keepdims=True)
+        order = one_hot(o_ref[:, 3:4], rows)
+        high, middle, low = split3(result)
+        out_ref[...] = dot(order, high.astype(BF16)) + dot(order, middle.astype(BF16)) + dot(order, low.astype(BF16))
+
+    return call(
+        kernel,
+        "visual_tail",
+        (shape_of(F32, rows, width), shape_of(F32, 1, width), shape_of(F32, 1, width)),
+        (received, top, stream, mid_grad, mark, gain, orders),
+        6 * rows * rows * width,
+        scratch_shapes=[pltpu.VMEM((rows, width), F32)],
+    )
+
+
+def places(bits):
+    found = []
+    for place in range(1 << bits):
+        rel = 0
+        for bit in range(bits):
+            if place >> (bits - 1 - bit) & 1:
+                rel |= 1 << bit
+        found.append(rel)
+    return found
+
+
+def grad_call(kernel, name, at, in_specs, args, into, out_block, steps, scratch, flops):
+    extra = {}
+    if into is not None:
+        extra = dict(input_output_aliases={len(args): 0, len(args) + 1: 1})
+        args = tuple(args) + tuple(into)
+        in_specs = in_specs + [pl.BlockSpec(memory_space=pl.ANY)] * 2
+    size = 2 * sum(int(np.prod(a.shape)) for a in args[2:4])
+    return pl.pallas_call(
+        kernel,
+        out_shape=(shape_of(BF16, *at),) * 2,
+        name=name,
+        grid_spec=pltpu.PrefetchScalarGridSpec(
+            num_scalar_prefetch=2,
+            grid=(steps,),
+            in_specs=in_specs,
+            out_specs=[out_block, out_block],
+            scratch_shapes=scratch,
+        ),
+        cost_estimate=pl.CostEstimate(flops=flops, bytes_accessed=size, transcendentals=0),
+        **extra,
+    )(*args)
+
+
+def narrow_grad(where, pairs, at, offset, into, name, tile=D, first=0, steps=None, split=False):
+    page_index, win_index = where
+    depth = pairs[0][0].shape[1]
+    pages = at[1] * 2
+    block = depth // pages
+    order = places(pages.bit_length() - 1)
+    count = pages // 2
+    if steps is None:
+        steps = pairs[0][1].shape[1] // tile
+    many = len(pairs)
+
+    def kernel(p_ref, w_ref, *refs):
+        lefts, rights = refs[:many], refs[many : 2 * many]
+        keep_ref, send_ref = refs[-2 - 2 * many : -2 * many]
+        turned, moved = refs[-2 * many : -many], refs[-many:]
+
+        @pl.when(pl.program_id(0) == 0)
+        def _():
+            for left, turn, move in zip(lefts, turned, moved):
+                turn[...] = left[...].T
+                for place, rel in enumerate(order):
+                    source = pl.multiple_of((p_ref[0] ^ rel) * block, block)
+                    move[place * block : (place + 1) * block, :] = turn[pl.ds(source, block), :]
+
+        kept = sent = None
+        for right, move in zip(rights, moved):
+            right_side = right[...]
+            one, two = dot(move[: depth // 2, :], right_side), dot(move[depth // 2 :, :], right_side)
+            kept, sent = (one, two) if kept is None else (kept + one, sent + two)
+        keep_ref[...] = kept.astype(BF16).reshape(keep_ref.shape)
+        send_ref[...] = sent.astype(BF16).reshape(send_ref.shape)
+
+    if split:
+        out_block = pl.BlockSpec((1, count, block, tile), lambda n, p, w: (n ^ w[0], 0, offset // block, 0))
+    else:
+        out_block = pl.BlockSpec((1, count, block, tile), lambda n, p, w: (0, 0, offset // block + n, 0))
+    in_specs = [whole(*left.shape) for left, _ in pairs] + [
+        pl.BlockSpec((right.shape[0], tile), lambda n, p, w: (0, first + n)) for _, right in pairs
+    ]
+    rows = sum(left.shape[0] for left, _ in pairs)
+    args = (page_index, win_index) + tuple(left for left, _ in pairs) + tuple(right for _, right in pairs)
+    scratch = [pltpu.VMEM((depth, left.shape[0]), BF16) for left, _ in pairs] * 2
+    return grad_call(kernel, name, at, in_specs, args, into, out_block, steps, scratch, 2 * rows * depth * tile * steps)
+
+
+def wide_grad(where, left, right, at, offset, into, name):
+    page_index, win_index = where
+    rows, depth = left.shape
+    pages = at[1] * 2
+    block = depth // pages
+    piece = block // 2
+    bits = pages.bit_length() - 1
+    count = pages // 2
+
+    def other_bits(place):
+        rel = 0
+        for bit in range(1, bits):
+            rel = rel | ((place >> (bits - 1 - bit)) & 1) << (bit - 1)
+        return rel
+
+    def kernel(p_ref, w_ref, l_ref, r_ref, *refs):
+        keep_ref, send_ref, turned_sc = refs[-3:]
+        turned_sc[...] = l_ref[...].T
+        right_side = r_ref[...]
+        for out_ref, side in ((keep_ref, p_ref[0] & 1), (send_ref, 1 - (p_ref[0] & 1))):
+            for rel in range(2):
+                source = pl.multiple_of(side * block + (w_ref[0] ^ rel) * piece, piece)
+                out_ref[rel, 0] = dot(turned_sc[pl.ds(source, piece), :], right_side).astype(BF16)
+
+    out_block = pl.BlockSpec((2, 1, piece, D), lambda s, p, w: (0, s, offset // piece, 0))
+    in_specs = [pl.BlockSpec((rows, 2 * block), lambda s, p, w: (0, (p[0] >> 1) ^ other_bits(s))), whole(rows, D)]
+    scratch = [pltpu.VMEM((2 * block, rows), BF16)]
+    args = (page_index, win_index, left, right)
+    return grad_call(kernel, name, at, in_specs, args, into, out_block, count, scratch, 2 * rows * depth * D)
+
+
+def swap_page(x, bit):
+    return lax.ppermute(x, "page", [(i, i ^ (1 << bit)) for i in range(lax.axis_size("page"))])
+
+
+def swap_win(x):
+    return lax.ppermute(x, "win", [(0, 1), (1, 0)])
+
+
+def total(parts):
+    result = parts[0].astype(F32)
+    for part in parts[1:]:
+        result = result + part.astype(F32)
+    return result.astype(BF16)
+
+
+class Reduction:
+    def __init__(self, kept, sent, split):
+        self.bits = lax.axis_size("page").bit_length() - 1
+        self.todo = ["0"] + (["win"] if split else []) + [str(bit) for bit in range(1, self.bits)] + ["last"]
+        self.split = split
+        self.parts = [kept]
+        self.sent = sent
+
+    def prepare(self):
+        name = self.todo[0]
+        if name == "0":
+            return self.sent
+        if name == "last":
+            return total([part[0] for part in self.parts])
+        if name == "win":
+            sent = total([part[1] for part in self.parts])
+            self.parts = [part[0] for part in self.parts]
+            return sent
+        if self.parts[0].ndim == 4:
+            self.parts = [part[0] for part in self.parts]
+        count = self.parts[0].shape[0] // 2
+        sent = total([part[count:] for part in self.parts])
+        self.parts = [part[:count] for part in self.parts]
+        return sent
+
+    def launch(self, sent):
+        name = self.todo.pop(0)
+        if name == "last":
+            self.own, self.other = sent, swap_win(sent)
+        elif name == "win":
+            self.parts.append(swap_win(sent))
+        else:
+            self.parts.append(swap_page(sent, int(name)))
+
+    def finish(self):
+        own, other = self.own.astype(F32), self.other.astype(F32)
+        if not self.split:
+            return own + other
+        first = lax.axis_index("win") == 0
+        return jnp.stack([jnp.where(first, own, other), jnp.where(first, other, own)])
+
+
+class SmallSum:
+    def __init__(self, vectors):
+        self.count = len(vectors)
+        self.value = jnp.concatenate(vectors + [jnp.zeros((8 - len(vectors), D), F32)], 0)
+        self.todo = list(range(lax.axis_size("page").bit_length() - 1)) + ["win"]
+
+    def prepare(self):
+        return self.value
+
+    def launch(self, sent):
+        name = self.todo.pop(0)
+        self.value = sent + (swap_win(sent) if name == "win" else swap_page(sent, name))
+
+    def finish(self):
+        size = D // lax.axis_size("page")
+        own = lax.dynamic_slice_in_dim(self.value, lax.axis_index("page") * size, size, 1)
+        return [own[n] for n in range(self.count)]
+
+
+def pump(anchor, *sums, after=()):
+    values = lax.optimization_barrier((anchor, *(r.prepare() for r in sums), *after))
+    for r, sent in zip(sums, values[1:]):
+        r.launch(sent)
+    return values[0]
+
+
+def drain(*sums):
+    while any(r.todo for r in sums):
+        live = [r for r in sums if r.todo]
+        for r, sent in zip(live, lax.optimization_barrier(tuple(r.prepare() for r in live))):
+            r.launch(sent)
+    return [r.finish() for r in sums]
+
+
+def untile(rows, start, count, block):
+    return jnp.concatenate([rows[start + n * block : start + (n + 1) * block] for n in range(count)], 1)
+
+
+def shards(
+    visual_in, text_in, highlight, text_mask, window_proj, window_out, visual_up, visual_down, text_query, keyval_proj,
+    cross_out, text_up, text_down, norm_window, norm_visual, norm_text, norm_pages, norm_reply, highlight_embed,
+    visual_upstream, text_upstream,
+):
+    pages = lax.axis_size("page")
+    page_rows, cols = visual_in.shape[1:3]
+    rows = page_rows * cols
+    own_count = text_upstream.shape[1]
+    win = lax.axis_index("win").astype(jnp.int32)
+    page = lax.axis_index("page").astype(jnp.int32)
+    own_index = win[None]
+    where = (page[None], own_index)
+    first_index = jnp.stack([win, win])
+    other_index = jnp.stack([win, 1 - win])
+    orders = jnp.asarray(window_take(page_rows, cols))
+    gains = [g.reshape(1, D) for g in (norm_window, norm_visual, norm_text, norm_pages, norm_reply, highlight_embed)]
+    g_window, g_visual, g_text, g_pages, g_reply, embed = gains
+    text = text_in[0]
+    text_up_stream = text_upstream[0]
+    tie = lax.optimization_barrier
+    count = pages // 2
+    block = D // pages
+    tall = FF // pages
+
+    stream, first_normed, normed, mark = visual_pre(visual_in.reshape(rows, D), highlight[0], embed, g_window, orders)
+    ahead = swap_win(first_normed)
+    queries, text_normed, text_kv = text_pre(own_index, text, g_text, text_query, keyval_proj, own_count)
+    ahead, queries = tie((ahead, queries))
+    shifted, win_q, win_k, win_v, win_log, top, low = window_forward(normed, ahead, window_proj)
+    behind = swap_win(low)
+    unshifted, mid, ff_normed, active, slope, final, pages_normed, page_kv, visual_out = visual_forward(
+        behind, top, stream, window_out, g_visual, visual_up, visual_down, g_pages, keyval_proj, orders
+    )
+    away = cross_forward(other_index, queries, page_kv, text_kv, text_mask)
+    theirs = swap_win(away)
+    mine = cross_forward(first_index, queries, page_kv, text_kv, text_mask)
+    theirs, mine = tie((theirs, mine))
+    (text_out, context, reply_normed, text_active, text_hidden_grad, text_mid_grad, branch, pack, reply_gain) = text_block(
+        own_index, mine, theirs, text, cross_out, g_reply, text_up, text_down, text_up_stream
+    )
+    pack_other = swap_win(pack)
+    at = (1, count, tall + block, D)
+    first = narrow_grad(where, [(reply_normed, text_hidden_grad)], at, 0, None, "text_up_grad")
+    first = narrow_grad(where, [(context, branch)], at, tall, first, "cross_out_grad")
+    reply_a = Reduction(*first, False)
+    text_active = pump(text_active, reply_a)
+    second = wide_grad(where, text_active, text_up_stream, (2, count, tall // 2, D), 0, None, "text_down_grad")
+    reply_b = Reduction(*second, True)
+    pack_other = pump(pack_other, reply_a, reply_b)
+    page_kv_grad, text_kv_grad, query_mine, query_away = cross_backward(
+        other_index, queries, page_kv, text_kv, text_mask, pack, pack_other
+    )
+    query_theirs = swap_win(query_away)
+    page_kv_grad = pump(page_kv_grad, reply_b)
+    (out_grad, hidden_grad, mid_grad, window_branch, context_first, context_second, pages_gain, visual_gain) = visual_backward(
+        page_kv_grad, keyval_proj, final, visual_upstream.reshape(rows, D), orders, g_pages, mid, g_visual,
+        window_out, visual_up, visual_down, slope,
+    )
+    later = swap_win(context_first)
+    hidden_grad = pump(hidden_grad, reply_a, reply_b, after=(query_theirs,))
+    at = (1, count, tall + 2 * block, D)
+    third = narrow_grad(where, [(ff_normed, hidden_grad)], at, 0, None, "visual_up_grad")
+    third = narrow_grad(where, [(unshifted, window_branch)], at, tall, third, "window_out_grad")
+    text_grad, query_grad, text_gain = text_tail(
+        own_index, query_mine, query_theirs, text_kv_grad, text, text_mid_grad, g_text, text_query, keyval_proj
+    )
+    third = narrow_grad(where, [(text_normed, query_grad)], at, tall + block, third, "text_query_grad")
+    visual_a = Reduction(*third, False)
+    active = pump(active, reply_a, reply_b, visual_a)
+    at_b = (2, count, tall // 2 + block, D)
+    fourth = wide_grad(where, active, out_grad, at_b, 0, None, "visual_down_grad")
+    fourth = narrow_grad(
+        where, [(text_normed, text_kv_grad), (pages_normed, page_kv_grad)], at_b, tall // 2, fourth, "keyval_grad", split=True
+    )
+    visual_b = Reduction(*fourth, True)
+    later = pump(later, reply_a, reply_b, visual_a, visual_b)
+    packed_grad, top_grad, low_grad = window_backward(win_q, win_k, win_v, win_log, context_second, later, window_proj)
+    earlier = swap_win(low_grad)
+    packed_grad = pump(packed_grad, reply_b, visual_b)
+    fifth = narrow_grad(where, [(shifted, packed_grad)], (1, count, 2 * block, D), 0, None, "window_proj_grad", steps=2)
+    sixth = narrow_grad(
+        where, [(shifted, packed_grad)], (2, count, block, D // 2), 0, None, "window_value_grad", D // 2, 4, 2, True
+    )
+    window_a = Reduction(*fifth, False)
+    window_b = Reduction(*sixth, True)
+    earlier = pump(earlier, window_a, window_b)
+    visual_grad, window_gain, embed_grad = visual_tail(earlier, top_grad, stream, mid_grad, mark, g_window, orders)
+    sums = SmallSum([window_gain, visual_gain, text_gain, pages_gain, reply_gain, embed_grad])
+    visual_a, visual_b, window_a, window_b, sums = drain(visual_a, visual_b, window_a, window_b, sums)
+    reply_a, reply_b = reply_a.finish(), reply_b.finish()
+    return (
+        visual_out.reshape(visual_in.shape),
+        text_out[None],
+        visual_grad.reshape(visual_in.shape),
+        text_grad[None],
+        jnp.concatenate([untile(window_a, 0, 2, block), window_b[0], window_b[1]], 1),
+        visual_a[tall : tall + block],
+        untile(visual_a, 0, FF // D, block),
+        visual_b[:, : tall // 2].reshape(tall, D),
+        visual_a[tall + block :],
+        jnp.concatenate([visual_b[0, tall // 2 :], visual_b[1, tall // 2 :]], 1),
+        reply_a[tall:],
+        untile(reply_a, 0, FF // D, block),
+        reply_b.reshape(tall, D),
+        *sums,
+    )
 
 
 epsilon = 1e-05
@@ -27,7 +1205,7 @@
     return center * lax.rsqrt(spread + epsilon) * norm_gain
 
 
-def norm_back(stream, norm_gain, upstream):
+def plain_norm_back(stream, norm_gain, upstream):
     _, pullback = jax.vjp(lambda inner_part: layer_norm(inner_part, norm_gain), stream)
     center = stream - jnp.mean(stream, -1, keepdims=True)
     spread = jnp.mean(center * center, -1, keepdims=True)
@@ -83,7 +1261,7 @@
     _, pullback = jax.vjp(gelu_exact, hidden)
     hidden_grad = pullback(matmul_back(out_grad, downward))[0].astype(jnp.bfloat16)
     up_grad = weight_grad(keep_rows(normed), keep_rows(hidden_grad))
-    stream_grad, gain_terms = norm_back(stream, norm_gain, matmul_back(hidden_grad, upward))
+    stream_grad, gain_terms = plain_norm_back(stream, norm_gain, matmul_back(hidden_grad, upward))
     return (upstream + stream_grad, column_total(keep_rows(gain_terms)), up_grad, down_grad)
 
 
@@ -154,7 +1332,7 @@
     )
 
 
-def cross_forward(inputs):
+def plain_cross_forward(inputs):
     queries, page_kv, text_kv, permitted_mask = inputs
     row_peak, row_total, page_part, text_part = cross_stats(inputs)
     cross_log = row_peak + jnp.log(row_total)
@@ -228,12 +1406,12 @@
     return (query_grad, page_grad, text_grad)
 
 
-def cross_backward(inputs):
+def plain_cross_backward(inputs):
     row_dot = cross_row_dot(inputs)
     return cross_grads(tuple(inputs) + (row_dot,))
 
 
-def shards(
+def plain_shards(
     visual_in,
     text_in,
     highlight,
@@ -298,12 +1476,12 @@
     text_queries = matmul(rows_normed, text_query).astype(jnp.bfloat16)
     row_count = text_queries.shape[1]
     row_ids = first_row + jnp.arange(row_count)[:, None]
-    key_ids = jnp.arange(PAGE_QUERY_COUNT)[None, :]
+    key_ids = jnp.arange(text_in.shape[1])[None, :]
     permitted_mask = (key_ids <= row_ids)[None] & (text_mask[:, None, :] == 1)
     query_heads = text_queries.reshape(page_count, row_count, HEADS, HEAD_DIM)
     page_kv = lax.all_gather(local_kv, "win", axis=1, tiled=True)
     cross_log, cross_context = lax.map(
-        cross_forward, (query_heads, page_kv, text_kv, permitted_mask)
+        plain_cross_forward, (query_heads, page_kv, text_kv, permitted_mask)
     )
     cross_flat = cross_context.reshape(page_count, row_count, D)
     text_mid = rows_stream + matmul(cross_flat, cross_out)
@@ -319,7 +1497,7 @@
         .reshape(page_count, row_count, HEADS, HEAD_DIM)
     )
     query_grad, page_kv_grad, text_keyvalue_gradient = lax.map(
-        cross_backward, (query_heads, page_kv, text_kv, permitted_mask, cross_log, context_grad)
+        plain_cross_backward, (query_heads, page_kv, text_kv, permitted_mask, cross_log, context_grad)
     )
     query_own = query_grad.reshape(page_count, row_count, D).astype(jnp.bfloat16)
     page_kv_own, text_kv_own = (
@@ -337,11 +1515,11 @@
         pages_normed, page_kv_own
     )
     text_normed_grad = matmul_back(query_own, text_query) + matmul_back(text_kv_own, keyval_proj)
-    text_in_grad, text_terms = norm_back(own_rows(text_stream), norm_text, text_normed_grad)
+    text_in_grad, text_terms = plain_norm_back(own_rows(text_stream), norm_text, text_normed_grad)
     text_grad = unchanged(text_mid_grad) + text_in_grad
     text_gain = column_total(text_terms)
     pages_grad = matmul_back(page_kv_own, keyval_proj).reshape(visual_final.shape)
-    final_extra, pages_terms = norm_back(visual_final, norm_pages, pages_grad)
+    final_extra, pages_terms = plain_norm_back(visual_final, norm_pages, pages_grad)
     pages_gain = column_total(pages_terms)
     visual_mid_grad, visual_gain, visual_up_grad, visual_down_grad = feed_back(
         visual_mid,
@@ -394,7 +1572,7 @@
     shifted_grad = jnp.roll(matmul_back(projected_grad, window_proj).astype(jnp.bfloat16), SHIFT, 2)
     grad_earlier = shifted_2(shifted_grad[:, SHIFT:], "win", 1)
     normed_grad = jnp.concatenate([grad_earlier, shifted_grad[:, :SHIFT]], 1)
-    stream_extra, window_terms = norm_back(stream, norm_window, normed_grad.astype(jnp.float32))
+    stream_extra, window_terms = plain_norm_back(stream, norm_window, normed_grad.astype(jnp.float32))
     visual_grad = visual_mid_grad + stream_extra
     window_gain = column_total(window_terms)
     embed_grad = column_total(highlight[..., None].astype(jnp.float32) * visual_grad)
@@ -502,52 +1680,20 @@
 
 
 def solution(mesh):
+    fits = mesh.shape["win"] == 2 and mesh.shape["page"] == 16
     return jax.shard_map(
-        shards,
+        shards if fits else plain_shards,
         mesh=mesh,
-        in_specs=(
-            P("page", "win", None, None),
-            P("page", None, None),
-            P("page", "win", None),
-            P("page", None),
-            P(),
-            P(),
-            P(),
-            P(),
-            P(),
-            P(),
-            P(),
-            P(),
-            P(),
-            P(),
-            P(),
-            P(),
-            P(),
-            P(),
-            P(),
-            P("page", "win", None, None),
-            P("page", "win", None),
-        ),
+        in_specs=(P("page", "win", None, None), P("page", None, None), P("page", "win", None), P("page", None))
+        + (P(),) * 15
+        + (P("page", "win", None, None), P("page", "win", None)),
         out_specs=(
             P("page", "win", None, None),
             P("page", "win", None),
             P("page", "win", None, None),
             P("page", "win", None),
-            P("page", None),
-            P("page", None),
-            P("page", None),
-            P("page", None),
-            P("page", None),
-            P("page", None),
-            P("page", None),
-            P("page", None),
-            P("page", None),
-            P("page"),
-            P("page"),
-            P("page"),
-            P("page"),
-            P("page"),
-            P("page"),
-        ),
+        )
+        + (P("page", None),) * 9
+        + (P("page"),) * 6,
         check_vma=False,
     )

time: 1100 us -> 452 us (0.41)
  waiting for transfers between devices: 512 us -> 103 us
  Pallas kernels: 0 us -> 224 us
  matrix products: 211 us -> 0 us
  local copies, waits for them, and re-layouts: 187 us -> 12.6 us
  blocking collectives: 63.6 us -> 0 us
  starting transfers between devices: 6.6 us -> 46.9 us
  other arithmetic: 92.1 us -> 60.5 us
  between operations: 16.8 us -> 1.16 us
    reduce_scatter x9 -> x0, waiting for transfers between devices: 456 us -> none  [the longest x1 79 us: shards(): lax.psum_scatter(text_down_grad.astype(jnp.bfloat16), 'page', scatter_dim...]
    pallas_call x0 -> x22, Pallas kernels: none -> 224 us  [the longest x12 167 us: call(): pl.pallas_call(kernel, out_shape=out_shape, name=name, cost_estimate=pl.C...]
    dot_general x48 -> x0, matrix products: 211 us -> none  [the longest x10 50.9 us: matmul(): result = jnp.dot(flattened, right_side, preferred_element_type=jnp.float32)]
    ppermute x4 -> x45, waiting for transfers between devices: 27 us -> 103 us  [the longest x28 54.8 us: swap_page(): lax.ppermute(x, 'page', [(i, i ^ 1 << bit) for i in range(lax.axis_size('...]
    unnamed x270 -> x33, local copies, waits for them, and re-layouts: 75.5 us -> 4.32 us
    unnamed x1 -> x0, blocking collectives: 58 us -> none
    ppermute x4 -> x45, starting transfers between devices: 5.64 us -> 46.9 us  [the longest x28 27.3 us: swap_page(): lax.ppermute(x, 'page', [(i, i ^ 1 << bit) for i in range(lax.axis_size('...]
    reduce_sum x21 -> x0, other arithmetic: 32.2 us -> none  [the longest x4 9.24 us: column_total(): return jnp.sum(gain_terms.reshape(-1, gain_terms.shape[-1]), 0)]
  transfers between devices with their start and end apart: 17 -> 45, of which waited for: 12 -> 16; matrix products, arithmetic and copies ran while one was open for 25% -> 13% of each run, Pallas kernels for 0% -> 33%
where the time goes in v1:
time: 452 us; the launch traced here: 448 us
  Pallas kernels  224 us (50%)
  waiting for transfers between devices  103 us (23%)
  other arithmetic  60.5 us (13%)
  starting transfers between devices  46.9 us (10%)
  local copies, waits for them, and re-layouts  12.6 us (3%)
    pallas_call x12, Pallas kernels, call(): pl.pallas_call(kernel, out_shape=out_shape, name=name, cost_estimate=pl.C...  167 us
    pallas_call x10, Pallas kernels, grad_call(): pl.pallas_call(kernel, out_shape=(shape_of(BF16, *at),) * 2, name=name, g...  56.9 us
    ppermute x28, waiting for transfers between devices, swap_page(): lax.ppermute(x, 'page', [(i, i ^ 1 << bit) for i in range(lax.axis_size('...  54.8 us
    convert_element_type x27, other arithmetic, total(): return result.astype(BF16)  52.2 us
    ppermute x17, waiting for transfers between devices, swap_win(): return lax.ppermute(x, 'win', [(0, 1), (1, 0)])  47.8 us
    ppermute x28, starting transfers between devices, swap_page(): lax.ppermute(x, 'page', [(i, i ^ 1 << bit) for i in range(lax.axis_size('...  27.3 us
    ppermute x17, starting transfers between devices, swap_win(): return lax.ppermute(x, 'win', [(0, 1), (1, 0)])  19.6 us
  transfers between devices with their start and end apart: 45, of which 16 were waited for; matrix products, arithmetic and copies ran while one was open for 13% of the time, Pallas kernels for 33%

profile of v1, /device:TPU:0, one launch (start us, length us, event | category | flops | bytes accessed | tf_op | source)
XLA Modules:
  0.0 447.7 jit_solution(9807823092579107883)
XLA Ops:
  4.5 4.2 visual_pre.1
  12.2 4.6 %text_pre.1 = (bf16[400,768]{1,0:T(8,128)(2,1)}, bf16[200,768]{1,0:T(8,128)(2,1)}, bf16[200,1536]{1,0:T(8,128)(2,1)}) custom-call(s32[1]{0:T(128)} %bitcast.1.w_ref, bf16[400,768]{1,0:T(8,128)(2,1)} %bitcast.241, bf16[400,768]{1,0:T(8,128)(2,1)} %bitcast.242, f32[1,768]{1,0:T(1,128)} %reshape.458.g_ref, bf16[768,768]{1,0:T(8,128)(2,1)} %q_ref.3, ...), custom_call_target="tpu_custom_call" | custom-call | flops 943718400 | bytes 6306820 | tf_op jit(solution)/shard_map/text_pre/pallas_call | solution.py:128
  16.8 5.2 %collective-permute-done.r_ref = bf16[288,768]{1,0:T(8,128)(2,1)S(1)} collective-permute-done((bf16[288,768]{1,0:T(8,128)(2,1)}, bf16[288,768]{1,0:T(8,128)(2,1)S(1)}, u32[]{:S(2)}, u32[]{:S(2)}) %collective-permute-start) | collective-permute-done | bytes 442400 | tf_op jit(solution)/shard_map/ppermute | solution.py:994
  22.8 12.5 %window_forward.1 = (bf16[576,768]{1,0:T(8,128)(2,1)}, bf16[576,768]{1,0:T(8,128)(2,1)}, bf16[576,768]{1,0:T(8,128)(2,1)}, bf16[576,768]{1,0:T(8,128)(2,1)}, f32...) custom-call(bf16[288,768]{1,0:T(8,128)(2,1)} %get-tuple-element.142.n_ref, ...), custom_call_target="tpu_custom_call" | custom-call | flops 2293235712 | bytes 16220160 | tf_op jit(solution)/shard_map/window_forward/pallas_call | solution.py:128
  38.8 8.1 %collective-permute-done.1.r_ref = bf16[288,768]{1,0:T(8,128)(2,1)S(1)} collective-permute-done((bf16[288,768]{1,0:T(8,128)(2,1)}, bf16[288,768]{1,0:T(8,128)(2,1)S(1)}, u32[]{:S(2)}, u32[]{:S(2)}) %collective-permute-start.1) | collective-permute-done | bytes 442400 | tf_op jit(solution)/shard_map/ppermute | solution.py:994
  47.7 27.6 %visual_forward.1 = (bf16[576,768]{1,0:T(8,128)(2,1)}, f32[576,768]{1,0:T(8,128)}, bf16[576,768]{1,0:T(8,128)(2,1)}, bf16[576,3072]{1,0:T(8,128)(2,1)}, bf16[576...) custom-call(bf16[288,768]{1,0:T(8,128)(2,1)} %copy-done.13, ...), custom_call_target="tpu_custom_call" | custom-call | flops 7983857664 | bytes 31570944 | tf_op jit(solution)/shard_map/visual_forward/pallas_call | solution.py:128
  75.3 9.0 %cross_forward.2 = bf16[200,896]{1,0:T(8,128)(2,1)} custom-call(s32[2]{0:T(128)} %pad_add_fusion.i_ref, bf16[400,768]{1,0:T(8,128)(2,1)} %get-tuple-element.150.q_ref.q0_ref.q1_ref, bf16[576,1536]{1,0:T(8,128)(2,1)} %get-tuple-element.151.pk_ref.pv_ref, bf16[576,1536]{1,0:T(8,128)(2,1)} %get-tuple-element.151.pk_ref.pv_ref, ...), custom_call_target="tpu_custom_call" | custom-call | flops 953548800 | bytes 5742152 | tf_op jit(solution)/shard_map/cross_forward/pallas_call | solution.py:128
  86.9 9.2 %cross_forward.3.a_ref = bf16[200,896]{1,0:T(8,128)(2,1)} custom-call(s32[2]{0:T(128)} %pad_add_fusion.1.i_ref, bf16[400,768]{1,0:T(8,128)(2,1)} %get-tuple-element.150.q_ref.q0_ref.q1_ref, bf16[576,1536]{1,0:T(8,128)(2,1)} %get-tuple-element.151.pk_ref.pv_ref, bf16[576,1536]{1,0:T(8,128)(2,1)} %get-tuple-element.151.pk_ref.pv_ref, ...), custom_call_target="tpu_custom_call" | custom-call | flops 953548800 | bytes 5742152 | tf_op jit(solution)/shard_map/cross_forward/pallas_call | solution.py:128
  96.8 16.1 %text_block.1 = (bf16[200,768]{1,0:T(8,128)(2,1)}, bf16[200,768]{1,0:T(8,128)(2,1)}, bf16[200,768]{1,0:T(8,128)(2,1)}, bf16[200,3072]{1,0:T(8,128)(2,1)}, bf16[2...) custom-call(s32[1]{0:T(128)} %bitcast.1.w_ref, ...), custom_call_target="tpu_custom_call" | custom-call | flops 4246732800 | bytes 16920580 | tf_op jit(solution)/shard_map/text_block/pallas_call | solution.py:128
  112.9 5.3 %text_up_grad.1 = (bf16[1,8,240,768]{3,2,1,0:T(8,128)(2,1)}, bf16[1,8,240,768]{3,2,1,0:T(8,128)(2,1)}) custom-call(s32[1]{0:T(128)} %bitcast.7.p_ref, s32[1]{0:T(128)} %bitcast.1.w_ref, bf16[200,768]{1,0:T(8,128)(2,1)} %get-tuple-element.163.refs_0_, bf16[200,3072]{1,0:T(8,128)(2,1)} %get-tuple-element.164.refs_1_), custom_call_target="tpu_custom_call" | custom-call | flops 943718400 | bytes 1536000 | tf_op jit(solution)/shard_map/text_up_grad/pallas_call | solution.py:897
  121.5 7.8 %text_down_grad.1 = (bf16[2,8,96,768]{3,2,1,0:T(8,128)(2,1)}, bf16[2,8,96,768]{3,2,1,0:T(8,128)(2,1)}) custom-call(s32[1]{0:T(128)} %bitcast.7.p_ref, s32[1]{0:T(128)} %bitcast.1.w_ref, bf16[200,3072]{1,0:T(8,128)(2,1)} %get-tuple-element.171.l_ref, bf16[200,768]{1,0:T(8,128)(2,1)} %bitcast.252), custom_call_target="tpu_custom_call" | custom-call | flops 943718400 | bytes 1536000 | tf_op jit(solution)/shard_map/text_down_grad/pallas_call | solution.py:897
  133.7 21.6 %cross_backward.1 = (bf16[576,1536]{1,0:T(8,128)(2,1)}, bf16[200,1536]{1,0:T(8,128)(2,1)}, f32[200,768]{1,0:T(8,128)}, bf16[200,768]{1,0:T(8,128)(2,1)}) custom-call(s32[2]{0:T(128)} %pad_add_fusion.i_ref, bf16[400,768]{1,0:T(8,128)(2,1)} %get-tuple-element.150.q_ref.q0_ref.q1_ref, bf16[400,768]{1,0:T(8,128)(2,1)} %get-tuple-element.150.q_ref.q0_ref.q1_ref, ...), custom_call_target="tpu_custom_call" | custom-call | flops 4767744000 | bytes 10020424 | tf_op jit(solution)/shard_map/cross_backward/pallas_call | solution.py:128
  160.2 7.0 %collective-permute-done.7 = bf16[4,240,768]{2,1,0:T(8,128)(2,1)} collective-permute-done((bf16[4,240,768]{2,1,0:T(8,128)(2,1)}, bf16[4,240,768]{2,1,0:T(8,128)(2,1)}, u32[]{:S(2)}, u32[]{:S(2)}) %collective-permute-start.7) | collective-permute-done | bytes 1474592 | tf_op jit(solution)/shard_map/ppermute | solution.py:990
  169.6 25.8 %visual_backward.1 = (bf16[576,768]{1,0:T(8,128)(2,1)}, bf16[576,3072]{1,0:T(8,128)(2,1)}, f32[576,768]{1,0:T(8,128)}, bf16[576,768]{1,0:T(8,128)(2,1)}, bf16[28...) custom-call(bf16[576,1536]{1,0:T(8,128)(2,1)} %get-tuple-element.177.kv_ref.refs_3_, ...), custom_call_target="tpu_custom_call" | custom-call | flops 7983857664 | bytes 30692352 | tf_op jit(solution)/shard_map/visual_backward/pallas_call | solution.py:128
  201.7 5.1 %text_tail.1 = (f32[200,768]{1,0:T(8,128)}, bf16[200,768]{1,0:T(8,128)(2,1)}, f32[1,768]{1,0:T(1,128)}) custom-call(s32[1]{0:T(128)} %bitcast.1.w_ref, f32[200,768]{1,0:T(8,128)} %get-tuple-element.191.a_ref, bf16[200,768]{1,0:T(8,128)(2,1)} %copy-done.6, bf16[200,1536]{1,0:T(8,128)(2,1)} %get-tuple-element.192.kv_ref.refs_2_, bf16[400,768]{1,0:T(8,128)(2,1)} %bitcast.244, ...), custom_call_target="tpu_custom_call" | custom-call | flops 707788800 | bytes 7231492 | tf_op jit(solution)/shard_map/text_tail/pallas_call | solution.py:128
  206.7 7.9 %visual_up_grad.1 = (bf16[1,8,288,768]{3,2,1,0:T(8,128)(2,1)}, bf16[1,8,288,768]{3,2,1,0:T(8,128)(2,1)}) custom-call(s32[1]{0:T(128)} %bitcast.7.p_ref, s32[1]{0:T(128)} %bitcast.1.w_ref, bf16[576,768]{1,0:T(8,128)(2,1)} %get-tuple-element.197.refs_0_, bf16[576,3072]{1,0:T(8,128)(2,1)} %get-tuple-element.198.refs_1_), custom_call_target="tpu_custom_call" | custom-call | flops 2717908992 | bytes 4423680 | tf_op jit(solution)/shard_map/visual_up_grad/pallas_call | solution.py:897
  214.6 3.9 window_out_grad.1
  229.9 10.8 %visual_down_grad.1 = (bf16[2,8,144,768]{3,2,1,0:T(8,128)(2,1)}, bf16[2,8,144,768]{3,2,1,0:T(8,128)(2,1)}) custom-call(s32[1]{0:T(128)} %bitcast.7.p_ref, s32[1]{0:T(128)} %bitcast.1.w_ref, bf16[576,3072]{1,0:T(8,128)(2,1)} %get-tuple-element.209.l_ref, bf16[576,768]{1,0:T(8,128)(2,1)} %get-tuple-element.210.r_ref), custom_call_target="tpu_custom_call" | custom-call | flops 2717908992 | bytes 4423680 | tf_op jit(solution)/shard_map/visual_down_grad/pallas_call | solution.py:897
  240.8 6.7 %keyval_grad.1 = (bf16[2,8,144,768]{3,2,1,0:T(8,128)(2,1)}, bf16[2,8,144,768]{3,2,1,0:T(8,128)(2,1)}) custom-call(s32[1]{0:T(128)} %bitcast.7.p_ref, s32[1]{0:T(128)} %bitcast.1.w_ref, bf16[200,768]{1,0:T(8,128)(2,1)} %get-tuple-element.190.refs_0_, bf16[576,768]{1,0:T(8,128)(2,1)} %get-tuple-element.208.refs_1_, ...), custom_call_target="tpu_custom_call", output_to_operand_aliasing={{0}: (6, {}), {1}: (7, {})} | custom-call | flops 1830813696 | bytes 1191936 | tf_op jit(solution)/shard_map/keyval_grad/pallas_call | solution.py:897
  255.8 24.4 %window_backward.1 = (bf16[576,2304]{1,0:T(8,128)(2,1)}, bf16[288,768]{1,0:T(8,128)(2,1)}, bf16[288,768]{1,0:T(8,128)(2,1)}) custom-call(bf16[576,768]{1,0:T(8,128)(2,1)} %get-tuple-element.156.q_ref, bf16[576,768]{1,0:T(8,128)(2,1)} %get-tuple-element.157.k_ref, bf16[576,768]{1,0:T(8,128)(2,1)} %get-tuple-element.158.v_ref, ...), custom_call_target="tpu_custom_call" | custom-call | flops 2675441664 | bytes 17989632 | tf_op jit(solution)/shard_map/window_backward/pallas_call | solution.py:128
  282.9 3.7 fusion.1
  288.0 3.9 window_value_grad.1
  291.9 5.3 %window_proj_grad.1 = (bf16[1,8,96,768]{3,2,1,0:T(8,128)(2,1)}, bf16[1,8,96,768]{3,2,1,0:T(8,128)(2,1)}) custom-call(s32[1]{0:T(128)} %bitcast.7.p_ref, s32[1]{0:T(128)} %bitcast.1.w_ref, bf16[576,768]{1,0:T(8,128)(2,1)} %get-tuple-element.216.refs_0_, bf16[576,2304]{1,0:T(8,128)(2,1)} %get-tuple-element.221.refs_1_), custom_call_target="tpu_custom_call" | custom-call | flops 1358954496 | bytes 3538944 | tf_op jit(solution)/shard_map/window_proj_grad/pallas_call | solution.py:897
  301.0 7.0 %visual_tail.1 = (f32[576,768]{1,0:T(8,128)}, f32[1,768]{1,0:T(1,128)}, f32[1,768]{1,0:T(1,128)}) custom-call(bf16[288,768]{1,0:T(8,128)(2,1)} %collective-permute-done.15.r_ref, bf16[288,768]{1,0:T(8,128)(2,1)} %get-tuple-element.225.t_ref, f32[576,768]{1,0:T(8,128)} %get-tuple-element.148.s_ref, f32[576,768]{1,0:T(8,128)} %get-tuple-element.226.m_ref, ...), custom_call_target="tpu_custom_call" | custom-call | flops 1528823808 | bytes 6506496 | tf_op jit(solution)/shard_map/visual_tail/pallas_call | solution.py:128
  313.5 18.0 %collective-permute-done.18 = bf16[8,144,768]{2,1,0:T(8,128)(2,1)} collective-permute-done((bf16[8,144,768]{2,1,0:T(8,128)(2,1)}, bf16[8,144,768]{2,1,0:T(8,128)(2,1)}, u32[]{:S(2)}, u32[]{:S(2)}) %collective-permute-start.18) | collective-permute-done | bytes 1769504 | tf_op jit(solution)/shard_map/ppermute | solution.py:994
  340.9 3.8 collective-permute-done.25
  345.8 6.8 %collective-permute-done.24 = bf16[4,96,768]{2,1,0:T(8,128)(2,1)} collective-permute-done((bf16[4,96,768]{2,1,0:T(8,128)(2,1)}, bf16[4,96,768]{2,1,0:T(8,128)(2,1)}, u32[]{:S(2)}, u32[]{:S(2)}) %collective-permute-start.24) | collective-permute-done | bytes 589856 | tf_op jit(solution)/shard_map/ppermute | solution.py:990
  355.9 12.3 %collective-permute-done.22 = bf16[4,144,768]{2,1,0:T(8,128)(2,1)S(1)} collective-permute-done((bf16[4,144,768]{2,1,0:T(8,128)(2,1)}, bf16[4,144,768]{2,1,0:T(8,128)(2,1)S(1)}, u32[]{:S(2)}, u32[]{:S(2)}) %collective-permute-start.22) | collective-permute-done | bytes 884768 | tf_op jit(solution)/shard_map/ppermute | solution.py:990
  378.1 6.7 %collective-permute-done.29 = bf16[2,96,768]{2,1,0:T(8,128)(2,1)S(1)} collective-permute-done((bf16[2,96,768]{2,1,0:T(8,128)(2,1)S(1)}, bf16[2,96,768]{2,1,0:T(8,128)(2,1)S(1)}, u32[]{:S(2)}, u32[]{:S(2)}) %collective-permute-start.29) | collective-permute-done | bytes 294944 | tf_op jit(solution)/shard_map/ppermute | solution.py:990
  385.9 5.7 %collective-permute-done.28 = bf16[1,288,768]{2,1,0:T(8,128)(2,1)S(1)} collective-permute-done((bf16[1,288,768]{2,1,0:T(8,128)(2,1)S(1)}, bf16[1,288,768]{2,1,0:T(8,128)(2,1)S(1)}, u32[]{:S(2)}, u32[]{:S(2)}) %collective-permute-start.28) | collective-permute-done | bytes 442400 | tf_op jit(solution)/shard_map/ppermute | solution.py:990
  403.3 11.5 %collective-permute-done.33 = bf16[1,96,768]{2,1,0:T(8,128)(2,1)S(1)} collective-permute-done((bf16[1,96,768]{2,1,0:T(8,128)(2,1)S(1)}, bf16[1,96,768]{2,1,0:T(8,128)(2,1)S(1)}, u32[]{:S(2)}, u32[]{:S(2)}) %collective-permute-start.33) | collective-permute-done | bytes 147488 | tf_op jit(solution)/shard_map/ppermute | solution.py:990
  430.6 12.6 %collective-permute-done.39 = bf16[48,384]{1,0:T(8,128)(2,1)S(1)} collective-permute-done((bf16[48,384]{1,0:T(8,128)(2,1)S(1)}, bf16[48,384]{1,0:T(8,128)(2,1)S(1)}, u32[]{:S(2)}, u32[]{:S(2)}) %collective-permute-start.39) | collective-permute-done | bytes 36896 | tf_op jit(solution)/shard_map/ppermute | solution.py:994
  (172 shorter events, 126.7 us)
Async XLA Ops:
  8.7 13.3 %collective-permute-start = (bf16[288,768]{1,0:T(8,128)(2,1)}, bf16[288,768]{1,0:T(8,128)(2,1)S(1)}, u32[]{:S(2)}, u32[]{:S(2)}) collective-permute-start(bf16[288,768]{1,0:T(8,128)(2,1)} %get-tuple-element.143), channel_id=1, source_target_pairs={{0,1},{1,0},{2,3},{3,2},{4,5},{5,4},{6,7},{7,6},{8,9},{9,8},{10,11... | collective-permute-start | bytes 1327112 | tf_op jit(solution)/shard_map/ppermute | solution.py:994
  132.1 23.1 %collective-permute-start.5 = (bf16[2,8,96,768]{3,2,1,0:T(8,128)(2,1)}, bf16[2,8,96,768]{3,2,1,0:T(8,128)(2,1)}, u32[]{:S(2)}, u32[]{:S(2)}) collective-permute-start(bf16[2,8,96,768]{3,2,1,0:T(8,128)(2,1)} %get-tuple-element.176), channel_id=1, source_target_pairs={{0,2},{2,0},{4,6},{6,4},{8,10},{10,8},{12,14},{14,12},{16,18},{18,... | collective-permute-start | bytes 7077896 | tf_op jit(solution)/shard_map/ppermute | solution.py:990
  132.1 35.0 %collective-permute-start.7 = (bf16[4,240,768]{2,1,0:T(8,128)(2,1)}, bf16[4,240,768]{2,1,0:T(8,128)(2,1)}, u32[]{:S(2)}, u32[]{:S(2)}) collective-permute-start(bf16[4,240,768]{2,1,0:T(8,128)(2,1)} %fusion.4), channel_id=1, source_target_pairs={{0,4},{2,6},{4,0},{6,2},{8,12},{10,14},{12,8},{14,10},{16,20},{18,... | collective-permute-start | bytes 4423688 | tf_op jit(solution)/shard_map/ppermute | solution.py:990
  158.2 37.2 %collective-permute-start.8 = (bf16[8,96,768]{2,1,0:T(8,128)(2,1)}, bf16[8,96,768]{2,1,0:T(8,128)(2,1)}, u32[]{:S(2)}, u32[]{:S(2)}) collective-permute-start(bf16[8,96,768]{2,1,0:T(8,128)(2,1)} %fusion.6), channel_id=1, source_target_pairs={{0,1},{1,0},{2,3},{3,2},{4,5},{5,4},{6,7},{7,6},{8,9},{9,8},{10,11... | collective-permute-start | bytes 3538952 | tf_op jit(solution)/shard_map/ppermute | solution.py:994
  159.7 38.2 %collective-permute-start.9 = (bf16[200,768]{1,0:T(8,128)(2,1)}, bf16[200,768]{1,0:T(8,128)(2,1)S(1)}, u32[]{:S(2)}, u32[]{:S(2)}) collective-permute-start(bf16[200,768]{1,0:T(8,128)(2,1)} %get-tuple-element.186), channel_id=1, source_target_pairs={{0,1},{1,0},{2,3},{3,2},{4,5},{5,4},{6,7},{7,6},{8,9},{9,8},{10,11... | collective-permute-start | bytes 921608 | tf_op jit(solution)/shard_map/ppermute | solution.py:994
  198.6 22.6 %collective-permute-start.11 = (bf16[4,96,768]{2,1,0:T(8,128)(2,1)}, bf16[4,96,768]{2,1,0:T(8,128)(2,1)S(1)}, u32[]{:S(2)}, u32[]{:S(2)}) collective-permute-start(bf16[4,96,768]{2,1,0:T(8,128)(2,1)} %fusion.7), channel_id=1, source_target_pairs={{0,4},{2,6},{4,0},{6,2},{8,12},{10,14},{12,8},{14,10},{16,20},{18,... | collective-permute-start | bytes 1769480 | tf_op jit(solution)/shard_map/ppermute | solution.py:990
  200.1 23.3 %collective-permute-start.10 = (bf16[2,240,768]{2,1,0:T(8,128)(2,1)}, bf16[2,240,768]{2,1,0:T(8,128)(2,1)}, u32[]{:S(2)}, u32[]{:S(2)}) collective-permute-start(bf16[2,240,768]{2,1,0:T(8,128)(2,1)} %fusion.5), channel_id=1, source_target_pairs={{0,8},{2,10},{4,12},{6,14},{8,0},{10,2},{12,4},{14,6},{16,24},{18,... | collective-permute-start | bytes 2211848 | tf_op jit(solution)/shard_map/ppermute | solution.py:990
  225.5 26.3 %collective-permute-start.14 = (bf16[1,8,288,768]{3,2,1,0:T(8,128)(2,1)}, bf16[1,8,288,768]{3,2,1,0:T(8,128)(2,1)}, u32[]{:S(2)}, u32[]{:S(2)}) collective-permute-start(bf16[1,8,288,768]{3,2,1,0:T(8,128)(2,1)} %get-tuple-element.207), channel_id=1, source_target_pairs={{0,2},{2,0},{4,6},{6,4},{8,10},{10,8},{12,14},{14,12},{16,18},{18,... | collective-permute-start | bytes 10616840 | tf_op jit(solution)/shard_map/ppermute | solution.py:990
  225.5 29.4 %collective-permute-start.6 = (bf16[288,768]{1,0:T(8,128)(2,1)}, bf16[288,768]{1,0:T(8,128)(2,1)}, u32[]{:S(2)}, u32[]{:S(2)}) collective-permute-start(bf16[288,768]{1,0:T(8,128)(2,1)} %get-tuple-element.182), channel_id=1, source_target_pairs={{0,1},{1,0},{2,3},{3,2},{4,5},{5,4},{6,7},{7,6},{8,9},{9,8},{10,11... | collective-permute-start | bytes 1327112 | tf_op jit(solution)/shard_map/ppermute | solution.py:994
  226.9 22.5 %collective-permute-start.12 = (bf16[1,240,768]{2,1,0:T(8,128)(2,1)}, bf16[1,240,768]{2,1,0:T(8,128)(2,1)}, u32[]{:S(2)}, u32[]{:S(2)}) collective-permute-start(bf16[1,240,768]{2,1,0:T(8,128)(2,1)} %fusion.15), channel_id=1, source_target_pairs={{0,16},{2,18},{4,20},{6,22},{8,24},{10,26},{12,28},{14,30},{16,0},... | collective-permute-start | bytes 1105928 | tf_op jit(solution)/shard_map/ppermute | solution.py:990
  229.5 18.0 %collective-permute-start.13 = (bf16[2,96,768]{2,1,0:T(8,128)(2,1)}, bf16[2,96,768]{2,1,0:T(8,128)(2,1)}, u32[]{:S(2)}, u32[]{:S(2)}) collective-permute-start(bf16[2,96,768]{2,1,0:T(8,128)(2,1)} %fusion.19), channel_id=1, source_target_pairs={{0,8},{2,10},{4,12},{6,14},{8,0},{10,2},{12,4},{14,6},{16,24},{18,... | collective-permute-start | bytes 884744 | tf_op jit(solution)/shard_map/ppermute | solution.py:990
  254.9 27.9 %collective-permute-start.17 = (bf16[2,8,144,768]{3,2,1,0:T(8,128)(2,1)}, bf16[2,8,144,768]{3,2,1,0:T(8,128)(2,1)}, u32[]{:S(2)}, u32[]{:S(2)}) collective-permute-start(bf16[2,8,144,768]{3,2,1,0:T(8,128)(2,1)} %get-tuple-element.220), channel_id=1, source_target_pairs={{0,2},{2,0},{4,6},{6,4},{8,10},{10,8},{12,14},{14,12},{16,18},{18,... | collective-permute-start | bytes 10616840 | tf_op jit(solution)/shard_map/ppermute | solution.py:990
  254.9 43.4 %collective-permute-start.19 = (bf16[4,288,768]{2,1,0:T(8,128)(2,1)}, bf16[4,288,768]{2,1,0:T(8,128)(2,1)}, u32[]{:S(2)}, u32[]{:S(2)}) collective-permute-start(bf16[4,288,768]{2,1,0:T(8,128)(2,1)} %fusion), channel_id=1, source_target_pairs={{0,4},{2,6},{4,0},{6,2},{8,12},{10,14},{12,8},{14,10},{16,20},{18,... | collective-permute-start | bytes 5308424 | tf_op jit(solution)/shard_map/ppermute | solution.py:990
  255.5 25.4 %collective-permute-start.16 = (bf16[1,96,768]{2,1,0:T(8,128)(2,1)}, bf16[1,96,768]{2,1,0:T(8,128)(2,1)}, u32[]{:S(2)}, u32[]{:S(2)}) collective-permute-start(bf16[1,96,768]{2,1,0:T(8,128)(2,1)} %fusion.36), channel_id=1, source_target_pairs={{0,16},{2,18},{4,20},{6,22},{8,24},{10,26},{12,28},{14,30},{16,0},... | collective-permute-start | bytes 442376 | tf_op jit(solution)/shard_map/ppermute | solution.py:990
  280.2 16.9 %collective-permute-start.15 = (bf16[288,768]{1,0:T(8,128)(2,1)}, bf16[288,768]{1,0:T(8,128)(2,1)}, u32[]{:S(2)}, u32[]{:S(2)}) collective-permute-start(bf16[288,768]{1,0:T(8,128)(2,1)} %get-tuple-element.215), channel_id=1, source_target_pairs={{0,1},{1,0},{2,3},{3,2},{4,5},{5,4},{6,7},{7,6},{8,9},{9,8},{10,11... | collective-permute-start | bytes 1327112 | tf_op jit(solution)/shard_map/ppermute | solution.py:994
  286.6 44.9 %collective-permute-start.18 = (bf16[8,144,768]{2,1,0:T(8,128)(2,1)}, bf16[8,144,768]{2,1,0:T(8,128)(2,1)}, u32[]{:S(2)}, u32[]{:S(2)}) collective-permute-start(bf16[8,144,768]{2,1,0:T(8,128)(2,1)} %fusion.1), channel_id=1, source_target_pairs={{0,1},{1,0},{2,3},{3,2},{4,5},{5,4},{6,7},{7,6},{8,9},{9,8},{10,11... | collective-permute-start | bytes 5308424 | tf_op jit(solution)/shard_map/ppermute | solution.py:994
  297.2 14.1 %collective-permute-start.20 = (bf16[1,8,96,768]{3,2,1,0:T(8,128)(2,1)}, bf16[1,8,96,768]{3,2,1,0:T(8,128)(2,1)}, u32[]{:S(2)}, u32[]{:S(2)}) collective-permute-start(bf16[1,8,96,768]{3,2,1,0:T(8,128)(2,1)} %get-tuple-element.233), channel_id=1, source_target_pairs={{0,2},{2,0},{4,6},{6,4},{8,10},{10,8},{12,14},{14,12},{16,18},{18,... | collective-permute-start | bytes 3538952 | tf_op jit(solution)/shard_map/ppermute | solution.py:990
  297.2 12.2 %collective-permute-start.21 = (bf16[2,8,48,384]{3,2,1,0:T(8,128)(2,1)}, bf16[2,8,48,384]{3,2,1,0:T(8,128)(2,1)}, u32[]{:S(2)}, u32[]{:S(2)}) collective-permute-start(bf16[2,8,48,384]{3,2,1,0:T(8,128)(2,1)} %get-tuple-element.235), channel_id=1, source_target_pairs={{0,2},{2,0},{4,6},{6,4},{8,10},{10,8},{12,14},{14,12},{16,18},{18,... | collective-permute-start | bytes 1769480 | tf_op jit(solution)/shard_map/ppermute | solution.py:990
  297.7 41.0 %collective-permute-start.42 = (bf16[240,768]{1,0:T(8,128)(2,1)}, bf16[240,768]{1,0:T(8,128)(2,1)}, u32[]{:S(2)}, u32[]{:S(2)}) collective-permute-start(bf16[240,768]{1,0:T(8,128)(2,1)} %fusion.13), channel_id=1, source_target_pairs={{0,1},{1,0},{2,3},{3,2},{4,5},{5,4},{6,7},{7,6},{8,9},{9,8},{10,11... | collective-permute-start | bytes 1105928 | tf_op jit(solution)/shard_map/ppermute | solution.py:994
  334.4 19.9 %collective-permute-start.23 = (bf16[2,288,768]{2,1,0:T(8,128)(2,1)}, bf16[2,288,768]{2,1,0:T(8,128)(2,1)}, u32[]{:S(2)}, u32[]{:S(2)}) collective-permute-start(bf16[2,288,768]{2,1,0:T(8,128)(2,1)} %fusion.3), channel_id=1, source_target_pairs={{0,8},{2,10},{4,12},{6,14},{8,0},{10,2},{12,4},{14,6},{16,24},{18,... | collective-permute-start | bytes 2654216 | tf_op jit(solution)/shard_map/ppermute | solution.py:990
  336.0 16.6 %collective-permute-start.24 = (bf16[4,96,768]{2,1,0:T(8,128)(2,1)}, bf16[4,96,768]{2,1,0:T(8,128)(2,1)}, u32[]{:S(2)}, u32[]{:S(2)}) collective-permute-start(bf16[4,96,768]{2,1,0:T(8,128)(2,1)} %fusion.16), channel_id=1, source_target_pairs={{0,4},{2,6},{4,0},{6,2},{8,12},{10,14},{12,8},{14,10},{16,20},{18,... | collective-permute-start | bytes 1769480 | tf_op jit(solution)/shard_map/ppermute | solution.py:990
  338.2 30.0 %collective-permute-start.22 = (bf16[4,144,768]{2,1,0:T(8,128)(2,1)}, bf16[4,144,768]{2,1,0:T(8,128)(2,1)S(1)}, u32[]{:S(2)}, u32[]{:S(2)}) collective-permute-start(bf16[4,144,768]{2,1,0:T(8,128)(2,1)} %fusion.2), channel_id=1, source_target_pairs={{0,4},{2,6},{4,0},{6,2},{8,12},{10,14},{12,8},{14,10},{16,20},{18,... | collective-permute-start | bytes 2654216 | tf_op jit(solution)/shard_map/ppermute | solution.py:990
  369.7 15.1 %collective-permute-start.29 = (bf16[2,96,768]{2,1,0:T(8,128)(2,1)S(1)}, bf16[2,96,768]{2,1,0:T(8,128)(2,1)S(1)}, u32[]{:S(2)}, u32[]{:S(2)}) collective-permute-start(bf16[2,96,768]{2,1,0:T(8,128)(2,1)S(1)} %fusion.17), channel_id=1, source_target_pairs={{0,8},{2,10},{4,12},{6,14},{8,0},{10,2},{12,4},{14,6},{16,24},{18,... | collective-permute-start | bytes 884744 | tf_op jit(solution)/shard_map/ppermute | solution.py:990
  373.0 18.6 %collective-permute-start.28 = (bf16[1,288,768]{2,1,0:T(8,128)(2,1)S(1)}, bf16[1,288,768]{2,1,0:T(8,128)(2,1)S(1)}, u32[]{:S(2)}, u32[]{:S(2)}) collective-permute-start(bf16[1,288,768]{2,1,0:T(8,128)(2,1)S(1)} %fusion.12), channel_id=1, source_target_pairs={{0,16},{2,18},{4,20},{6,22},{8,24},{10,26},{12,28},{14,30},{16,0},... | collective-permute-start | bytes 1327112 | tf_op jit(solution)/shard_map/ppermute | solution.py:990
  375.6 19.0 %collective-permute-start.27 = (bf16[2,144,768]{2,1,0:T(8,128)(2,1)S(1)}, bf16[2,144,768]{2,1,0:T(8,128)(2,1)S(1)}, u32[]{:S(2)}, u32[]{:S(2)}) collective-permute-start(bf16[2,144,768]{2,1,0:T(8,128)(2,1)S(1)} %fusion.10), channel_id=1, source_target_pairs={{0,8},{2,10},{4,12},{6,14},{8,0},{10,2},{12,4},{14,6},{16,24},{18,... | collective-permute-start | bytes 1327112 | tf_op jit(solution)/shard_map/ppermute | solution.py:990
  398.9 21.4 %collective-permute-start.43 = (bf16[96,768]{1,0:T(8,128)(2,1)S(1)}, bf16[96,768]{1,0:T(8,128)(2,1)S(1)}, u32[]{:S(2)}, u32[]{:S(2)}) collective-permute-start(bf16[96,768]{1,0:T(8,128)(2,1)S(1)} %copy-done.4), channel_id=1, source_target_pairs={{0,1},{1,0},{2,3},{3,2},{4,5},{5,4},{6,7},{7,6},{8,9},{9,8},{10,11... | collective-permute-start | bytes 442376 | tf_op jit(solution)/shard_map/ppermute | solution.py:994
  399.5 16.4 %collective-permute-start.32 = (bf16[1,144,768]{2,1,0:T(8,128)(2,1)S(1)}, bf16[1,144,768]{2,1,0:T(8,128)(2,1)S(1)}, u32[]{:S(2)}, u32[]{:S(2)}) collective-permute-start(bf16[1,144,768]{2,1,0:T(8,128)(2,1)S(1)} %fusion.25), channel_id=1, source_target_pairs={{0,16},{2,18},{4,20},{6,22},{8,24},{10,26},{12,28},{14,30},{16,0},... | collective-permute-start | bytes 663560 | tf_op jit(solution)/shard_map/ppermute | solution.py:990
  402.0 12.8 %collective-permute-start.33 = (bf16[1,96,768]{2,1,0:T(8,128)(2,1)S(1)}, bf16[1,96,768]{2,1,0:T(8,128)(2,1)S(1)}, u32[]{:S(2)}, u32[]{:S(2)}) collective-permute-start(bf16[1,96,768]{2,1,0:T(8,128)(2,1)S(1)} %fusion.32), channel_id=1, source_target_pairs={{0,16},{2,18},{4,20},{6,22},{8,24},{10,26},{12,28},{14,30},{16,0},... | collective-permute-start | bytes 442376 | tf_op jit(solution)/shard_map/ppermute | solution.py:990
  425.9 19.8 %collective-permute-start.40 = (bf16[288,768]{1,0:T(8,128)(2,1)S(1)}, bf16[288,768]{1,0:T(8,128)(2,1)S(1)}, u32[]{:S(2)}, u32[]{:S(2)}) collective-permute-start(bf16[288,768]{1,0:T(8,128)(2,1)S(1)} %fusion.8), channel_id=1, source_target_pairs={{0,1},{1,0},{2,3},{3,2},{4,5},{5,4},{6,7},{7,6},{8,9},{9,8},{10,11... | collective-permute-start | bytes 1327112 | tf_op jit(solution)/shard_map/ppermute | solution.py:994
  426.5 16.7 %collective-permute-start.36 = (bf16[96,768]{1,0:T(8,128)(2,1)S(1)}, bf16[96,768]{1,0:T(8,128)(2,1)S(1)}, u32[]{:S(2)}, u32[]{:S(2)}) collective-permute-start(bf16[96,768]{1,0:T(8,128)(2,1)S(1)} %fusion.29), channel_id=1, source_target_pairs={{0,1},{1,0},{2,3},{3,2},{4,5},{5,4},{6,7},{7,6},{8,9},{9,8},{10,11... | collective-permute-start | bytes 442376 | tf_op jit(solution)/shard_map/ppermute | solution.py:994
  427.9 16.1 %collective-permute-start.41 = (bf16[144,768]{1,0:T(8,128)(2,1)S(1)}, bf16[144,768]{1,0:T(8,128)(2,1)S(1)}, u32[]{:S(2)}, u32[]{:S(2)}) collective-permute-start(bf16[144,768]{1,0:T(8,128)(2,1)S(1)} %fusion.22), channel_id=1, source_target_pairs={{0,1},{1,0},{2,3},{3,2},{4,5},{5,4},{6,7},{7,6},{8,9},{9,8},{10,11... | collective-permute-start | bytes 663560 | tf_op jit(solution)/shard_map/ppermute | solution.py:994
  428.5 14.7 %collective-permute-start.39 = (bf16[48,384]{1,0:T(8,128)(2,1)S(1)}, bf16[48,384]{1,0:T(8,128)(2,1)S(1)}, u32[]{:S(2)}, u32[]{:S(2)}) collective-permute-start(bf16[48,384]{1,0:T(8,128)(2,1)S(1)} %fusion.39), channel_id=1, source_target_pairs={{0,1},{1,0},{2,3},{3,2},{4,5},{5,4},{6,7},{7,6},{8,9},{9,8},{10,11... | collective-permute-start | bytes 110600 | tf_op jit(solution)/shard_map/ppermute | solution.py:994
  (29 other events, 222.2 us)

commit v2 on v1

--- a/solution.py
+++ b/solution.py
@@ -50,38 +50,30 @@
 
 
 def poly(x, terms):
-    total = jnp.full_like(x, terms[0])
-    for term in terms[1:]:
+    total = x * terms[0] + terms[1]
+    for term in terms[2:]:
         total = total * x + term
     return total
 
 
-ERF_TOP = (
-    0.00022905065861350646,
-    0.0034082910107109506,
-    0.050955695062380861,
-    0.18520832239976145,
-    1.128379143519084,
+ERF_TERMS = (
+    1.58960242e-07,
+    -5.98569105e-06,
+    8.97125902e-05,
+    -6.25719583e-04,
+    -1.84383680e-04,
+    1.02765481e-01,
+    1.12837971,
 )
-ERF_BOTTOM = (
-    -1.1791602954361697e-7,
-    0.000023547966471313185,
-    0.0010179625278914885,
-    0.014070470171167667,
-    0.11098505178285362,
-    0.49746925110067538,
-    1.0,
-)
-ERF_EDGE = 3.7439211627767994
+GELU_TERMS = tuple(term * 0.5 ** (len(ERF_TERMS) - 1 - n + 0.5) for n, term in enumerate(ERF_TERMS))
+DENSITY = float(np.log2((2 * np.pi) ** -0.5))
+HALF_LOG = float(-0.5 * np.log2(np.e))
 
 
 def gelu_parts(hidden):
-    z = hidden * (0.5**0.5)
-    edge = jnp.clip(z, -ERF_EDGE, ERF_EDGE)
-    square = edge * edge
-    half = (0.5 * edge) * poly(square, ERF_TOP) / poly(square, ERF_BOTTOM)
-    share = 0.5 + half
-    slope = share + hidden * (jnp.exp(-(z * z)) * ((2 * np.pi) ** -0.5))
+    square = hidden * hidden
+    share = 0.5 + 0.5 * jnp.tanh(hidden * poly(jnp.minimum(square, 36.0), GELU_TERMS))
+    slope = share + hidden * jnp.exp2(square * HALF_LOG + DENSITY)
     return hidden * share, slope
 
 
@@ -118,6 +110,10 @@
 
 
 def whole(*shape):
+    return pl.BlockSpec(memory_space=pltpu.VMEM)
+
+
+def window(*shape):
     return pl.BlockSpec(shape, lambda *_: (0,) * len(shape))
 
 
@@ -130,8 +126,13 @@
         out_shape=out_shape,
         name=name,
         cost_estimate=pl.CostEstimate(flops=int(flops), bytes_accessed=size, transcendentals=0),
+        compiler_params=pltpu.CompilerParams(vmem_limit_bytes=30 << 20),
         **options,
     )(*args)
+
+
+def from_hbm(weights):
+    return pltpu.with_memory_space_constraint(weights, pltpu.HBM)
 
 
 def shape_of(dtype, *shape):
@@ -222,11 +223,57 @@
     )
 
 
+def quad_masks():
+    lane = lanes_of(1, QUAD)
+    return [((lane >= h * HEAD_DIM) & (lane < (h + 1) * HEAD_DIM)).astype(F32).astype(BF16) for h in range(4)]
+
+
+def by_head(rows, masks):
+    return jnp.concatenate([rows * mask for mask in masks], 0)
+
+
+def spread(columns, size, width):
+    tiles = []
+    for start in range(0, 4 * size, PAIR):
+        stop = min(start + PAIR, 4 * size)
+        first, last = start // size, (stop - 1) // size
+        if first == last:
+            tiles.append(columns[first])
+        else:
+            lane = lanes_of(width, stop - start) + start
+            tiles.append(jnp.where(lane < last * size, columns[first], columns[last]))
+    return tiles
+
+
+def tiles_of(x):
+    return [x[:, start : min(start + PAIR, x.shape[1])] for start in range(0, x.shape[1], PAIR)]
+
+
+def quad_peaks(scores, size):
+    rows = scores.shape[0]
+    peaks = []
+    for h in range(4):
+        start = h * size // PAIR * PAIR
+        stop = min(-(-(h + 1) * size // PAIR) * PAIR, 4 * size)
+        lane = lanes_of(rows, stop - start) + start
+        part = scores[:, start:stop]
+        peaks.append(jnp.max(jnp.where((lane >= h * size) & (lane < (h + 1) * size), part, -jnp.inf), -1, keepdims=True))
+    return peaks
+
+
+def quad_lanes(columns, rows):
+    low = lanes_of(rows) < HEAD_DIM
+    return jnp.concatenate(
+        [jnp.where(low, columns[0], columns[1]), jnp.where(low, columns[2], columns[3])], 1
+    )
+
+
 def window_forward(normed, received, window_proj):
     half, width = normed.shape
     rows = 2 * half
     part = half // WIN_ROW
     size = 2 * part
+    steps = width // QUAD
 
     def kernel(n_ref, r_ref, wq_ref, wk_ref, wv_ref, x_ref, q_ref, k_ref, v_ref, lse_ref, top_ref, low_ref, t_sc, l_sc):
         step = pl.program_id(0)
@@ -239,43 +286,34 @@
             for k in range(WIN_ROW):
                 pieces += [top[k * part : (k + 1) * part], low[k * part : (k + 1) * part]]
             x_ref[...] = jnp.concatenate(pieces, 0).astype(BF16)
-            lse_ref[...] = jnp.zeros_like(lse_ref)
 
         x = x_ref[...]
-        queries = (dot(x, wq_ref[...]).astype(BF16).astype(F32) * SCALE).astype(BF16)
-        q_ref[...] = queries
+        q_ref[...] = (dot(x, wq_ref[...]).astype(BF16).astype(F32) * SCALE).astype(BF16)
         k_ref[...] = dot(x, wk_ref[...]).astype(BF16)
         v_ref[...] = dot(x, wv_ref[...]).astype(BF16)
-        masks = head_masks()
+        masks = quad_masks()
         lane = lanes_of(size)
+        key_row = lax.broadcasted_iota(jnp.int32, (4 * size, PAIR), 0)
+        key_lane = lanes_of(4 * size)
+        ends = ((key_row >= key_lane * size) & (key_row < (key_lane + 1) * size)).astype(F32).astype(BF16)
         for k in range(WIN_ROW):
             at = slice(k * size, (k + 1) * size)
-            stat = lse_ref[at, :]
-            for pair in range(QUAD // PAIR):
-                cols = slice(pair * PAIR, (pair + 1) * PAIR)
-                q2, k2, v2 = q_ref[at, cols], k_ref[at, cols], v_ref[at, cols]
-                outs = []
-                for t in range(2):
-                    scores = dot_t(q2, k2 * masks[t])
-                    peak = jnp.max(scores, -1, keepdims=True)
-                    attend = jnp.exp(scores - peak).astype(BF16)
-                    out = dot(attend, v2 * masks[t] + masks[1 - t])
-                    outs.append(out)
-                    total = out[:, HEAD_DIM * (1 - t) : HEAD_DIM * (1 - t) + 1]
-                    stat = jnp.where(
-                        lane == step * (QUAD // HEAD_DIM) + 2 * pair + t, peak + jnp.log(total), stat
-                    )
-                low_lane = lane < HEAD_DIM
-                value = jnp.where(low_lane, outs[0], outs[1])
-                total = pltpu.roll(jnp.where(low_lane, outs[1], outs[0]), HEAD_DIM, 1)
-                context = value / total
-                t_sc[k * part : (k + 1) * part, cols] = context[:part]
-                l_sc[k * part : (k + 1) * part, cols] = context[part:]
-            lse_ref[at, :] = stat
+            scores = dot_t(q_ref[at, :], by_head(k_ref[at, :], masks))
+            peaks = quad_peaks(scores, size)
+            shares = [jnp.exp(tile - peak) for tile, peak in zip(tiles_of(scores), spread(peaks, size, size))]
+            attend = jnp.concatenate(shares, 1).astype(BF16)
+            totals = dot(attend, ends)
+            columns = [totals[:, h : h + 1] for h in range(4)]
+            context = dot(attend, by_head(v_ref[at, :], masks)) / quad_lanes(columns, size)
+            t_sc[k * part : (k + 1) * part, :] = context[:part]
+            l_sc[k * part : (k + 1) * part, :] = context[part:]
+            stat = jnp.zeros((size, PAIR), F32)
+            for h in range(4):
+                stat = jnp.where(lane == h, peaks[h] + jnp.log(columns[h]), stat)
+            lse_ref[0, at, :] = stat
         top_ref[...] = t_sc[...].astype(BF16)
         low_ref[...] = l_sc[...].astype(BF16)
 
-    steps = width // QUAD
     grid_spec = pltpu.PrefetchScalarGridSpec(
         num_scalar_prefetch=0,
         grid=(steps,),
@@ -283,7 +321,7 @@
         + [pl.BlockSpec((width, QUAD), lambda j, n=n: (0, n * steps + j)) for n in range(3)],
         out_specs=[whole(rows, width)]
         + [pl.BlockSpec((rows, QUAD), lambda j: (0, j))] * 3
-        + [whole(rows, PAIR)]
+        + [pl.BlockSpec((1, rows, PAIR), lambda j: (j, 0, 0))]
         + [pl.BlockSpec((half, QUAD), lambda j: (0, j))] * 2,
         scratch_shapes=[pltpu.VMEM((half, QUAD), F32)] * 2,
     )
@@ -292,7 +330,7 @@
         "window_forward",
         (shape_of(BF16, rows, width),)
         + (shape_of(BF16, rows, width),) * 3
-        + (shape_of(F32, rows, PAIR),)
+        + (shape_of(F32, steps, rows, PAIR),)
         + (shape_of(BF16, half, width),) * 2,
         (normed, received, window_proj, window_proj, window_proj),
         2 * rows * width * (3 * width + 2 * size),
@@ -301,7 +339,7 @@
 
 
 FF_CHUNK = 512
-ROW_BLOCK = 144
+ROW_BLOCK = 192
 
 
 def visual_forward(received, top, stream, window_out, gain, up, down, pages_gain, keyval_proj, orders):
@@ -325,13 +363,14 @@
             hat, _ = norm_parts(mid)
             normed_ref[...] = (hat * g_ref[...]).astype(BF16)
 
+        cols = pl.ds(pl.multiple_of(step * FF_CHUNK, FF_CHUNK), FF_CHUNK)
         for block in range(rows // ROW_BLOCK):
             at = slice(block * ROW_BLOCK, (block + 1) * ROW_BLOCK)
             hidden = dot(normed_ref[at, :], up_ref[...])
             active, slope = gelu_parts(hidden)
             active = active.astype(BF16)
-            active_ref[at, :] = active
-            slope_ref[at, :] = slope.astype(BF16)
+            active_ref[at, cols] = active
+            slope_ref[at, cols] = slope.astype(BF16)
             final_ref[at, :] += dot(active, down_ref[...])
 
         @pl.when(step == steps - 1)
@@ -353,8 +392,8 @@
         ],
         out_specs=[
             whole(rows, width), whole(rows, width), whole(rows, width),
-            pl.BlockSpec((rows, FF_CHUNK), lambda j: (0, j)), pl.BlockSpec((rows, FF_CHUNK), lambda j: (0, j)),
-            whole(rows, width), whole(rows, width), whole(rows, 2 * width), whole(rows, width),
+            whole(rows, up.shape[1]), whole(rows, up.shape[1]),
+            whole(rows, width), whole(rows, width), whole(rows, 2 * width), window(rows, width),
         ],
     )
     return call(
@@ -538,7 +577,7 @@
             whole(own_count, width),
         ],
         out_specs=[
-            whole(own_count, width), whole(own_count, width), whole(own_count, width),
+            window(own_count, width), whole(own_count, width), whole(own_count, width),
             pl.BlockSpec((own_count, FF_CHUNK), lambda j, w: (0, j)), pl.BlockSpec((own_count, FF_CHUNK), lambda j, w: (0, j)),
             whole(own_count, width), whole(own_count, width), whole(own_count, width + STAT), whole(1, width),
         ],
@@ -686,7 +725,7 @@
         in_specs=[whole(own_count, width)] * 2
         + [whole(own_count, 2 * width), pl.BlockSpec((own_count, width), lambda j, w: (w[0], 0)), whole(own_count, width)]
         + [whole(1, width), whole(width, width), whole(width, 2 * width)],
-        out_specs=[whole(own_count, width), whole(own_count, width), whole(1, width)],
+        out_specs=[window(own_count, width), whole(own_count, width), whole(1, width)],
     )
     return call(
         kernel,
@@ -767,7 +806,7 @@
     )
 
 
-def window_backward(queries, keys, values, logs, top, received, window_proj):
+def window_backward(queries, keys, values, logs, top_context, low_context, top, received, window_proj):
     rows, width = queries.shape
     half = rows // 2
     part = half // WIN_ROW
@@ -775,7 +814,7 @@
     steps = width // QUAD
 
     def kernel(
-        q_ref, k_ref, v_ref, lse_ref, t_ref, r_ref, wq_ref, wk_ref, wv_ref,
+        q_ref, k_ref, v_ref, lse_ref, tc_ref, lc_ref, t_ref, r_ref, wq_ref, wk_ref, wv_ref,
         packed_ref, top_ref, low_ref, acc_sc, dq_ref, dk_ref, dv_ref,
     ):
         step = pl.program_id(0)
@@ -784,49 +823,57 @@
         def _():
             acc_sc[...] = jnp.zeros_like(acc_sc)
 
-        masks = head_masks()
-        lane = lanes_of(size)
-        low_lane = lane < HEAD_DIM
-        top = t_ref[...].astype(F32)
-        low = r_ref[...].astype(F32)
+        masks = quad_masks()
+        low_lane = lanes_of(size) < HEAD_DIM
+        top, low = t_ref[...].astype(F32), r_ref[...].astype(F32)
+        top_products, low_products = top * tc_ref[...].astype(F32), low * lc_ref[...].astype(F32)
+
+        def joined(first, second, k):
+            at = slice(k * part, (k + 1) * part)
+            return jnp.concatenate([first[at], second[at]], 0)
+
+        def own_lanes(x):
+            one = jnp.where(low_lane, x[:size, :PAIR], x[size : 2 * size, :PAIR])
+            two = jnp.where(low_lane, x[2 * size : 3 * size, PAIR:], x[3 * size :, PAIR:])
+            return jnp.concatenate([one, two], 1)
+
         for k in range(WIN_ROW):
             at = slice(k * size, (k + 1) * size)
-            grads = jnp.concatenate([top[k * part : (k + 1) * part], low[k * part : (k + 1) * part]], 0).astype(BF16)
-            stat = lse_ref[at, :]
-            for pair in range(QUAD // PAIR):
-                cols = slice(pair * PAIR, (pair + 1) * PAIR)
-                q2, k2, v2, g2 = q_ref[at, cols], k_ref[at, cols], v_ref[at, cols], grads[:, cols]
-                query_grad = None
-                key_grads, value_grads = [], []
-                for t in range(2):
-                    head = step * (QUAD // HEAD_DIM) + 2 * pair + t
-                    log = jnp.sum(jnp.where(lane == head, stat, 0.0), 1, keepdims=True)
-                    key = k2 * masks[t]
-                    share = jnp.exp(dot_t(q2, key) - log)
-                    share_grad = dot_t(g2, v2 * masks[t])
-                    along = jnp.sum(share * share_grad, -1, keepdims=True)
-                    score_grad = (share * (share_grad - along)).astype(BF16)
-                    part_grad = dot(score_grad, key)
-                    query_grad = part_grad if query_grad is None else query_grad + part_grad
-                    key_grads.append(t_dot(score_grad, q2))
-                    value_grads.append(t_dot(share.astype(BF16), g2))
-                dq_ref[at, cols] = (query_grad * SCALE).astype(BF16)
-                dk_ref[at, cols] = jnp.where(low_lane, key_grads[0], key_grads[1]).astype(BF16)
-                dv_ref[at, cols] = jnp.where(low_lane, value_grads[0], value_grads[1]).astype(BF16)
+            grads = joined(top, low, k).astype(BF16)
+            products = joined(top_products, low_products, k)
+            alongs = []
+            for pair in range(2):
+                product = products[:, pair * PAIR : (pair + 1) * PAIR]
+                alongs.append(jnp.sum(jnp.where(low_lane, product, 0.0), -1, keepdims=True))
+                alongs.append(jnp.sum(jnp.where(low_lane, 0.0, product), -1, keepdims=True))
+            queries4 = q_ref[at, :]
+            keys4 = by_head(k_ref[at, :], masks)
+            scores = dot_t(queries4, keys4)
+            share_grads = dot_t(grads, by_head(v_ref[at, :], masks))
+            stat = lse_ref[0, at, :]
+            log_tiles = spread([stat[:, h : h + 1] for h in range(4)], size, size)
+            along_tiles = spread(alongs, size, size)
+            shares, score_grads = [], []
+            for score, share_grad, log, along in zip(tiles_of(scores), tiles_of(share_grads), log_tiles, along_tiles):
+                share = jnp.exp(score - log)
+                shares.append(share)
+                score_grads.append(share * (share_grad - along))
+            share = jnp.concatenate(shares, 1).astype(BF16)
+            score_grad = jnp.concatenate(score_grads, 1).astype(BF16)
+            dq_ref[at, :] = (dot(score_grad, keys4) * SCALE).astype(BF16)
+            dk_ref[at, :] = own_lanes(t_dot(score_grad, queries4)).astype(BF16)
+            dv_ref[at, :] = own_lanes(t_dot(share, grads)).astype(BF16)
         acc_sc[...] += dot_t(dq_ref[...], wq_ref[...]) + dot_t(dk_ref[...], wk_ref[...]) + dot_t(dv_ref[...], wv_ref[...])
         for n, ref in enumerate((dq_ref, dk_ref, dv_ref)):
             packed_ref[:, pl.ds(pl.multiple_of(n * width + step * QUAD, QUAD), QUAD)] = ref[...]
 
         @pl.when(step == steps - 1)
         def _():
+            tops, lows = [], []
             for k in range(WIN_ROW):
                 at = k * size
-                top_piece, low_piece = acc_sc[at : at + part, :], acc_sc[at + part : at + size, :]
-                if k == 0:
-                    tops, lows = [top_piece], [low_piece]
-                else:
-                    tops.append(top_piece)
-                    lows.append(low_piece)
+                tops.append(acc_sc[at : at + part, :])
+                lows.append(acc_sc[at + part : at + size, :])
             top_ref[...] = jnp.concatenate(tops, 0).astype(BF16)
             low_ref[...] = jnp.concatenate(lows, 0).astype(BF16)
 
@@ -835,7 +882,8 @@
     grid_spec = pltpu.PrefetchScalarGridSpec(
         num_scalar_prefetch=0,
         grid=(steps,),
-        in_specs=[block, block, block, whole(rows, PAIR), half_block, half_block]
+        in_specs=[block, block, block, pl.BlockSpec((1, rows, PAIR), lambda j: (j, 0, 0))]
+        + [half_block] * 4
         + [pl.BlockSpec((width, QUAD), lambda j, n=n: (0, n * steps + j)) for n in range(3)],
         out_specs=[whole(rows, 3 * width), whole(half, width), whole(half, width)],
         scratch_shapes=[pltpu.VMEM((rows, width), F32)] + [pltpu.VMEM((rows, QUAD), BF16)] * 3,
@@ -844,7 +892,7 @@
         kernel,
         "window_backward",
         (shape_of(BF16, rows, 3 * width),) + (shape_of(BF16, half, width),) * 2,
-        (queries, keys, values, logs, top, received, window_proj, window_proj, window_proj),
+        (queries, keys, values, logs, top_context, low_context, top, received, window_proj, window_proj, window_proj),
         2 * rows * width * (3 * width + 5 * size),
         grid_spec=grid_spec,
     )
@@ -906,6 +954,7 @@
             scratch_shapes=scratch,
         ),
         cost_estimate=pl.CostEstimate(flops=flops, bytes_accessed=size, transcendentals=0),
+        compiler_params=pltpu.CompilerParams(vmem_limit_bytes=30 << 20),
         **extra,
     )(*args)
 
@@ -943,7 +992,10 @@
         send_ref[...] = sent.astype(BF16).reshape(send_ref.shape)
 
     if split:
-        out_block = pl.BlockSpec((1, count, block, tile), lambda n, p, w: (n ^ w[0], 0, offset // block, 0))
+        per = steps // 2
+        out_block = pl.BlockSpec(
+            (1, count, block, tile), lambda n, p, w: ((n // per) ^ w[0], 0, offset // block + n % per, 0)
+        )
     else:
         out_block = pl.BlockSpec((1, count, block, tile), lambda n, p, w: (0, 0, offset // block + n, 0))
     in_specs = [whole(*left.shape) for left, _ in pairs] + [
@@ -1012,7 +1064,8 @@
     def prepare(self):
         name = self.todo[0]
         if name == "0":
-            return self.sent
+            self.parts[0], sent = lax.optimization_barrier((self.parts[0], self.sent))
+            return sent
         if name == "last":
             return total([part[0] for part in self.parts])
         if name == "win":
@@ -1046,35 +1099,39 @@
 class SmallSum:
     def __init__(self, vectors):
         self.count = len(vectors)
-        self.value = jnp.concatenate(vectors + [jnp.zeros((8 - len(vectors), D), F32)], 0)
+        self.parts = [jnp.concatenate(vectors + [jnp.zeros((8 - len(vectors), D), F32)], 0)]
         self.todo = list(range(lax.axis_size("page").bit_length() - 1)) + ["win"]
 
     def prepare(self):
-        return self.value
+        self.parts = [sum(self.parts)]
+        return self.parts[0]
 
     def launch(self, sent):
         name = self.todo.pop(0)
-        self.value = sent + (swap_win(sent) if name == "win" else swap_page(sent, name))
+        self.parts.append(swap_win(sent) if name == "win" else swap_page(sent, name))
 
     def finish(self):
         size = D // lax.axis_size("page")
-        own = lax.dynamic_slice_in_dim(self.value, lax.axis_index("page") * size, size, 1)
+        own = lax.dynamic_slice_in_dim(sum(self.parts), lax.axis_index("page") * size, size, 1)
         return [own[n] for n in range(self.count)]
 
 
-def pump(anchor, *sums, after=()):
-    values = lax.optimization_barrier((anchor, *(r.prepare() for r in sums), *after))
-    for r, sent in zip(sums, values[1:]):
-        r.launch(sent)
-    return values[0]
-
-
-def drain(*sums):
-    while any(r.todo for r in sums):
-        live = [r for r in sums if r.todo]
-        for r, sent in zip(live, lax.optimization_barrier(tuple(r.prepare() for r in live))):
-            r.launch(sent)
-    return [r.finish() for r in sums]
+class Order:
+    def __init__(self, token):
+        self.token = token
+
+    def before(self, value):
+        value, self.token = lax.optimization_barrier((value, self.token))
+        return value
+
+    def after(self, value):
+        self.token = value
+
+    def step(self, *sums):
+        for one in sums:
+            one.parts[-1] = self.before(one.parts[-1])
+            self.token = one.prepare()
+            one.launch(self.token)
 
 
 def untile(rows, start, count, block):
@@ -1102,6 +1159,9 @@
     text = text_in[0]
     text_up_stream = text_upstream[0]
     tie = lax.optimization_barrier
+    visual_up_hbm, visual_down_hbm, text_up_hbm, text_down_hbm, window_proj_hbm = (
+        from_hbm(w) for w in (visual_up, visual_down, text_up, text_down, window_proj)
+    )
     count = pages // 2
     block = D // pages
     tall = FF // pages
@@ -1110,79 +1170,109 @@
     ahead = swap_win(first_normed)
     queries, text_normed, text_kv = text_pre(own_index, text, g_text, text_query, keyval_proj, own_count)
     ahead, queries = tie((ahead, queries))
-    shifted, win_q, win_k, win_v, win_log, top, low = window_forward(normed, ahead, window_proj)
+    shifted, win_q, win_k, win_v, win_log, top, low = window_forward(normed, ahead, window_proj_hbm)
     behind = swap_win(low)
     unshifted, mid, ff_normed, active, slope, final, pages_normed, page_kv, visual_out = visual_forward(
-        behind, top, stream, window_out, g_visual, visual_up, visual_down, g_pages, keyval_proj, orders
+        behind, top, stream, window_out, g_visual, visual_up_hbm, visual_down_hbm, g_pages, keyval_proj, orders
     )
     away = cross_forward(other_index, queries, page_kv, text_kv, text_mask)
     theirs = swap_win(away)
     mine = cross_forward(first_index, queries, page_kv, text_kv, text_mask)
     theirs, mine = tie((theirs, mine))
     (text_out, context, reply_normed, text_active, text_hidden_grad, text_mid_grad, branch, pack, reply_gain) = text_block(
-        own_index, mine, theirs, text, cross_out, g_reply, text_up, text_down, text_up_stream
+        own_index, mine, theirs, text, cross_out, g_reply, text_up_hbm, text_down_hbm, text_up_stream
     )
     pack_other = swap_win(pack)
+    order = Order(pack)
     at = (1, count, tall + block, D)
-    first = narrow_grad(where, [(reply_normed, text_hidden_grad)], at, 0, None, "text_up_grad")
-    first = narrow_grad(where, [(context, branch)], at, tall, first, "cross_out_grad")
-    reply_a = Reduction(*first, False)
-    text_active = pump(text_active, reply_a)
-    second = wide_grad(where, text_active, text_up_stream, (2, count, tall // 2, D), 0, None, "text_down_grad")
-    reply_b = Reduction(*second, True)
-    pack_other = pump(pack_other, reply_a, reply_b)
+    grads = narrow_grad(where, [(reply_normed, text_hidden_grad)], at, 0, None, "text_up_grad")
+    grads = narrow_grad(where, [(context, branch)], at, tall, grads, "cross_out_grad")
+    reply_a = Reduction(*grads, False)
+    order.step(reply_a)
+    grads = wide_grad(
+        where, order.before(text_active), text_up_stream, (2, count, tall // 2, D), 0, None, "text_down_grad"
+    )
+    reply_b = Reduction(*grads, True)
+    order.after(grads[0])
+    order.step(reply_a, reply_b)
+    pack_other = order.before(pack_other)
+    order.after(pack_other)
+    order.step(reply_b)
     page_kv_grad, text_kv_grad, query_mine, query_away = cross_backward(
-        other_index, queries, page_kv, text_kv, text_mask, pack, pack_other
-    )
+        other_index, queries, page_kv, text_kv, text_mask, pack, order.before(pack_other)
+    )
+    order.after(page_kv_grad)
+    order.step(reply_a, reply_b)
     query_theirs = swap_win(query_away)
-    page_kv_grad = pump(page_kv_grad, reply_b)
     (out_grad, hidden_grad, mid_grad, window_branch, context_first, context_second, pages_gain, visual_gain) = visual_backward(
-        page_kv_grad, keyval_proj, final, visual_upstream.reshape(rows, D), orders, g_pages, mid, g_visual,
-        window_out, visual_up, visual_down, slope,
+        order.before(page_kv_grad), keyval_proj, final, visual_upstream.reshape(rows, D), orders, g_pages, mid, g_visual,
+        window_out, visual_up_hbm, visual_down_hbm, slope,
     )
     later = swap_win(context_first)
-    hidden_grad = pump(hidden_grad, reply_a, reply_b, after=(query_theirs,))
-    at = (1, count, tall + 2 * block, D)
-    third = narrow_grad(where, [(ff_normed, hidden_grad)], at, 0, None, "visual_up_grad")
-    third = narrow_grad(where, [(unshifted, window_branch)], at, tall, third, "window_out_grad")
+    order.after(out_grad)
+    order.step(reply_a, reply_b)
+    grads = wide_grad(where, order.before(active), out_grad, (2, count, tall // 2, D), 0, None, "visual_down_grad")
+    visual_b = Reduction(*grads, True)
+    order.after(grads[0])
+    order.step(visual_b)
+    grads = narrow_grad(
+        where, [(order.before(ff_normed), hidden_grad)], (1, count, tall, D), 0, None, "visual_up_grad"
+    )
+    visual_a = Reduction(*grads, False)
+    order.after(grads[0])
+    order.step(visual_a, visual_b, reply_b)
     text_grad, query_grad, text_gain = text_tail(
-        own_index, query_mine, query_theirs, text_kv_grad, text, text_mid_grad, g_text, text_query, keyval_proj
-    )
-    third = narrow_grad(where, [(text_normed, query_grad)], at, tall + block, third, "text_query_grad")
-    visual_a = Reduction(*third, False)
-    active = pump(active, reply_a, reply_b, visual_a)
-    at_b = (2, count, tall // 2 + block, D)
-    fourth = wide_grad(where, active, out_grad, at_b, 0, None, "visual_down_grad")
-    fourth = narrow_grad(
-        where, [(text_normed, text_kv_grad), (pages_normed, page_kv_grad)], at_b, tall // 2, fourth, "keyval_grad", split=True
-    )
-    visual_b = Reduction(*fourth, True)
-    later = pump(later, reply_a, reply_b, visual_a, visual_b)
-    packed_grad, top_grad, low_grad = window_backward(win_q, win_k, win_v, win_log, context_second, later, window_proj)
+        own_index, query_mine, order.before(query_theirs), text_kv_grad, text, text_mid_grad, g_text, text_query, keyval_proj
+    )
+    at = (1, count, 4 * block, D)
+    at_b = (2, count, 3 * block, D // 2)
+    grads_a = narrow_grad(where, [(text_normed, query_grad)], at, 2 * block, None, "text_query_grad")
+    grads_a = narrow_grad(where, [(unshifted, window_branch)], at, 3 * block, grads_a, "window_out_grad")
+    order.after(grads_a[0])
+    order.step(visual_a)
+    pairs = [(order.before(text_normed), text_kv_grad), (pages_normed, page_kv_grad)]
+    grads_b = narrow_grad(where, pairs, at_b, 0, None, "keyval_grad", D // 2, split=True)
+    order.after(grads_b[0])
+    order.step(reply_a)
+    packed_grad, top_grad, low_grad = window_backward(
+        win_q, win_k, win_v, win_log, top, low, context_second, order.before(later), window_proj_hbm
+    )
     earlier = swap_win(low_grad)
-    packed_grad = pump(packed_grad, reply_b, visual_b)
-    fifth = narrow_grad(where, [(shifted, packed_grad)], (1, count, 2 * block, D), 0, None, "window_proj_grad", steps=2)
-    sixth = narrow_grad(
-        where, [(shifted, packed_grad)], (2, count, block, D // 2), 0, None, "window_value_grad", D // 2, 4, 2, True
-    )
-    window_a = Reduction(*fifth, False)
-    window_b = Reduction(*sixth, True)
-    earlier = pump(earlier, window_a, window_b)
-    visual_grad, window_gain, embed_grad = visual_tail(earlier, top_grad, stream, mid_grad, mark, g_window, orders)
+    order.after(packed_grad)
+    order.step(reply_b)
+    grads_a = narrow_grad(where, [(shifted, order.before(packed_grad))], at, 0, grads_a, "window_proj_grad", steps=2)
+    window_a = Reduction(*grads_a, False)
+    order.after(grads_a[0])
+    order.step(visual_b, visual_a)
+    grads_b = narrow_grad(
+        where, [(shifted, order.before(packed_grad))], at_b, 2 * block, grads_b, "window_value_grad", D // 2, 4, 2, True
+    )
+    window_b = Reduction(*grads_b, True)
+    order.after(grads_b[0])
+    order.step(window_a, window_b, window_a, window_b)
+    visual_grad, window_gain, embed_grad = visual_tail(
+        order.before(earlier), top_grad, stream, mid_grad, mark, g_window, orders
+    )
     sums = SmallSum([window_gain, visual_gain, text_gain, pages_gain, reply_gain, embed_grad])
-    visual_a, visual_b, window_a, window_b, sums = drain(visual_a, visual_b, window_a, window_b, sums)
-    reply_a, reply_b = reply_a.finish(), reply_b.finish()
+    order.after(window_gain)
+    order.step(sums, visual_b, visual_a, window_a, sums, window_b, visual_b, visual_a, sums, window_a, window_b)
+    order.step(visual_b, sums, window_a, window_b, sums, window_b)
+    left = [one for one in (reply_a, reply_b, visual_a, visual_b, window_a, window_b, sums) if one.todo]
+    assert not left
+    reply_a, reply_b, visual_a, visual_b, window_a, window_b, sums = (
+        one.finish() for one in (reply_a, reply_b, visual_a, visual_b, window_a, window_b, sums)
+    )
     return (
         visual_out.reshape(visual_in.shape),
         text_out[None],
         visual_grad.reshape(visual_in.shape),
         text_grad[None],
-        jnp.concatenate([untile(window_a, 0, 2, block), window_b[0], window_b[1]], 1),
-        visual_a[tall : tall + block],
+        jnp.concatenate([untile(window_a, 0, 2, block), window_b[0, 2 * block :], window_b[1, 2 * block :]], 1),
+        window_a[3 * block :],
         untile(visual_a, 0, FF // D, block),
-        visual_b[:, : tall // 2].reshape(tall, D),
-        visual_a[tall + block :],
-        jnp.concatenate([visual_b[0, tall // 2 :], visual_b[1, tall // 2 :]], 1),
+        visual_b.reshape(tall, D),
+        window_a[2 * block : 3 * block],
+        jnp.concatenate([window_b[h, n * block : (n + 1) * block] for h in range(2) for n in range(2)], 1),
         reply_a[tall:],
         untile(reply_a, 0, FF // D, block),
         reply_b.reshape(tall, D),

time: 452 us -> 390 us (0.86)
  Pallas kernels: 224 us -> 156 us
  local copies, waits for them, and re-layouts: 12.6 us -> 38.7 us
  other arithmetic: 60.5 us -> 42.9 us
    pallas_call x12, Pallas kernels: 167 us -> 119 us  [call(): pl.pallas_call(kernel, out_shape=out_shape, name=name, cost_estimate=pl.C...]
    unnamed x33 -> x205, local copies, waits for them, and re-layouts: 4.32 us -> 35 us
    pallas_call x10, Pallas kernels: 56.9 us -> 36.9 us  [grad_call(): pl.pallas_call(kernel, out_shape=(shape_of(BF16, *at),) * 2, name=name, g...]
    convert_element_type x27, other arithmetic: 52.2 us -> 35.3 us  [total(): return result.astype(BF16)]
  transfers between devices with their start and end apart: 45 -> 45, of which waited for: 16 -> 18; matrix products, arithmetic and copies ran while one was open for 13% -> 11% of each run, Pallas kernels for 33% -> 23%
where the time goes in v2:
time: 390 us; the launch traced here: 386 us
  Pallas kernels  156 us (40%)
  waiting for transfers between devices  104 us (27%)
  starting transfers between devices  42.9 us (11%)
  other arithmetic  42.9 us (11%)
  local copies, waits for them, and re-layouts  38.7 us (10%)
    pallas_call x12, Pallas kernels, call(): pl.pallas_call(kernel, out_shape=out_shape, name=name, cost_estimate=pl.C...  119 us
    ppermute x28, waiting for transfers between devices, swap_page(): lax.ppermute(x, 'page', [(i, i ^ 1 << bit) for i in range(lax.axis_size('...  59.3 us
    ppermute x17, waiting for transfers between devices, swap_win(): return lax.ppermute(x, 'win', [(0, 1), (1, 0)])  44.5 us
    pallas_call x10, Pallas kernels, grad_call(): pl.pallas_call(kernel, out_shape=(shape_of(BF16, *at),) * 2, name=name, g...  36.9 us
    convert_element_type x27, other arithmetic, total(): return result.astype(BF16)  35.3 us
    unnamed x205, local copies, waits for them, and re-layouts  35 us
    ppermute x28, starting transfers between devices, swap_page(): lax.ppermute(x, 'page', [(i, i ^ 1 << bit) for i in range(lax.axis_size('...  23.3 us
    ppermute x17, starting transfers between devices, swap_win(): return lax.ppermute(x, 'win', [(0, 1), (1, 0)])  19.6 us
  transfers between devices with their start and end apart: 45, of which 18 were waited for; matrix products, arithmetic and copies ran while one was open for 11% of the time, Pallas kernels for 23%

profile of v2, /device:TPU:0, one launch (start us, length us, event | category | flops | bytes accessed | tf_op | source)
XLA Modules:
  0.0 386.0 jit_solution(8881601327548474022)
XLA Ops:
  9.0 2.9 collective-permute-start
  16.6 5.7 %collective-permute-done.r_ref = bf16[288,768]{1,0:T(8,128)(2,1)S(1)} collective-permute-done((bf16[288,768]{1,0:T(8,128)(2,1)}, bf16[288,768]{1,0:T(8,128)(2,1)S(1)}, u32[]{:S(2)}, u32[]{:S(2)}) %collective-permute-start) | collective-permute-done | bytes 442400 | tf_op jit(solution)/shard_map/ppermute | solution.py:1046
  24.1 10.6 %window_forward.1 = (bf16[576,768]{1,0:T(8,128)(2,1)S(1)}, bf16[576,768]{1,0:T(8,128)(2,1)S(1)}, bf16[576,768]{1,0:T(8,128)(2,1)S(1)}, bf16[576,768]{1,0:T(8,128...) custom-call(bf16[288,768]{1,0:T(8,128)(2,1)S(1)} %get-tuple-element.156.n_ref, ...), custom_call_target="tpu_custom_call" | custom-call | flops 2293235712 | bytes 16809984 | tf_op jit(solution)/shard_map/window_forward/pallas_call | solution.py:124
  42.0 8.7 %collective-permute-done.1.r_ref = bf16[288,768]{1,0:T(8,128)(2,1)S(1)} collective-permute-done((bf16[288,768]{1,0:T(8,128)(2,1)S(1)}, bf16[288,768]{1,0:T(8,128)(2,1)S(1)}, u32[]{:S(2)}, u32[]{:S(2)}) %collective-permute-start.1) | collective-permute-done | bytes 442400 | tf_op jit(solution)/shard_map/ppermute | solution.py:1046
  57.9 18.5 %visual_forward.1 = (bf16[576,768]{1,0:T(8,128)(2,1)S(1)}, f32[576,768]{1,0:T(8,128)S(1)}, bf16[576,768]{1,0:T(8,128)(2,1)S(1)}, bf16[576,3072]{1,0:T(8,128)(2,1...) custom-call(bf16[288,768]{1,0:T(8,128)(2,1)S(1)} %copy-done.51, ...), custom_call_target="tpu_custom_call" | custom-call | flops 7983857664 | bytes 31570944 | tf_op jit(solution)/shard_map/visual_forward/pallas_call | solution.py:124
  81.8 7.8 %cross_forward.2 = bf16[200,896]{1,0:T(8,128)(2,1)} custom-call(s32[2]{0:T(128)S(1)} %pad_add_fusion.i_ref, bf16[400,768]{1,0:T(8,128)(2,1)S(1)} %copy-done.12, bf16[576,1536]{1,0:T(8,128)(2,1)S(1)} %get-tuple-element.165.pk_ref.pv_ref, bf16[576,1536]{1,0:T(8,128)(2,1)S(1)} %get-tuple-element.165.pk_ref.pv_ref, ...), custom_call_target="tpu_custom_call" | custom-call | flops 953548800 | bytes 5742152 | tf_op jit(solution)/shard_map/cross_forward/pallas_call | solution.py:124
  92.1 7.4 %cross_forward.3.a_ref = bf16[200,896]{1,0:T(8,128)(2,1)S(1)} custom-call(s32[2]{0:T(128)S(1)} %pad_add_fusion.1.i_ref, bf16[400,768]{1,0:T(8,128)(2,1)S(1)} %copy-done.13, bf16[576,1536]{1,0:T(8,128)(2,1)S(1)} %get-tuple-element.165.pk_ref.pv_ref, bf16[576,1536]{1,0:T(8,128)(2,1)S(1)} %get-tuple-element.165.pk_ref.pv_ref, ...), custom_call_target="tpu_custom_call" | custom-call | flops 953548800 | bytes 5742152 | tf_op jit(solution)/shard_map/cross_forward/pallas_call | solution.py:124
  99.6 13.8 %text_block.1 = (bf16[200,768]{1,0:T(8,128)(2,1)}, bf16[200,768]{1,0:T(8,128)(2,1)S(1)}, bf16[200,768]{1,0:T(8,128)(2,1)S(1)}, bf16[200,3072]{1,0:T(8,128)(2,1)S...) custom-call(s32[1]{0:T(128)} %bitcast.1.w_ref, ...), custom_call_target="tpu_custom_call" | custom-call | flops 4246732800 | bytes 16920580 | tf_op jit(solution)/shard_map/text_block/pallas_call | solution.py:124
  117.4 3.8 text_down_grad.1
  125.4 8.6 %collective-permute-done.3.b_ref = bf16[200,896]{1,0:T(8,128)(2,1)S(1)} collective-permute-done((bf16[200,896]{1,0:T(8,128)(2,1)S(1)}, bf16[200,896]{1,0:T(8,128)(2,1)S(1)}, u32[]{:S(2)}, u32[]{:S(2)}) %collective-permute-start.3) | collective-permute-done | bytes 358432 | tf_op jit(solution)/shard_map/ppermute | solution.py:1046
  135.5 18.7 %cross_backward.1 = (bf16[576,1536]{1,0:T(8,128)(2,1)S(1)}, bf16[200,1536]{1,0:T(8,128)(2,1)S(1)}, f32[200,768]{1,0:T(8,128)S(1)}, bf16[200,768]{1,0:T(8,128)(2,1)S(1)}) custom-call(s32[2]{0:T(128)S(1)} %pad_add_fusion.i_ref, bf16[400,768]{1,0:T(8,128)(2,1)S(1)} %copy-done.14, bf16[400,768]{1,0:T(8,128)(2,1)S(1)} %copy-done.14, ...), custom_call_target="tpu_custom_call" | custom-call | flops 4767744000 | bytes 10020424 | tf_op jit(solution)/shard_map/cross_backward/pallas_call | solution.py:124
  154.3 4.0 %collective-permute-done.7 = bf16[4,240,768]{2,1,0:T(8,128)(2,1)S(1)} collective-permute-done((bf16[4,240,768]{2,1,0:T(8,128)(2,1)S(1)}, bf16[4,240,768]{2,1,0:T(8,128)(2,1)S(1)}, u32[]{:S(2)}, u32[]{:S(2)}) %collective-permute-start.7) | collective-permute-done | bytes 1474592 | tf_op jit(solution)/shard_map/ppermute | solution.py:1042
  165.8 18.2 %visual_backward.1 = (bf16[576,768]{1,0:T(8,128)(2,1)S(1)}, bf16[576,3072]{1,0:T(8,128)(2,1)S(1)}, f32[576,768]{1,0:T(8,128)S(1)}, bf16[576,768]{1,0:T(8,128)(2,...) custom-call(bf16[576,1536]{1,0:T(8,128)(2,1)S(1)} %get-tuple-element, ...), custom_call_target="tpu_custom_call" | custom-call | flops 7983857664 | bytes 30692352 | tf_op jit(solution)/shard_map/visual_backward/pallas_call | solution.py:124
  183.9 2.6 fusion.14
  188.0 8.6 %visual_down_grad.1 = (bf16[2,8,96,768]{3,2,1,0:T(8,128)(2,1)S(1)}, bf16[2,8,96,768]{3,2,1,0:T(8,128)(2,1)S(1)}) custom-call(s32[1]{0:T(128)} %bitcast.7.p_ref, s32[1]{0:T(128)} %bitcast.1.w_ref, bf16[576,3072]{1,0:T(8,128)(2,1)S(1)} %copy-done.71, bf16[576,768]{1,0:T(8,128)(2,1)S(1)} %get-tuple-element.206.r_ref), custom_call_target="tpu_custom_call" | custom-call | flops 2717908992 | bytes 4423680 | tf_op jit(solution)/shard_map/visual_down_grad/pallas_call | solution.py:945
  196.7 5.3 %visual_up_grad.1 = (bf16[1,8,192,768]{3,2,1,0:T(8,128)(2,1)S(1)}, bf16[1,8,192,768]{3,2,1,0:T(8,128)(2,1)S(1)}) custom-call(s32[1]{0:T(128)} %bitcast.7.p_ref, s32[1]{0:T(128)} %bitcast.1.w_ref, bf16[576,768]{1,0:T(8,128)(2,1)S(1)} %copy-done.81, bf16[576,3072]{1,0:T(8,128)(2,1)S(1)} %get-tuple-element.217.refs_1_), custom_call_target="tpu_custom_call" | custom-call | flops 2717908992 | bytes 4423680 | tf_op jit(solution)/shard_map/visual_up_grad/pallas_call | solution.py:945
  209.1 10.9 %collective-permute-done.14 = bf16[2,96,768]{2,1,0:T(8,128)(2,1)S(1)} collective-permute-done((bf16[2,96,768]{2,1,0:T(8,128)(2,1)S(1)}, bf16[2,96,768]{2,1,0:T(8,128)(2,1)S(1)}, u32[]{:S(2)}, u32[]{:S(2)}) %collective-permute-start.14) | collective-permute-done | bytes 294944 | tf_op jit(solution)/shard_map/ppermute | solution.py:1042
  233.8 5.8 %keyval_grad.1 = (bf16[2,8,144,384]{3,2,1,0:T(8,128)(2,1)S(1)}, bf16[2,8,144,384]{3,2,1,0:T(8,128)(2,1)}) custom-call(s32[1]{0:T(128)} %bitcast.7.p_ref, s32[1]{0:T(128)} %bitcast.1.w_ref, bf16[200,768]{1,0:T(8,128)(2,1)S(1)} %copy-done.54, bf16[576,768]{1,0:T(8,128)(2,1)S(1)} %copy-done.73, bf16[200,1536]{1,0:T(8,128)(2,1)S(1)} %copy-done.31, ...), custom_call_target="tpu_custom_call" | custom-call | flops 1830813696 | bytes 1191936 | tf_op jit(solution)/shard_map/keyval_grad/pallas_call | solution.py:945
  241.9 13.2 %window_backward.1 = (bf16[576,2304]{1,0:T(8,128)(2,1)S(1)}, bf16[288,768]{1,0:T(8,128)(2,1)S(1)}, bf16[288,768]{1,0:T(8,128)(2,1)S(1)}) custom-call(bf16[576,768]{1,0:T(8,128)(2,1)S(1)} %copy-done.21, bf16[576,768]{1,0:T(8,128)(2,1)S(1)} %copy-done.23, bf16[576,768]{1,0:T(8,128)(2,1)S(1)} %copy-done.25, f32[3,576,128]{2,1,0:T(8,128)S(1)} %copy-done.27, ...), custom_call_target="tpu_custom_call" | custom-call | flops 2675441664 | bytes 19464192 | tf_op jit(solution)/shard_map/window_backward/pallas_call | solution.py:124
  257.4 3.6 window_proj_grad.1
  264.8 3.0 window_value_grad.1
  272.0 9.3 %collective-permute-done.42 = bf16[240,768]{1,0:T(8,128)(2,1)} collective-permute-done((bf16[240,768]{1,0:T(8,128)(2,1)}, bf16[240,768]{1,0:T(8,128)(2,1)}, u32[]{:S(2)}, u32[]{:S(2)}) %collective-permute-start.42) | collective-permute-done | bytes 368672 | tf_op jit(solution)/shard_map/ppermute | solution.py:1046
  283.2 2.7 fusion.5
  291.3 4.8 %visual_tail.1 = (f32[576,768]{1,0:T(8,128)}, f32[1,768]{1,0:T(1,128)S(1)}, f32[1,768]{1,0:T(1,128)S(1)}) custom-call(bf16[288,768]{1,0:T(8,128)(2,1)S(1)} %collective-permute-done.16.r_ref, bf16[288,768]{1,0:T(8,128)(2,1)S(1)} %copy-done.47, f32[576,768]{1,0:T(8,128)S(1)} %copy-done.63, f32[576,768]{1,0:T(8,128)S(1)} %copy-done.65, ...), custom_call_target="tpu_custom_call" | custom-call | flops 1528823808 | bytes 6506496 | tf_op jit(solution)/shard_map/visual_tail/pallas_call | solution.py:124
  296.1 3.0 collective-permute-done.24
  303.0 18.5 %collective-permute-done.22 = bf16[4,192,768]{2,1,0:T(8,128)(2,1)} collective-permute-done((bf16[4,192,768]{2,1,0:T(8,128)(2,1)}, bf16[4,192,768]{2,1,0:T(8,128)(2,1)}, u32[]{:S(2)}, u32[]{:S(2)}) %collective-permute-start.22) | collective-permute-done | bytes 1179680 | tf_op jit(solution)/shard_map/ppermute | solution.py:1042
  329.5 5.3 %collective-permute-done.28 = bf16[1,192,768]{2,1,0:T(8,128)(2,1)S(1)} collective-permute-done((bf16[1,192,768]{2,1,0:T(8,128)(2,1)S(1)}, bf16[1,192,768]{2,1,0:T(8,128)(2,1)S(1)}, u32[]{:S(2)}, u32[]{:S(2)}) %collective-permute-start.28) | collective-permute-done | bytes 294944 | tf_op jit(solution)/shard_map/ppermute | solution.py:1042
  338.4 6.4 %collective-permute-done.40 = bf16[192,768]{1,0:T(8,128)(2,1)S(1)} collective-permute-done((bf16[192,768]{1,0:T(8,128)(2,1)S(1)}, bf16[192,768]{1,0:T(8,128)(2,1)S(1)}, u32[]{:S(2)}, u32[]{:S(2)}) %collective-permute-start.40) | collective-permute-done | bytes 294944 | tf_op jit(solution)/shard_map/ppermute | solution.py:1046
  346.0 2.9 collective-permute-done.34
  358.8 7.9 %collective-permute-done.31 = bf16[1,192,768]{2,1,0:T(8,128)(2,1)S(1)} collective-permute-done((bf16[1,192,768]{2,1,0:T(8,128)(2,1)S(1)}, bf16[1,192,768]{2,1,0:T(8,128)(2,1)S(1)}, u32[]{:S(2)}, u32[]{:S(2)}) %collective-permute-start.31) | collective-permute-done | bytes 294944 | tf_op jit(solution)/shard_map/ppermute | solution.py:1042
  373.2 4.3 %collective-permute-done.37 = bf16[1,144,384]{2,1,0:T(8,128)(2,1)S(1)} collective-permute-done((bf16[1,144,384]{2,1,0:T(8,128)(2,1)S(1)}, bf16[1,144,384]{2,1,0:T(8,128)(2,1)S(1)}, u32[]{:S(2)}, u32[]{:S(2)}) %collective-permute-start.37) | collective-permute-done | bytes 110624 | tf_op jit(solution)/shard_map/ppermute | solution.py:1042
  380.3 3.0 collective-permute-done.39
  (343 shorter events, 134.3 us)
Async XLA Ops:
  9.0 13.3 %collective-permute-start = (bf16[288,768]{1,0:T(8,128)(2,1)}, bf16[288,768]{1,0:T(8,128)(2,1)S(1)}, u32[]{:S(2)}, u32[]{:S(2)}) collective-permute-start(bf16[288,768]{1,0:T(8,128)(2,1)} %get-tuple-element.157), channel_id=1, source_target_pairs={{0,1},{1,0},{2,3},{3,2},{4,5},{5,4},{6,7},{7,6},{8,9},{9,8},{10,11... | collective-permute-start | bytes 1327112 | tf_op jit(solution)/shard_map/ppermute | solution.py:1046
  124.0 34.3 %collective-permute-start.7 = (bf16[4,240,768]{2,1,0:T(8,128)(2,1)S(1)}, bf16[4,240,768]{2,1,0:T(8,128)(2,1)S(1)}, u32[]{:S(2)}, u32[]{:S(2)}) collective-permute-start(bf16[4,240,768]{2,1,0:T(8,128)(2,1)S(1)} %fusion), channel_id=1, source_target_pairs={{0,4},{2,6},{4,0},{6,2},{8,12},{10,14},{12,8},{14,10},{16,20},{18,... | collective-permute-start | bytes 4423688 | tf_op jit(solution)/shard_map/ppermute | solution.py:1042
  134.3 27.5 %collective-permute-start.6 = (bf16[8,96,768]{2,1,0:T(8,128)(2,1)S(1)}, bf16[8,96,768]{2,1,0:T(8,128)(2,1)S(1)}, u32[]{:S(2)}, u32[]{:S(2)}) collective-permute-start(bf16[8,96,768]{2,1,0:T(8,128)(2,1)S(1)} %fusion.2), channel_id=1, source_target_pairs={{0,1},{1,0},{2,3},{3,2},{4,5},{5,4},{6,7},{7,6},{8,9},{9,8},{10,11... | collective-permute-start | bytes 3538952 | tf_op jit(solution)/shard_map/ppermute | solution.py:1046
  158.6 25.3 %collective-permute-start.9 = (bf16[2,240,768]{2,1,0:T(8,128)(2,1)S(1)}, bf16[2,240,768]{2,1,0:T(8,128)(2,1)S(1)}, u32[]{:S(2)}, u32[]{:S(2)}) collective-permute-start(bf16[2,240,768]{2,1,0:T(8,128)(2,1)S(1)} %fusion.1), channel_id=1, source_target_pairs={{0,8},{2,10},{4,12},{6,14},{8,0},{10,2},{12,4},{14,6},{16,24},{18,... | collective-permute-start | bytes 2211848 | tf_op jit(solution)/shard_map/ppermute | solution.py:1042
  162.1 24.4 %collective-permute-start.11 = (bf16[4,96,768]{2,1,0:T(8,128)(2,1)S(1)}, bf16[4,96,768]{2,1,0:T(8,128)(2,1)S(1)}, u32[]{:S(2)}, u32[]{:S(2)}) collective-permute-start(bf16[4,96,768]{2,1,0:T(8,128)(2,1)S(1)} %fusion.9), channel_id=1, source_target_pairs={{0,4},{2,6},{4,0},{6,2},{8,12},{10,14},{12,8},{14,10},{16,20},{18,... | collective-permute-start | bytes 1769480 | tf_op jit(solution)/shard_map/ppermute | solution.py:1042
  202.0 29.2 %collective-permute-start.12 = (bf16[1,8,192,768]{3,2,1,0:T(8,128)(2,1)S(1)}, bf16[1,8,192,768]{3,2,1,0:T(8,128)(2,1)S(1)}, u32[]{:S(2)}, u32[]{:S(2)}) collective-permute-start(bf16[1,8,192,768]{3,2,1,0:T(8,128)(2,1)S(1)} %get-tuple-element.221), channel_id=1, source_target_pairs={{0,2},{2,0},{4,6},{6,4},{8,10},{10,8},{12,14},{14,12},{16,18},{18,... | collective-permute-start | bytes 7077896 | tf_op jit(solution)/shard_map/ppermute | solution.py:1042
  202.6 20.2 %collective-permute-start.13 = (bf16[200,768]{1,0:T(8,128)(2,1)S(1)}, bf16[200,768]{1,0:T(8,128)(2,1)S(1)}, u32[]{:S(2)}, u32[]{:S(2)}) collective-permute-start(bf16[200,768]{1,0:T(8,128)(2,1)S(1)} %copy-done.56), channel_id=1, source_target_pairs={{0,1},{1,0},{2,3},{3,2},{4,5},{5,4},{6,7},{7,6},{8,9},{9,8},{10,11... | collective-permute-start | bytes 921608 | tf_op jit(solution)/shard_map/ppermute | solution.py:1046
  203.1 36.6 %collective-permute-start.10 = (bf16[1,240,768]{2,1,0:T(8,128)(2,1)}, bf16[1,240,768]{2,1,0:T(8,128)(2,1)S(1)}, u32[]{:S(2)}, u32[]{:S(2)}) collective-permute-start(bf16[1,240,768]{2,1,0:T(8,128)(2,1)} %fusion.14), channel_id=1, source_target_pairs={{0,16},{2,18},{4,20},{6,22},{8,24},{10,26},{12,28},{14,30},{16,0},... | collective-permute-start | bytes 1105928 | tf_op jit(solution)/shard_map/ppermute | solution.py:1042
  205.7 36.2 %collective-permute-start.8 = (bf16[288,768]{1,0:T(8,128)(2,1)}, bf16[288,768]{1,0:T(8,128)(2,1)S(1)}, u32[]{:S(2)}, u32[]{:S(2)}) collective-permute-start(bf16[288,768]{1,0:T(8,128)(2,1)} %get-tuple-element.205), channel_id=1, source_target_pairs={{0,1},{1,0},{2,3},{3,2},{4,5},{5,4},{6,7},{7,6},{8,9},{9,8},{10,11... | collective-permute-start | bytes 1327112 | tf_op jit(solution)/shard_map/ppermute | solution.py:1046
  207.2 12.8 %collective-permute-start.14 = (bf16[2,96,768]{2,1,0:T(8,128)(2,1)S(1)}, bf16[2,96,768]{2,1,0:T(8,128)(2,1)S(1)}, u32[]{:S(2)}, u32[]{:S(2)}) collective-permute-start(bf16[2,96,768]{2,1,0:T(8,128)(2,1)S(1)} %fusion.24), channel_id=1, source_target_pairs={{0,8},{2,10},{4,12},{6,14},{8,0},{10,2},{12,4},{14,6},{16,24},{18,... | collective-permute-start | bytes 884744 | tf_op jit(solution)/shard_map/ppermute | solution.py:1042
  220.1 41.0 %collective-permute-start.18 = (bf16[8,96,768]{2,1,0:T(8,128)(2,1)S(1)}, bf16[8,96,768]{2,1,0:T(8,128)(2,1)S(1)}, u32[]{:S(2)}, u32[]{:S(2)}) collective-permute-start(bf16[8,96,768]{2,1,0:T(8,128)(2,1)S(1)} %fusion.3), channel_id=1, source_target_pairs={{0,1},{1,0},{2,3},{3,2},{4,5},{5,4},{6,7},{7,6},{8,9},{9,8},{10,11... | collective-permute-start | bytes 3538952 | tf_op jit(solution)/shard_map/ppermute | solution.py:1046
  222.7 32.4 %collective-permute-start.19 = (bf16[1,96,768]{2,1,0:T(8,128)(2,1)S(1)}, bf16[1,96,768]{2,1,0:T(8,128)(2,1)S(1)}, u32[]{:S(2)}, u32[]{:S(2)}) collective-permute-start(bf16[1,96,768]{2,1,0:T(8,128)(2,1)S(1)} %fusion.38), channel_id=1, source_target_pairs={{0,16},{2,18},{4,20},{6,22},{8,24},{10,26},{12,28},{14,30},{16,0},... | collective-permute-start | bytes 442376 | tf_op jit(solution)/shard_map/ppermute | solution.py:1042
  231.5 32.0 %collective-permute-start.17 = (bf16[4,192,768]{2,1,0:T(8,128)(2,1)S(1)}, bf16[4,192,768]{2,1,0:T(8,128)(2,1)S(1)}, u32[]{:S(2)}, u32[]{:S(2)}) collective-permute-start(bf16[4,192,768]{2,1,0:T(8,128)(2,1)S(1)} %fusion.4), channel_id=1, source_target_pairs={{0,4},{2,6},{4,0},{6,2},{8,12},{10,14},{12,8},{14,10},{16,20},{18,... | collective-permute-start | bytes 3538952 | tf_op jit(solution)/shard_map/ppermute | solution.py:1042
  269.0 14.2 %collective-permute-start.21 = (bf16[1,8,192,768]{3,2,1,0:T(8,128)(2,1)}, bf16[1,8,192,768]{3,2,1,0:T(8,128)(2,1)}, u32[]{:S(2)}, u32[]{:S(2)}) collective-permute-start(bf16[1,8,192,768]{3,2,1,0:T(8,128)(2,1)} %get-tuple-element.256), channel_id=1, source_target_pairs={{0,2},{2,0},{4,6},{6,4},{8,10},{10,8},{12,14},{14,12},{16,18},{18,... | collective-permute-start | bytes 7077896 | tf_op jit(solution)/shard_map/ppermute | solution.py:1042
  269.0 19.2 %collective-permute-start.20 = (bf16[2,8,144,384]{3,2,1,0:T(8,128)(2,1)}, bf16[2,8,144,384]{3,2,1,0:T(8,128)(2,1)}, u32[]{:S(2)}, u32[]{:S(2)}) collective-permute-start(bf16[2,8,144,384]{3,2,1,0:T(8,128)(2,1)} %get-tuple-element.260), channel_id=1, source_target_pairs={{0,2},{2,0},{4,6},{6,4},{8,10},{10,8},{12,14},{14,12},{16,18},{18,... | collective-permute-start | bytes 5308424 | tf_op jit(solution)/shard_map/ppermute | solution.py:1042
  269.5 11.8 %collective-permute-start.42 = (bf16[240,768]{1,0:T(8,128)(2,1)}, bf16[240,768]{1,0:T(8,128)(2,1)}, u32[]{:S(2)}, u32[]{:S(2)}) collective-permute-start(bf16[240,768]{1,0:T(8,128)(2,1)} %fusion.12), channel_id=1, source_target_pairs={{0,1},{1,0},{2,3},{3,2},{4,5},{5,4},{6,7},{7,6},{8,9},{9,8},{10,11... | collective-permute-start | bytes 1105928 | tf_op jit(solution)/shard_map/ppermute | solution.py:1046
  270.0 20.7 %collective-permute-start.16 = (bf16[288,768]{1,0:T(8,128)(2,1)S(1)}, bf16[288,768]{1,0:T(8,128)(2,1)S(1)}, u32[]{:S(2)}, u32[]{:S(2)}) collective-permute-start(bf16[288,768]{1,0:T(8,128)(2,1)S(1)} %copy-done.49), channel_id=1, source_target_pairs={{0,1},{1,0},{2,3},{3,2},{4,5},{5,4},{6,7},{7,6},{8,9},{9,8},{10,11... | collective-permute-start | bytes 1327112 | tf_op jit(solution)/shard_map/ppermute | solution.py:1046
  271.6 85.3 %collective-permute-start.43 = (bf16[96,768]{1,0:T(8,128)(2,1)}, bf16[96,768]{1,0:T(8,128)(2,1)}, u32[]{:S(2)}, u32[]{:S(2)}) collective-permute-start(bf16[96,768]{1,0:T(8,128)(2,1)} %fusion.32), channel_id=1, source_target_pairs={{0,1},{1,0},{2,3},{3,2},{4,5},{5,4},{6,7},{7,6},{8,9},{9,8},{10,11... | collective-permute-start | bytes 442376 | tf_op jit(solution)/shard_map/ppermute | solution.py:1046
  282.5 16.6 %collective-permute-start.24 = (bf16[4,96,768]{2,1,0:T(8,128)(2,1)}, bf16[4,96,768]{2,1,0:T(8,128)(2,1)}, u32[]{:S(2)}, u32[]{:S(2)}) collective-permute-start(bf16[4,96,768]{2,1,0:T(8,128)(2,1)} %fusion.7), channel_id=1, source_target_pairs={{0,4},{2,6},{4,0},{6,2},{8,12},{10,14},{12,8},{14,10},{16,20},{18,... | collective-permute-start | bytes 1769480 | tf_op jit(solution)/shard_map/ppermute | solution.py:1042
  285.9 35.6 %collective-permute-start.22 = (bf16[4,192,768]{2,1,0:T(8,128)(2,1)}, bf16[4,192,768]{2,1,0:T(8,128)(2,1)}, u32[]{:S(2)}, u32[]{:S(2)}) collective-permute-start(bf16[4,192,768]{2,1,0:T(8,128)(2,1)} %fusion.5), channel_id=1, source_target_pairs={{0,4},{2,6},{4,0},{6,2},{8,12},{10,14},{12,8},{14,10},{16,20},{18,... | collective-permute-start | bytes 3538952 | tf_op jit(solution)/shard_map/ppermute | solution.py:1042
  288.2 13.2 %collective-permute-start.23 = (bf16[2,192,768]{2,1,0:T(8,128)(2,1)}, bf16[2,192,768]{2,1,0:T(8,128)(2,1)}, u32[]{:S(2)}, u32[]{:S(2)}) collective-permute-start(bf16[2,192,768]{2,1,0:T(8,128)(2,1)} %fusion.8), channel_id=1, source_target_pairs={{0,8},{2,10},{4,12},{6,14},{8,0},{10,2},{12,4},{14,6},{16,24},{18,... | collective-permute-start | bytes 1769480 | tf_op jit(solution)/shard_map/ppermute | solution.py:1042
  290.8 35.4 %collective-permute-start.30 = (bf16[8,144,384]{2,1,0:T(8,128)(2,1)}, bf16[8,144,384]{2,1,0:T(8,128)(2,1)}, u32[]{:S(2)}, u32[]{:S(2)}) collective-permute-start(bf16[8,144,384]{2,1,0:T(8,128)(2,1)} %fusion.10), channel_id=1, source_target_pairs={{0,1},{1,0},{2,3},{3,2},{4,5},{5,4},{6,7},{7,6},{8,9},{9,8},{10,11... | collective-permute-start | bytes 2654216 | tf_op jit(solution)/shard_map/ppermute | solution.py:1046
  299.1 24.4 %collective-permute-start.26 = (f32[8,768]{1,0:T(8,128)S(1)}, f32[8,768]{1,0:T(8,128)S(1)}, u32[]{:S(2)}, u32[]{:S(2)}) collective-permute-start(f32[8,768]{1,0:T(8,128)S(1)} %concatenate.15), channel_id=1, source_target_pairs={{0,2},{2,0},{4,6},{6,4},{8,10},{10,8},{12,14},{14,12},{16,18},{18,... | collective-permute-start | bytes 73736 | tf_op jit(solution)/shard_map/ppermute | solution.py:1042
  301.4 26.9 %collective-permute-start.29 = (bf16[2,96,768]{2,1,0:T(8,128)(2,1)S(1)}, bf16[2,96,768]{2,1,0:T(8,128)(2,1)S(1)}, u32[]{:S(2)}, u32[]{:S(2)}) collective-permute-start(bf16[2,96,768]{2,1,0:T(8,128)(2,1)S(1)} %fusion.20), channel_id=1, source_target_pairs={{0,8},{2,10},{4,12},{6,14},{8,0},{10,2},{12,4},{14,6},{16,24},{18,... | collective-permute-start | bytes 884744 | tf_op jit(solution)/shard_map/ppermute | solution.py:1042
  321.6 13.3 %collective-permute-start.28 = (bf16[1,192,768]{2,1,0:T(8,128)(2,1)S(1)}, bf16[1,192,768]{2,1,0:T(8,128)(2,1)S(1)}, u32[]{:S(2)}, u32[]{:S(2)}) collective-permute-start(bf16[1,192,768]{2,1,0:T(8,128)(2,1)S(1)} %fusion.22), channel_id=1, source_target_pairs={{0,16},{2,18},{4,20},{6,22},{8,24},{10,26},{12,28},{14,30},{16,0},... | collective-permute-start | bytes 884744 | tf_op jit(solution)/shard_map/ppermute | solution.py:1042
  323.6 21.3 %collective-permute-start.25 = (bf16[2,192,768]{2,1,0:T(8,128)(2,1)S(1)}, bf16[2,192,768]{2,1,0:T(8,128)(2,1)S(1)}, u32[]{:S(2)}, u32[]{:S(2)}) collective-permute-start(bf16[2,192,768]{2,1,0:T(8,128)(2,1)S(1)} %fusion.6), channel_id=1, source_target_pairs={{0,8},{2,10},{4,12},{6,14},{8,0},{10,2},{12,4},{14,6},{16,24},{18,... | collective-permute-start | bytes 1769480 | tf_op jit(solution)/shard_map/ppermute | solution.py:1042
  326.1 12.2 %collective-permute-start.27 = (f32[8,768]{1,0:T(8,128)S(1)}, f32[8,768]{1,0:T(8,128)S(1)}, u32[]{:S(2)}, u32[]{:S(2)}) collective-permute-start(f32[8,768]{1,0:T(8,128)S(1)} %add.425), channel_id=1, source_target_pairs={{0,4},{2,6},{4,0},{6,2},{8,12},{10,14},{12,8},{14,10},{16,20},{18,... | collective-permute-start | bytes 73736 | tf_op jit(solution)/shard_map/ppermute | solution.py:1042
  338.3 11.7 %collective-permute-start.33 = (bf16[1,96,768]{2,1,0:T(8,128)(2,1)S(1)}, bf16[1,96,768]{2,1,0:T(8,128)(2,1)S(1)}, u32[]{:S(2)}, u32[]{:S(2)}) collective-permute-start(bf16[1,96,768]{2,1,0:T(8,128)(2,1)S(1)} %fusion.35), channel_id=1, source_target_pairs={{0,16},{2,18},{4,20},{6,22},{8,24},{10,26},{12,28},{14,30},{16,0},... | collective-permute-start | bytes 442376 | tf_op jit(solution)/shard_map/ppermute | solution.py:1042
  353.8 12.9 %collective-permute-start.31 = (bf16[1,192,768]{2,1,0:T(8,128)(2,1)S(1)}, bf16[1,192,768]{2,1,0:T(8,128)(2,1)S(1)}, u32[]{:S(2)}, u32[]{:S(2)}) collective-permute-start(bf16[1,192,768]{2,1,0:T(8,128)(2,1)S(1)} %fusion.18), channel_id=1, source_target_pairs={{0,16},{2,18},{4,20},{6,22},{8,24},{10,26},{12,28},{14,30},{16,0},... | collective-permute-start | bytes 884744 | tf_op jit(solution)/shard_map/ppermute | solution.py:1042
  353.8 14.1 %collective-permute-start.36 = (bf16[2,144,384]{2,1,0:T(8,128)(2,1)S(1)}, bf16[2,144,384]{2,1,0:T(8,128)(2,1)S(1)}, u32[]{:S(2)}, u32[]{:S(2)}) collective-permute-start(bf16[2,144,384]{2,1,0:T(8,128)(2,1)S(1)} %fusion.26), channel_id=1, source_target_pairs={{0,8},{2,10},{4,12},{6,14},{8,0},{10,2},{12,4},{14,6},{16,24},{18,... | collective-permute-start | bytes 663560 | tf_op jit(solution)/shard_map/ppermute | solution.py:1042
  355.5 13.5 %collective-permute-start.38 = (f32[8,768]{1,0:T(8,128)S(1)}, f32[8,768]{1,0:T(8,128)S(1)}, u32[]{:S(2)}, u32[]{:S(2)}) collective-permute-start(f32[8,768]{1,0:T(8,128)S(1)} %add.455), channel_id=1, source_target_pairs={{0,16},{2,18},{4,20},{6,22},{8,24},{10,26},{12,28},{14,30},{16,0},... | collective-permute-start | bytes 73736 | tf_op jit(solution)/shard_map/ppermute | solution.py:1042
  371.0 13.1 %collective-permute-start.35 = (bf16[192,768]{1,0:T(8,128)(2,1)S(1)}, bf16[192,768]{1,0:T(8,128)(2,1)S(1)}, u32[]{:S(2)}, u32[]{:S(2)}) collective-permute-start(bf16[192,768]{1,0:T(8,128)(2,1)S(1)} %fusion.15), channel_id=1, source_target_pairs={{0,1},{1,0},{2,3},{3,2},{4,5},{5,4},{6,7},{7,6},{8,9},{9,8},{10,11... | collective-permute-start | bytes 884744 | tf_op jit(solution)/shard_map/ppermute | solution.py:1046
  (115 other events, 1092.9 us)

commit v3 on v2

--- a/solution.py
+++ b/solution.py
@@ -125,10 +125,14 @@
         kernel,
         out_shape=out_shape,
         name=name,
-        cost_estimate=pl.CostEstimate(flops=int(flops), bytes_accessed=size, transcendentals=0),
+        cost_estimate=pl.CostEstimate(flops=1024, bytes_accessed=1024, transcendentals=0),
         compiler_params=pltpu.CompilerParams(vmem_limit_bytes=30 << 20),
         **options,
     )(*args)
+
+
+def hbm_of(dtype, *shape):
+    return pltpu.HBM(shape, dtype)
 
 
 def from_hbm(weights):
@@ -207,14 +211,14 @@
             whole(*query_proj.shape),
             whole(*keyval_proj.shape),
         ],
-        out_specs=[whole(rows, width), whole(own_count, width), whole(own_count, 2 * width)],
+        out_specs=[window(rows, width), window(own_count, width), whole(own_count, 2 * width)],
     )
     return call(
         kernel,
         "text_pre",
         (
-            shape_of(BF16, rows, width),
-            shape_of(BF16, own_count, width),
+            hbm_of(BF16, rows, width),
+            hbm_of(BF16, own_count, width),
             shape_of(BF16, own_count, 2 * width),
         ),
         (own_index, text, text, gain, query_proj, keyval_proj),
@@ -319,7 +323,7 @@
         grid=(steps,),
         in_specs=[whole(half, width), whole(half, width)]
         + [pl.BlockSpec((width, QUAD), lambda j, n=n: (0, n * steps + j)) for n in range(3)],
-        out_specs=[whole(rows, width)]
+        out_specs=[window(rows, width)]
         + [pl.BlockSpec((rows, QUAD), lambda j: (0, j))] * 3
         + [pl.BlockSpec((1, rows, PAIR), lambda j: (j, 0, 0))]
         + [pl.BlockSpec((half, QUAD), lambda j: (0, j))] * 2,
@@ -328,9 +332,8 @@
     return call(
         kernel,
         "window_forward",
-        (shape_of(BF16, rows, width),)
-        + (shape_of(BF16, rows, width),) * 3
-        + (shape_of(F32, steps, rows, PAIR),)
+        (hbm_of(BF16, rows, width),) * 4
+        + (hbm_of(F32, steps, rows, PAIR),)
         + (shape_of(BF16, half, width),) * 2,
         (normed, received, window_proj, window_proj, window_proj),
         2 * rows * width * (3 * width + 2 * size),
@@ -349,9 +352,16 @@
 
     def kernel(
         r_ref, t_ref, s_ref, wo_ref, g_ref, up_ref, down_ref, pg_ref, kv_ref, o_ref,
-        unshifted_ref, mid_ref, normed_ref, active_ref, slope_ref, final_ref, pages_ref, page_kv_ref, out_ref,
+        unshifted_hbm, mid_hbm, normed_hbm, active_ref, slope_ref, final_hbm, pages_hbm, page_kv_ref, out_ref,
+        unshifted_ref, mid_ref, normed_ref, final_ref, pages_ref, sems,
     ):
         step = pl.program_id(0)
+        early = [
+            pltpu.make_async_copy(source, target, sems.at[n])
+            for n, (source, target) in enumerate(
+                ((unshifted_ref, unshifted_hbm), (mid_ref, mid_hbm), (normed_ref, normed_hbm))
+            )
+        ]
 
         @pl.when(step == 0)
         def _():
@@ -362,25 +372,32 @@
             final_ref[...] = mid
             hat, _ = norm_parts(mid)
             normed_ref[...] = (hat * g_ref[...]).astype(BF16)
-
-        cols = pl.ds(pl.multiple_of(step * FF_CHUNK, FF_CHUNK), FF_CHUNK)
+            for copy in early:
+                copy.start()
+
         for block in range(rows // ROW_BLOCK):
             at = slice(block * ROW_BLOCK, (block + 1) * ROW_BLOCK)
             hidden = dot(normed_ref[at, :], up_ref[...])
             active, slope = gelu_parts(hidden)
             active = active.astype(BF16)
-            active_ref[at, cols] = active
-            slope_ref[at, cols] = slope.astype(BF16)
+            active_ref[at, :] = active
+            slope_ref[at, :] = slope.astype(BF16)
             final_ref[at, :] += dot(active, down_ref[...])
 
         @pl.when(step == steps - 1)
         def _():
             final = final_ref[...]
+            final_copy = pltpu.make_async_copy(final_ref, final_hbm, sems.at[3])
+            final_copy.start()
             hat, _ = norm_parts(final)
             pages = (hat * pg_ref[...]).astype(BF16)
             pages_ref[...] = pages
+            pages_copy = pltpu.make_async_copy(pages_ref, pages_hbm, sems.at[4])
+            pages_copy.start()
             page_kv_ref[...] = dot(pages, kv_ref[...]).astype(BF16)
             out_ref[...] = dot(one_hot(o_ref[:, 3:4], rows), final.astype(BF16)).astype(BF16)
+            for copy in early + [final_copy, pages_copy]:
+                copy.wait()
 
     grid_spec = pltpu.PrefetchScalarGridSpec(
         num_scalar_prefetch=0,
@@ -390,19 +407,22 @@
             pl.BlockSpec((width, FF_CHUNK), lambda j: (0, j)), pl.BlockSpec((FF_CHUNK, width), lambda j: (j, 0)),
             whole(1, width), whole(*keyval_proj.shape), whole(*orders.shape),
         ],
-        out_specs=[
-            whole(rows, width), whole(rows, width), whole(rows, width),
-            whole(rows, up.shape[1]), whole(rows, up.shape[1]),
-            whole(rows, width), whole(rows, width), whole(rows, 2 * width), window(rows, width),
+        out_specs=[pl.BlockSpec(memory_space=pl.ANY)] * 3
+        + [pl.BlockSpec((rows, FF_CHUNK), lambda j: (0, j))] * 2
+        + [pl.BlockSpec(memory_space=pl.ANY)] * 2
+        + [whole(rows, 2 * width), window(rows, width)],
+        scratch_shapes=[
+            pltpu.VMEM((rows, width), BF16), pltpu.VMEM((rows, width), F32), pltpu.VMEM((rows, width), BF16),
+            pltpu.VMEM((rows, width), F32), pltpu.VMEM((rows, width), BF16), pltpu.SemaphoreType.DMA((5,)),
         ],
     )
     return call(
         kernel,
         "visual_forward",
         (
-            shape_of(BF16, rows, width), shape_of(F32, rows, width), shape_of(BF16, rows, width),
-            shape_of(BF16, rows, up.shape[1]), shape_of(BF16, rows, up.shape[1]),
-            shape_of(F32, rows, width), shape_of(BF16, rows, width), shape_of(BF16, rows, 2 * width), shape_of(BF16, rows, width),
+            hbm_of(BF16, rows, width), hbm_of(F32, rows, width), hbm_of(BF16, rows, width),
+            hbm_of(BF16, rows, up.shape[1]), hbm_of(BF16, rows, up.shape[1]),
+            hbm_of(F32, rows, width), hbm_of(BF16, rows, width), shape_of(BF16, rows, 2 * width), shape_of(BF16, rows, width),
         ),
         (received, top, stream, window_out, gain, up, down, pages_gain, keyval_proj, orders),
         2 * rows * width * (width + 2 * up.shape[1] + 2 * width + rows),
@@ -953,7 +973,7 @@
             out_specs=[out_block, out_block],
             scratch_shapes=scratch,
         ),
-        cost_estimate=pl.CostEstimate(flops=flops, bytes_accessed=size, transcendentals=0),
+        cost_estimate=pl.CostEstimate(flops=1024, bytes_accessed=1024, transcendentals=0),
         compiler_params=pltpu.CompilerParams(vmem_limit_bytes=30 << 20),
         **extra,
     )(*args)
@@ -1126,6 +1146,10 @@
 
     def after(self, value):
         self.token = value
+
+    def hold(self, *sums):
+        for one in sums:
+            one.other = self.before(one.other)
 
     def step(self, *sums):
         for one in sums:
@@ -1184,9 +1208,7 @@
     )
     pack_other = swap_win(pack)
     order = Order(pack)
-    at = (1, count, tall + block, D)
-    grads = narrow_grad(where, [(reply_normed, text_hidden_grad)], at, 0, None, "text_up_grad")
-    grads = narrow_grad(where, [(context, branch)], at, tall, grads, "cross_out_grad")
+    grads = narrow_grad(where, [(reply_normed, text_hidden_grad)], (1, count, tall, D), 0, None, "text_up_grad")
     reply_a = Reduction(*grads, False)
     order.step(reply_a)
     grads = wide_grad(
@@ -1194,10 +1216,9 @@
     )
     reply_b = Reduction(*grads, True)
     order.after(grads[0])
-    order.step(reply_a, reply_b)
     pack_other = order.before(pack_other)
     order.after(pack_other)
-    order.step(reply_b)
+    order.step(reply_a, reply_b, reply_b)
     page_kv_grad, text_kv_grad, query_mine, query_away = cross_backward(
         other_index, queries, page_kv, text_kv, text_mask, pack, order.before(pack_other)
     )
@@ -1206,57 +1227,67 @@
     query_theirs = swap_win(query_away)
     (out_grad, hidden_grad, mid_grad, window_branch, context_first, context_second, pages_gain, visual_gain) = visual_backward(
         order.before(page_kv_grad), keyval_proj, final, visual_upstream.reshape(rows, D), orders, g_pages, mid, g_visual,
-        window_out, visual_up_hbm, visual_down_hbm, slope,
+        window_out, visual_up_hbm, visual_down_hbm, from_hbm(slope),
     )
     later = swap_win(context_first)
     order.after(out_grad)
     order.step(reply_a, reply_b)
-    grads = wide_grad(where, order.before(active), out_grad, (2, count, tall // 2, D), 0, None, "visual_down_grad")
+    grads = wide_grad(
+        where, from_hbm(order.before(active)), out_grad, (2, count, tall // 2, D), 0, None, "visual_down_grad"
+    )
     visual_b = Reduction(*grads, True)
     order.after(grads[0])
     order.step(visual_b)
-    grads = narrow_grad(
-        where, [(order.before(ff_normed), hidden_grad)], (1, count, tall, D), 0, None, "visual_up_grad"
-    )
-    visual_a = Reduction(*grads, False)
-    order.after(grads[0])
-    order.step(visual_a, visual_b, reply_b)
+    at = (1, count, tall + 2 * block, D)
+    grads_a = narrow_grad(where, [(order.before(ff_normed), hidden_grad)], at, 0, None, "visual_up_grad")
+    order.after(grads_a[0])
+    later = order.before(later)
+    order.after(later)
+    order.step(visual_b, reply_b, reply_a)
     text_grad, query_grad, text_gain = text_tail(
         own_index, query_mine, order.before(query_theirs), text_kv_grad, text, text_mid_grad, g_text, text_query, keyval_proj
     )
-    at = (1, count, 4 * block, D)
-    at_b = (2, count, 3 * block, D // 2)
-    grads_a = narrow_grad(where, [(text_normed, query_grad)], at, 2 * block, None, "text_query_grad")
-    grads_a = narrow_grad(where, [(unshifted, window_branch)], at, 3 * block, grads_a, "window_out_grad")
+    grads_a = narrow_grad(where, [(text_normed, query_grad)], at, tall, grads_a, "text_query_grad")
+    grads_a = narrow_grad(where, [(unshifted, window_branch)], at, tall + block, grads_a, "window_out_grad")
+    visual_a = Reduction(*grads_a, False)
     order.after(grads_a[0])
     order.step(visual_a)
+    at_b = (2, count, 3 * block, D // 2)
     pairs = [(order.before(text_normed), text_kv_grad), (pages_normed, page_kv_grad)]
     grads_b = narrow_grad(where, pairs, at_b, 0, None, "keyval_grad", D // 2, split=True)
     order.after(grads_b[0])
-    order.step(reply_a)
+    order.step(visual_a)
+    grads_a = narrow_grad(
+        where, [(context, order.before(branch))], (1, count, 3 * block, D), 2 * block, None, "cross_out_grad"
+    )
+    order.after(grads_a[0])
+    order.hold(reply_a)
+    order.step(reply_b)
     packed_grad, top_grad, low_grad = window_backward(
         win_q, win_k, win_v, win_log, top, low, context_second, order.before(later), window_proj_hbm
     )
     earlier = swap_win(low_grad)
     order.after(packed_grad)
-    order.step(reply_b)
-    grads_a = narrow_grad(where, [(shifted, order.before(packed_grad))], at, 0, grads_a, "window_proj_grad", steps=2)
+    order.hold(reply_b)
+    grads_a = narrow_grad(
+        where, [(shifted, order.before(packed_grad))], (1, count, 3 * block, D), 0, grads_a, "window_proj_grad", steps=2
+    )
     window_a = Reduction(*grads_a, False)
     order.after(grads_a[0])
-    order.step(visual_b, visual_a)
+    order.step(visual_b)
     grads_b = narrow_grad(
         where, [(shifted, order.before(packed_grad))], at_b, 2 * block, grads_b, "window_value_grad", D // 2, 4, 2, True
     )
     window_b = Reduction(*grads_b, True)
     order.after(grads_b[0])
-    order.step(window_a, window_b, window_a, window_b)
+    order.step(window_a, window_b, visual_a, window_b, window_a)
     visual_grad, window_gain, embed_grad = visual_tail(
         order.before(earlier), top_grad, stream, mid_grad, mark, g_window, orders
     )
     sums = SmallSum([window_gain, visual_gain, text_gain, pages_gain, reply_gain, embed_grad])
     order.after(window_gain)
-    order.step(sums, visual_b, visual_a, window_a, sums, window_b, visual_b, visual_a, sums, window_a, window_b)
-    order.step(visual_b, sums, window_a, window_b, sums, window_b)
+    order.step(sums, visual_b, window_b, sums, visual_a, window_a, visual_b, window_b, sums, visual_a, window_a)
+    order.step(visual_b, window_b, sums, window_a, sums, window_b)
     left = [one for one in (reply_a, reply_b, visual_a, visual_b, window_a, window_b, sums) if one.todo]
     assert not left
     reply_a, reply_b, visual_a, visual_b, window_a, window_b, sums = (
@@ -1268,12 +1299,12 @@
         visual_grad.reshape(visual_in.shape),
         text_grad[None],
         jnp.concatenate([untile(window_a, 0, 2, block), window_b[0, 2 * block :], window_b[1, 2 * block :]], 1),
-        window_a[3 * block :],
+        visual_a[tall + block :],
         untile(visual_a, 0, FF // D, block),
         visual_b.reshape(tall, D),
-        window_a[2 * block : 3 * block],
+        visual_a[tall : tall + block],
         jnp.concatenate([window_b[h, n * block : (n + 1) * block] for h in range(2) for n in range(2)], 1),
-        reply_a[tall:],
+        window_a[2 * block :],
         untile(reply_a, 0, FF // D, block),
         reply_b.reshape(tall, D),
         *sums,

time: 390 us -> 357 us (0.915)
  waiting for transfers between devices: 104 us -> 71.5 us
  local copies, waits for them, and re-layouts: 38.7 us -> 29.6 us
  starting transfers between devices: 42.9 us -> 49.6 us
    ppermute x28, waiting for transfers between devices: 59.3 us -> 35.7 us  [swap_page(): lax.ppermute(x, 'page', [(i, i ^ 1 << bit) for i in range(lax.axis_size('...]
    unnamed x205 -> x155, local copies, waits for them, and re-layouts: 35 us -> 22.6 us
    ppermute x17, waiting for transfers between devices: 44.5 us -> 35.8 us  [swap_win(): return lax.ppermute(x, 'win', [(0, 1), (1, 0)])]
    ppermute x28, starting transfers between devices: 23.3 us -> 28.9 us  [swap_page(): lax.ppermute(x, 'page', [(i, i ^ 1 << bit) for i in range(lax.axis_size('...]
  transfers between devices with their start and end apart: 45 -> 45, of which waited for: 18 -> 22; matrix products, arithmetic and copies ran while one was open for 11% -> 13% of each run, Pallas kernels for 23% -> 24%
where the time goes in v3:
time: 357 us; the launch traced here: 353 us
  Pallas kernels  155 us (43%)
  waiting for transfers between devices  71.5 us (20%)
  starting transfers between devices  49.6 us (14%)
  other arithmetic  45.1 us (13%)
  local copies, waits for them, and re-layouts  29.6 us (8%)
    pallas_call x12, Pallas kernels, call(): pl.pallas_call(kernel, out_shape=out_shape, name=name, cost_estimate=pl.C...  119 us
    convert_element_type x27, other arithmetic, total(): return result.astype(BF16)  38.6 us
    pallas_call x10, Pallas kernels, grad_call(): pl.pallas_call(kernel, out_shape=(shape_of(BF16, *at),) * 2, name=name, g...  36.1 us
    ppermute x17, waiting for transfers between devices, swap_win(): return lax.ppermute(x, 'win', [(0, 1), (1, 0)])  35.8 us
    ppermute x28, waiting for transfers between devices, swap_page(): lax.ppermute(x, 'page', [(i, i ^ 1 << bit) for i in range(lax.axis_size('...  35.7 us
    ppermute x28, starting transfers between devices, swap_page(): lax.ppermute(x, 'page', [(i, i ^ 1 << bit) for i in range(lax.axis_size('...  28.9 us
    unnamed x155, local copies, waits for them, and re-layouts  22.6 us
    ppermute x17, starting transfers between devices, swap_win(): return lax.ppermute(x, 'win', [(0, 1), (1, 0)])  20.8 us
  transfers between devices with their start and end apart: 45, of which 22 were waited for; matrix products, arithmetic and copies ran while one was open for 13% of the time, Pallas kernels for 24%

profile of v3, /device:TPU:0, one launch (start us, length us, event | category | flops | bytes accessed | tf_op | source)
XLA Modules:
  0.0 352.8 jit_solution(8422085393040813872)
XLA Ops:
  8.3 2.9 collective-permute-start
  16.8 4.6 %collective-permute-done.r_ref = bf16[288,768]{1,0:T(8,128)(2,1)S(1)} collective-permute-done((bf16[288,768]{1,0:T(8,128)(2,1)S(1)}, bf16[288,768]{1,0:T(8,128)(2,1)S(1)}, u32[]{:S(2)}, u32[]{:S(2)}) %collective-permute-start) | collective-permute-done | bytes 442400 | tf_op jit(solution)/shard_map/ppermute | solution.py:1066
  21.4 11.2 %window_forward.1 = (bf16[576,768]{1,0:T(8,128)(2,1)}, bf16[576,768]{1,0:T(8,128)(2,1)}, bf16[576,768]{1,0:T(8,128)(2,1)}, bf16[576,768]{1,0:T(8,128)(2,1)}, f32...) custom-call(bf16[288,768]{1,0:T(8,128)(2,1)S(1)} %get-tuple-element.158.n_ref, ...), custom_call_target="tpu_custom_call" | custom-call | flops 1024 | bytes 1024 | tf_op jit(solution)/shard_map/window_forward/pallas_call | solution.py:124
  35.9 8.7 %collective-permute-done.1.r_ref = bf16[288,768]{1,0:T(8,128)(2,1)S(1)} collective-permute-done((bf16[288,768]{1,0:T(8,128)(2,1)S(1)}, bf16[288,768]{1,0:T(8,128)(2,1)S(1)}, u32[]{:S(2)}, u32[]{:S(2)}) %collective-permute-start.1) | collective-permute-done | bytes 442400 | tf_op jit(solution)/shard_map/ppermute | solution.py:1066
  51.9 18.8 %visual_forward.1 = (bf16[576,768]{1,0:T(8,128)(2,1)}, f32[576,768]{1,0:T(8,128)}, bf16[576,768]{1,0:T(8,128)(2,1)}, bf16[576,3072]{1,0:T(8,128)(2,1)}, bf16[576...) custom-call(bf16[288,768]{1,0:T(8,128)(2,1)S(1)} %copy-done.43, ...), custom_call_target="tpu_custom_call" | custom-call | flops 1024 | bytes 1024 | tf_op jit(solution)/shard_map/visual_forward/pallas_call | solution.py:124
  70.8 7.8 %cross_forward.2 = bf16[200,896]{1,0:T(8,128)(2,1)} custom-call(s32[2]{0:T(128)S(1)} %pad_add_fusion.i_ref, bf16[400,768]{1,0:T(8,128)(2,1)S(1)} %copy-done.5, bf16[576,1536]{1,0:T(8,128)(2,1)S(1)} %get-tuple-element.167.pk_ref.pv_ref, bf16[576,1536]{1,0:T(8,128)(2,1)S(1)} %get-tuple-element.167.pk_ref.pv_ref, ...), custom_call_target="tpu_custom_call" | custom-call | flops 1024 | bytes 1024 | tf_op jit(solution)/shard_map/cross_forward/pallas_call | solution.py:124
  80.0 7.2 %cross_forward.3.a_ref = bf16[200,896]{1,0:T(8,128)(2,1)S(1)} custom-call(s32[2]{0:T(128)S(1)} %pad_add_fusion.1.i_ref, bf16[400,768]{1,0:T(8,128)(2,1)S(1)} %copy-done.5, bf16[576,1536]{1,0:T(8,128)(2,1)S(1)} %get-tuple-element.167.pk_ref.pv_ref, bf16[576,1536]{1,0:T(8,128)(2,1)S(1)} %get-tuple-element.167.pk_ref.pv_ref, ...), custom_call_target="tpu_custom_call" | custom-call | flops 1024 | bytes 1024 | tf_op jit(solution)/shard_map/cross_forward/pallas_call | solution.py:124
  87.5 13.8 %text_block.1 = (bf16[200,768]{1,0:T(8,128)(2,1)}, bf16[200,768]{1,0:T(8,128)(2,1)S(1)}, bf16[200,768]{1,0:T(8,128)(2,1)S(1)}, bf16[200,3072]{1,0:T(8,128)(2,1)S...) custom-call(s32[1]{0:T(128)} %bitcast.1.w_ref, ...), custom_call_target="tpu_custom_call" | custom-call | flops 1024 | bytes 1024 | tf_op jit(solution)/shard_map/text_block/pallas_call | solution.py:124
  105.0 3.8 %text_down_grad.1 = (bf16[2,8,96,768]{3,2,1,0:T(8,128)(2,1)S(1)}, bf16[2,8,96,768]{3,2,1,0:T(8,128)(2,1)S(1)}) custom-call(s32[1]{0:T(128)} %bitcast.7.p_ref, s32[1]{0:T(128)} %bitcast.1.w_ref, bf16[200,3072]{1,0:T(8,128)(2,1)S(1)} %get-tuple-element.184.l_ref, bf16[200,768]{1,0:T(8,128)(2,1)S(1)} %bitcast.228), custom_call_target="tpu_custom_call" | custom-call | flops 1024 | bytes 1024 | tf_op jit(solution)/shard_map/text_down_grad/pallas_call | solution.py:965
  108.8 5.9 %collective-permute-done.3.b_ref = bf16[200,896]{1,0:T(8,128)(2,1)S(1)} collective-permute-done((bf16[200,896]{1,0:T(8,128)(2,1)S(1)}, bf16[200,896]{1,0:T(8,128)(2,1)S(1)}, u32[]{:S(2)}, u32[]{:S(2)}) %collective-permute-start.3) | collective-permute-done | bytes 358432 | tf_op jit(solution)/shard_map/ppermute | solution.py:1066
  116.5 3.1 collective-permute-done.5
  121.0 19.1 %cross_backward.1 = (bf16[576,1536]{1,0:T(8,128)(2,1)S(1)}, bf16[200,1536]{1,0:T(8,128)(2,1)S(1)}, f32[200,768]{1,0:T(8,128)S(1)}, bf16[200,768]{1,0:T(8,128)(2,1)S(1)}) custom-call(s32[2]{0:T(128)S(1)} %pad_add_fusion.i_ref, bf16[400,768]{1,0:T(8,128)(2,1)S(1)} %copy-done.5, bf16[400,768]{1,0:T(8,128)(2,1)S(1)} %copy-done.5, ...), custom_call_target="tpu_custom_call" | custom-call | flops 1024 | bytes 1024 | tf_op jit(solution)/shard_map/cross_backward/pallas_call | solution.py:124
  140.2 3.2 collective-permute-done.7
  150.6 17.3 %visual_backward.1 = (bf16[576,768]{1,0:T(8,128)(2,1)S(1)}, bf16[576,3072]{1,0:T(8,128)(2,1)S(1)}, f32[576,768]{1,0:T(8,128)S(1)}, bf16[576,768]{1,0:T(8,128)(2,...) custom-call(bf16[576,1536]{1,0:T(8,128)(2,1)S(1)} %get-tuple-element, ...), custom_call_target="tpu_custom_call" | custom-call | flops 1024 | bytes 1024 | tf_op jit(solution)/shard_map/visual_backward/pallas_call | solution.py:124
  171.0 9.2 %visual_down_grad.1 = (bf16[2,8,96,768]{3,2,1,0:T(8,128)(2,1)S(1)}, bf16[2,8,96,768]{3,2,1,0:T(8,128)(2,1)S(1)}) custom-call(s32[1]{0:T(128)} %bitcast.7.p_ref, s32[1]{0:T(128)} %bitcast.1.w_ref, bf16[576,3072]{1,0:T(8,128)(2,1)} %get-tuple-element.209.l_ref, bf16[576,768]{1,0:T(8,128)(2,1)S(1)} %get-tuple-element.206.r_ref), custom_call_target="tpu_custom_call" | custom-call | flops 1024 | bytes 1024 | tf_op jit(solution)/shard_map/visual_down_grad/pallas_call | solution.py:965
  182.4 2.6 collective-permute-start.16
  186.6 5.3 %visual_up_grad.1 = (bf16[1,8,288,768]{3,2,1,0:T(8,128)(2,1)S(1)}, bf16[1,8,288,768]{3,2,1,0:T(8,128)(2,1)S(1)}) custom-call(s32[1]{0:T(128)} %bitcast.7.p_ref, s32[1]{0:T(128)} %bitcast.1.w_ref, bf16[576,768]{1,0:T(8,128)(2,1)S(1)} %copy-done.35, bf16[576,3072]{1,0:T(8,128)(2,1)S(1)} %get-tuple-element.214.refs_1_), custom_call_target="tpu_custom_call" | custom-call | flops 1024 | bytes 1024 | tf_op jit(solution)/shard_map/visual_up_grad/pallas_call | solution.py:965
  195.0 4.0 %collective-permute-done.11 = bf16[2,96,768]{2,1,0:T(8,128)(2,1)} collective-permute-done((bf16[2,96,768]{2,1,0:T(8,128)(2,1)}, bf16[2,96,768]{2,1,0:T(8,128)(2,1)}, u32[]{:S(2)}, u32[]{:S(2)}) %collective-permute-start.11) | collective-permute-done | bytes 294944 | tf_op jit(solution)/shard_map/ppermute | solution.py:1062
  210.3 5.6 %keyval_grad.1 = (bf16[2,8,144,384]{3,2,1,0:T(8,128)(2,1)S(1)}, bf16[2,8,144,384]{3,2,1,0:T(8,128)(2,1)}) custom-call(s32[1]{0:T(128)} %bitcast.7.p_ref, s32[1]{0:T(128)} %bitcast.1.w_ref, bf16[200,768]{1,0:T(8,128)(2,1)S(1)} %copy-done.30, bf16[576,768]{1,0:T(8,128)(2,1)S(1)} %copy-done.34, bf16[200,1536]{1,0:T(8,128)(2,1)S(1)} %get-tuple-element.233.kv_ref.refs_2_, ...), custom_call_target="tpu_custom_call" | custom-call | flops 1024 | bytes 1024 | tf_op jit(solution)/shard_map/keyval_grad/pallas_call | solution.py:965
  223.3 13.4 %window_backward.1 = (bf16[576,2304]{1,0:T(8,128)(2,1)S(1)}, bf16[288,768]{1,0:T(8,128)(2,1)S(1)}, bf16[288,768]{1,0:T(8,128)(2,1)S(1)}) custom-call(bf16[576,768]{1,0:T(8,128)(2,1)S(1)} %copy-done.38, bf16[576,768]{1,0:T(8,128)(2,1)S(1)} %copy-done.39, bf16[576,768]{1,0:T(8,128)(2,1)S(1)} %copy-done.40, f32[3,576,128]{2,1,0:T(8,128)S(1)} %copy-done.41, ...), custom_call_target="tpu_custom_call" | custom-call | flops 1024 | bytes 1024 | tf_op jit(solution)/shard_map/window_backward/pallas_call | solution.py:124
  238.9 2.7 collective-permute-done.42
  241.6 3.6 %window_proj_grad.1 = (bf16[1,8,144,768]{3,2,1,0:T(8,128)(2,1)S(1)}, bf16[1,8,144,768]{3,2,1,0:T(8,128)(2,1)}) custom-call(s32[1]{0:T(128)} %bitcast.7.p_ref, s32[1]{0:T(128)} %bitcast.1.w_ref, bf16[576,768]{1,0:T(8,128)(2,1)S(1)} %copy-done.21, bf16[576,2304]{1,0:T(8,128)(2,1)S(1)} %get-tuple-element.252.refs_1_, ...), custom_call_target="tpu_custom_call", output_to_operand_aliasing={{0}: (4, {}), {1}: (5, {})} | custom-call | flops 1024 | bytes 1024 | tf_op jit(solution)/shard_map/window_proj_grad/pallas_call | solution.py:965
  247.8 2.8 window_value_grad.1
  254.4 5.0 %collective-permute-done.43 = bf16[96,768]{1,0:T(8,128)(2,1)} collective-permute-done((bf16[96,768]{1,0:T(8,128)(2,1)}, bf16[96,768]{1,0:T(8,128)(2,1)}, u32[]{:S(2)}, u32[]{:S(2)}) %collective-permute-start.43) | collective-permute-done | bytes 147488 | tf_op jit(solution)/shard_map/ppermute | solution.py:1066
  261.6 2.7 fusion.1
  264.3 2.6 fusion.8
  268.0 2.8 fusion.9
  272.8 4.7 %visual_tail.1 = (f32[576,768]{1,0:T(8,128)}, f32[1,768]{1,0:T(1,128)S(1)}, f32[1,768]{1,0:T(1,128)S(1)}) custom-call(bf16[288,768]{1,0:T(8,128)(2,1)S(1)} %collective-permute-done.14.r_ref, bf16[288,768]{1,0:T(8,128)(2,1)S(1)} %copy-done.45, f32[576,768]{1,0:T(8,128)S(1)} %copy-done.8, f32[576,768]{1,0:T(8,128)S(1)} %copy-done.29, ...), custom_call_target="tpu_custom_call" | custom-call | flops 1024 | bytes 1024 | tf_op jit(solution)/shard_map/visual_tail/pallas_call | solution.py:124
  283.3 3.6 %collective-permute-done.25 = bf16[8,144,384]{2,1,0:T(8,128)(2,1)} collective-permute-done((bf16[8,144,384]{2,1,0:T(8,128)(2,1)}, bf16[8,144,384]{2,1,0:T(8,128)(2,1)}, u32[]{:S(2)}, u32[]{:S(2)}) %collective-permute-start.25) | collective-permute-done | bytes 884768 | tf_op jit(solution)/shard_map/ppermute | solution.py:1066
  303.6 11.1 %collective-permute-done.28 = bf16[1,288,768]{2,1,0:T(8,128)(2,1)S(1)} collective-permute-done((bf16[1,288,768]{2,1,0:T(8,128)(2,1)S(1)}, bf16[1,288,768]{2,1,0:T(8,128)(2,1)S(1)}, u32[]{:S(2)}, u32[]{:S(2)}) %collective-permute-start.28) | collective-permute-done | bytes 442400 | tf_op jit(solution)/shard_map/ppermute | solution.py:1062
  329.4 2.9 collective-permute-start.38
  340.5 3.6 %collective-permute-done.37 = bf16[1,144,384]{2,1,0:T(8,128)(2,1)S(1)} collective-permute-done((bf16[1,144,384]{2,1,0:T(8,128)(2,1)S(1)}, bf16[1,144,384]{2,1,0:T(8,128)(2,1)S(1)}, u32[]{:S(2)}, u32[]{:S(2)}) %collective-permute-start.37) | collective-permute-done | bytes 110624 | tf_op jit(solution)/shard_map/ppermute | solution.py:1062
  (293 shorter events, 135.4 us)
Async XLA Ops:
  8.3 13.1 %collective-permute-start = (bf16[288,768]{1,0:T(8,128)(2,1)S(1)}, bf16[288,768]{1,0:T(8,128)(2,1)S(1)}, u32[]{:S(2)}, u32[]{:S(2)}) collective-permute-start(bf16[288,768]{1,0:T(8,128)(2,1)S(1)} %get-tuple-element.159), channel_id=1, source_target_pairs={{0,1},{1,0},{2,3},{3,2},{4,5},{5,4},{6,7},{7,6},{8,9},{9,8},{10,11... | collective-permute-start | bytes 1327112 | tf_op jit(solution)/shard_map/ppermute | solution.py:1066
  33.3 11.4 %collective-permute-start.1 = (bf16[288,768]{1,0:T(8,128)(2,1)S(1)}, bf16[288,768]{1,0:T(8,128)(2,1)S(1)}, u32[]{:S(2)}, u32[]{:S(2)}) collective-permute-start(bf16[288,768]{1,0:T(8,128)(2,1)S(1)} %get-tuple-element.162.lc_ref), channel_id=1, source_target_pairs={{0,1},{1,0},{2,3},{3,2},{4,5},{5,4},{6,7},{7,6},{8,9},{9,8},{10,11... | collective-permute-start | bytes 1327112 | tf_op jit(solution)/shard_map/ppermute | solution.py:1066
  103.8 10.9 %collective-permute-start.4 = (bf16[1,8,192,768]{3,2,1,0:T(8,128)(2,1)S(1)}, bf16[1,8,192,768]{3,2,1,0:T(8,128)(2,1)S(1)}, u32[]{:S(2)}, u32[]{:S(2)}) collective-permute-start(bf16[1,8,192,768]{3,2,1,0:T(8,128)(2,1)S(1)} %get-tuple-element.183), channel_id=1, source_target_pairs={{0,2},{2,0},{4,6},{6,4},{8,10},{10,8},{12,14},{14,12},{16,18},{18,... | collective-permute-start | bytes 7077896 | tf_op jit(solution)/shard_map/ppermute | solution.py:1062
  103.9 10.8 %collective-permute-start.3 = (bf16[200,896]{1,0:T(8,128)(2,1)S(1)}, bf16[200,896]{1,0:T(8,128)(2,1)S(1)}, u32[]{:S(2)}, u32[]{:S(2)}) collective-permute-start(bf16[200,896]{1,0:T(8,128)(2,1)S(1)} %get-tuple-element.176.a_ref), channel_id=1, source_target_pairs={{0,1},{1,0},{2,3},{3,2},{4,5},{5,4},{6,7},{7,6},{8,9},{9,8},{10,11... | collective-permute-start | bytes 1075208 | tf_op jit(solution)/shard_map/ppermute | solution.py:1066
  115.0 28.4 %collective-permute-start.7 = (bf16[4,192,768]{2,1,0:T(8,128)(2,1)S(1)}, bf16[4,192,768]{2,1,0:T(8,128)(2,1)S(1)}, u32[]{:S(2)}, u32[]{:S(2)}) collective-permute-start(bf16[4,192,768]{2,1,0:T(8,128)(2,1)S(1)} %fusion.2), channel_id=1, source_target_pairs={{0,4},{2,6},{4,0},{6,2},{8,12},{10,14},{12,8},{14,10},{16,20},{18,... | collective-permute-start | bytes 3538952 | tf_op jit(solution)/shard_map/ppermute | solution.py:1062
  119.9 28.1 %collective-permute-start.6 = (bf16[8,96,768]{2,1,0:T(8,128)(2,1)S(1)}, bf16[8,96,768]{2,1,0:T(8,128)(2,1)S(1)}, u32[]{:S(2)}, u32[]{:S(2)}) collective-permute-start(bf16[8,96,768]{2,1,0:T(8,128)(2,1)S(1)} %fusion.3), channel_id=1, source_target_pairs={{0,1},{1,0},{2,3},{3,2},{4,5},{5,4},{6,7},{7,6},{8,9},{9,8},{10,11... | collective-permute-start | bytes 3538952 | tf_op jit(solution)/shard_map/ppermute | solution.py:1066
  144.7 23.2 %collective-permute-start.10 = (bf16[2,192,768]{2,1,0:T(8,128)(2,1)S(1)}, bf16[2,192,768]{2,1,0:T(8,128)(2,1)S(1)}, u32[]{:S(2)}, u32[]{:S(2)}) collective-permute-start(bf16[2,192,768]{2,1,0:T(8,128)(2,1)S(1)} %fusion.6), channel_id=1, source_target_pairs={{0,8},{2,10},{4,12},{6,14},{8,0},{10,2},{12,4},{14,6},{16,24},{18,... | collective-permute-start | bytes 1769480 | tf_op jit(solution)/shard_map/ppermute | solution.py:1062
  149.2 19.8 %collective-permute-start.9 = (bf16[4,96,768]{2,1,0:T(8,128)(2,1)}, bf16[4,96,768]{2,1,0:T(8,128)(2,1)S(1)}, u32[]{:S(2)}, u32[]{:S(2)}) collective-permute-start(bf16[4,96,768]{2,1,0:T(8,128)(2,1)} %fusion.7), channel_id=1, source_target_pairs={{0,4},{2,6},{4,0},{6,2},{8,12},{10,14},{12,8},{14,10},{16,20},{18,... | collective-permute-start | bytes 1769480 | tf_op jit(solution)/shard_map/ppermute | solution.py:1062
  180.2 13.1 %collective-permute-start.12 = (bf16[2,8,96,768]{3,2,1,0:T(8,128)(2,1)S(1)}, bf16[2,8,96,768]{3,2,1,0:T(8,128)(2,1)}, u32[]{:S(2)}, u32[]{:S(2)}) collective-permute-start(bf16[2,8,96,768]{3,2,1,0:T(8,128)(2,1)S(1)} %get-tuple-element.212), channel_id=1, source_target_pairs={{0,2},{2,0},{4,6},{6,4},{8,10},{10,8},{12,14},{14,12},{16,18},{18,... | collective-permute-start | bytes 7077896 | tf_op jit(solution)/shard_map/ppermute | solution.py:1062
  180.3 13.0 %collective-permute-start.8 = (bf16[288,768]{1,0:T(8,128)(2,1)S(1)}, bf16[288,768]{1,0:T(8,128)(2,1)S(1)}, u32[]{:S(2)}, u32[]{:S(2)}) collective-permute-start(bf16[288,768]{1,0:T(8,128)(2,1)S(1)} %get-tuple-element.203), channel_id=1, source_target_pairs={{0,1},{1,0},{2,3},{3,2},{4,5},{5,4},{6,7},{7,6},{8,9},{9,8},{10,11... | collective-permute-start | bytes 1327112 | tf_op jit(solution)/shard_map/ppermute | solution.py:1066
  181.6 19.7 %collective-permute-start.15 = (bf16[200,768]{1,0:T(8,128)(2,1)S(1)}, bf16[200,768]{1,0:T(8,128)(2,1)S(1)}, u32[]{:S(2)}, u32[]{:S(2)}) collective-permute-start(bf16[200,768]{1,0:T(8,128)(2,1)S(1)} %get-tuple-element.230), channel_id=1, source_target_pairs={{0,1},{1,0},{2,3},{3,2},{4,5},{5,4},{6,7},{7,6},{8,9},{9,8},{10,11... | collective-permute-start | bytes 921608 | tf_op jit(solution)/shard_map/ppermute | solution.py:1066
  182.4 17.7 %collective-permute-start.16 = (bf16[1,192,768]{2,1,0:T(8,128)(2,1)}, bf16[1,192,768]{2,1,0:T(8,128)(2,1)S(1)}, u32[]{:S(2)}, u32[]{:S(2)}) collective-permute-start(bf16[1,192,768]{2,1,0:T(8,128)(2,1)} %fusion.19), channel_id=1, source_target_pairs={{0,16},{2,18},{4,20},{6,22},{8,24},{10,26},{12,28},{14,30},{16,0},... | collective-permute-start | bytes 884744 | tf_op jit(solution)/shard_map/ppermute | solution.py:1062
  185.0 14.0 %collective-permute-start.11 = (bf16[2,96,768]{2,1,0:T(8,128)(2,1)}, bf16[2,96,768]{2,1,0:T(8,128)(2,1)}, u32[]{:S(2)}, u32[]{:S(2)}) collective-permute-start(bf16[2,96,768]{2,1,0:T(8,128)(2,1)} %fusion.21), channel_id=1, source_target_pairs={{0,8},{2,10},{4,12},{6,14},{8,0},{10,2},{12,4},{14,6},{16,24},{18,... | collective-permute-start | bytes 884744 | tf_op jit(solution)/shard_map/ppermute | solution.py:1062
  206.8 11.4 %collective-permute-start.17 = (bf16[1,8,288,768]{3,2,1,0:T(8,128)(2,1)S(1)}, bf16[1,8,288,768]{3,2,1,0:T(8,128)(2,1)S(1)}, u32[]{:S(2)}, u32[]{:S(2)}) collective-permute-start(bf16[1,8,288,768]{3,2,1,0:T(8,128)(2,1)S(1)} %get-tuple-element.242), channel_id=1, source_target_pairs={{0,2},{2,0},{4,6},{6,4},{8,10},{10,8},{12,14},{14,12},{16,18},{18,... | collective-permute-start | bytes 10616840 | tf_op jit(solution)/shard_map/ppermute | solution.py:1062
  206.9 38.3 %collective-permute-start.18 = (bf16[8,96,768]{2,1,0:T(8,128)(2,1)S(1)}, bf16[8,96,768]{2,1,0:T(8,128)(2,1)S(1)}, u32[]{:S(2)}, u32[]{:S(2)}) collective-permute-start(bf16[8,96,768]{2,1,0:T(8,128)(2,1)S(1)} %fusion.4), channel_id=1, source_target_pairs={{0,1},{1,0},{2,3},{3,2},{4,5},{5,4},{6,7},{7,6},{8,9},{9,8},{10,11... | collective-permute-start | bytes 3538952 | tf_op jit(solution)/shard_map/ppermute | solution.py:1066
  209.6 32.0 %collective-permute-start.42 = (bf16[192,768]{1,0:T(8,128)(2,1)S(1)}, bf16[192,768]{1,0:T(8,128)(2,1)S(1)}, u32[]{:S(2)}, u32[]{:S(2)}) collective-permute-start(bf16[192,768]{1,0:T(8,128)(2,1)S(1)} %fusion.15), channel_id=1, source_target_pairs={{0,1},{1,0},{2,3},{3,2},{4,5},{5,4},{6,7},{7,6},{8,9},{9,8},{10,11... | collective-permute-start | bytes 884744 | tf_op jit(solution)/shard_map/ppermute | solution.py:1066
  220.9 40.7 %collective-permute-start.21 = (bf16[4,288,768]{2,1,0:T(8,128)(2,1)}, bf16[4,288,768]{2,1,0:T(8,128)(2,1)}, u32[]{:S(2)}, u32[]{:S(2)}) collective-permute-start(bf16[4,288,768]{2,1,0:T(8,128)(2,1)} %fusion), channel_id=1, source_target_pairs={{0,4},{2,6},{4,0},{6,2},{8,12},{10,14},{12,8},{14,10},{16,20},{18,... | collective-permute-start | bytes 5308424 | tf_op jit(solution)/shard_map/ppermute | solution.py:1062
  251.8 12.5 %collective-permute-start.20 = (bf16[2,8,144,384]{3,2,1,0:T(8,128)(2,1)}, bf16[2,8,144,384]{3,2,1,0:T(8,128)(2,1)}, u32[]{:S(2)}, u32[]{:S(2)}) collective-permute-start(bf16[2,8,144,384]{3,2,1,0:T(8,128)(2,1)} %get-tuple-element.262), channel_id=1, source_target_pairs={{0,2},{2,0},{4,6},{6,4},{8,10},{10,8},{12,14},{14,12},{16,18},{18,... | collective-permute-start | bytes 5308424 | tf_op jit(solution)/shard_map/ppermute | solution.py:1062
  251.8 16.2 %collective-permute-start.19 = (bf16[1,8,144,768]{3,2,1,0:T(8,128)(2,1)}, bf16[1,8,144,768]{3,2,1,0:T(8,128)(2,1)}, u32[]{:S(2)}, u32[]{:S(2)}) collective-permute-start(bf16[1,8,144,768]{3,2,1,0:T(8,128)(2,1)} %get-tuple-element.258), channel_id=1, source_target_pairs={{0,2},{2,0},{4,6},{6,4},{8,10},{10,8},{12,14},{14,12},{16,18},{18,... | collective-permute-start | bytes 5308424 | tf_op jit(solution)/shard_map/ppermute | solution.py:1062
  253.5 19.2 %collective-permute-start.14 = (bf16[288,768]{1,0:T(8,128)(2,1)}, bf16[288,768]{1,0:T(8,128)(2,1)S(1)}, u32[]{:S(2)}, u32[]{:S(2)}) collective-permute-start(bf16[288,768]{1,0:T(8,128)(2,1)} %copy-done.56), channel_id=1, source_target_pairs={{0,1},{1,0},{2,3},{3,2},{4,5},{5,4},{6,7},{7,6},{8,9},{9,8},{10,11... | collective-permute-start | bytes 1327112 | tf_op jit(solution)/shard_map/ppermute | solution.py:1066
  259.4 21.2 %collective-permute-start.26 = (bf16[4,96,768]{2,1,0:T(8,128)(2,1)}, bf16[4,96,768]{2,1,0:T(8,128)(2,1)}, u32[]{:S(2)}, u32[]{:S(2)}) collective-permute-start(bf16[4,96,768]{2,1,0:T(8,128)(2,1)} %fusion.5), channel_id=1, source_target_pairs={{0,4},{2,6},{4,0},{6,2},{8,12},{10,14},{12,8},{14,10},{16,20},{18,... | collective-permute-start | bytes 1769480 | tf_op jit(solution)/shard_map/ppermute | solution.py:1062
  266.9 20.0 %collective-permute-start.25 = (bf16[8,144,384]{2,1,0:T(8,128)(2,1)}, bf16[8,144,384]{2,1,0:T(8,128)(2,1)}, u32[]{:S(2)}, u32[]{:S(2)}) collective-permute-start(bf16[8,144,384]{2,1,0:T(8,128)(2,1)} %fusion.8), channel_id=1, source_target_pairs={{0,1},{1,0},{2,3},{3,2},{4,5},{5,4},{6,7},{7,6},{8,9},{9,8},{10,11... | collective-permute-start | bytes 2654216 | tf_op jit(solution)/shard_map/ppermute | solution.py:1066
  267.3 23.1 %collective-permute-start.23 = (bf16[2,288,768]{2,1,0:T(8,128)(2,1)}, bf16[2,288,768]{2,1,0:T(8,128)(2,1)}, u32[]{:S(2)}, u32[]{:S(2)}) collective-permute-start(bf16[2,288,768]{2,1,0:T(8,128)(2,1)} %fusion.1), channel_id=1, source_target_pairs={{0,8},{2,10},{4,12},{6,14},{8,0},{10,2},{12,4},{14,6},{16,24},{18,... | collective-permute-start | bytes 2654216 | tf_op jit(solution)/shard_map/ppermute | solution.py:1062
  270.8 24.1 %collective-permute-start.22 = (bf16[4,144,768]{2,1,0:T(8,128)(2,1)}, bf16[4,144,768]{2,1,0:T(8,128)(2,1)}, u32[]{:S(2)}, u32[]{:S(2)}) collective-permute-start(bf16[4,144,768]{2,1,0:T(8,128)(2,1)} %fusion.9), channel_id=1, source_target_pairs={{0,4},{2,6},{4,0},{6,2},{8,12},{10,14},{12,8},{14,10},{16,20},{18,... | collective-permute-start | bytes 2654216 | tf_op jit(solution)/shard_map/ppermute | solution.py:1062
  282.0 14.9 %collective-permute-start.31 = (bf16[2,96,768]{2,1,0:T(8,128)(2,1)S(1)}, bf16[2,96,768]{2,1,0:T(8,128)(2,1)S(1)}, u32[]{:S(2)}, u32[]{:S(2)}) collective-permute-start(bf16[2,96,768]{2,1,0:T(8,128)(2,1)S(1)} %fusion.17), channel_id=1, source_target_pairs={{0,8},{2,10},{4,12},{6,14},{8,0},{10,2},{12,4},{14,6},{16,24},{18,... | collective-permute-start | bytes 884744 | tf_op jit(solution)/shard_map/ppermute | solution.py:1062
  288.3 14.0 %collective-permute-start.30 = (bf16[4,144,384]{2,1,0:T(8,128)(2,1)S(1)}, bf16[4,144,384]{2,1,0:T(8,128)(2,1)S(1)}, u32[]{:S(2)}, u32[]{:S(2)}) collective-permute-start(bf16[4,144,384]{2,1,0:T(8,128)(2,1)S(1)} %fusion.12), channel_id=1, source_target_pairs={{0,4},{2,6},{4,0},{6,2},{8,12},{10,14},{12,8},{14,10},{16,20},{18,... | collective-permute-start | bytes 1327112 | tf_op jit(solution)/shard_map/ppermute | solution.py:1062
  289.0 14.5 %collective-permute-start.29 = (f32[8,768]{1,0:T(8,128)S(1)}, f32[8,768]{1,0:T(8,128)S(1)}, u32[]{:S(2)}, u32[]{:S(2)}) collective-permute-start(f32[8,768]{1,0:T(8,128)S(1)} %add.423), channel_id=1, source_target_pairs={{0,4},{2,6},{4,0},{6,2},{8,12},{10,14},{12,8},{14,10},{16,20},{18,... | collective-permute-start | bytes 73736 | tf_op jit(solution)/shard_map/ppermute | solution.py:1062
  292.0 22.8 %collective-permute-start.28 = (bf16[1,288,768]{2,1,0:T(8,128)(2,1)S(1)}, bf16[1,288,768]{2,1,0:T(8,128)(2,1)S(1)}, u32[]{:S(2)}, u32[]{:S(2)}) collective-permute-start(bf16[1,288,768]{2,1,0:T(8,128)(2,1)S(1)} %fusion.14), channel_id=1, source_target_pairs={{0,16},{2,18},{4,20},{6,22},{8,24},{10,26},{12,28},{14,30},{16,0},... | collective-permute-start | bytes 1327112 | tf_op jit(solution)/shard_map/ppermute | solution.py:1062
  296.2 20.1 %collective-permute-start.27 = (bf16[2,144,768]{2,1,0:T(8,128)(2,1)S(1)}, bf16[2,144,768]{2,1,0:T(8,128)(2,1)S(1)}, u32[]{:S(2)}, u32[]{:S(2)}) collective-permute-start(bf16[2,144,768]{2,1,0:T(8,128)(2,1)S(1)} %fusion.11), channel_id=1, source_target_pairs={{0,8},{2,10},{4,12},{6,14},{8,0},{10,2},{12,4},{14,6},{16,24},{18,... | collective-permute-start | bytes 1327112 | tf_op jit(solution)/shard_map/ppermute | solution.py:1062
  298.1 19.9 %collective-permute-start.35 = (bf16[1,96,768]{2,1,0:T(8,128)(2,1)S(1)}, bf16[1,96,768]{2,1,0:T(8,128)(2,1)S(1)}, u32[]{:S(2)}, u32[]{:S(2)}) collective-permute-start(bf16[1,96,768]{2,1,0:T(8,128)(2,1)S(1)} %fusion.35), channel_id=1, source_target_pairs={{0,16},{2,18},{4,20},{6,22},{8,24},{10,26},{12,28},{14,30},{16,0},... | collective-permute-start | bytes 442376 | tf_op jit(solution)/shard_map/ppermute | solution.py:1062
  323.8 10.7 %collective-permute-start.32 = (bf16[1,144,768]{2,1,0:T(8,128)(2,1)S(1)}, bf16[1,144,768]{2,1,0:T(8,128)(2,1)S(1)}, u32[]{:S(2)}, u32[]{:S(2)}) collective-permute-start(bf16[1,144,768]{2,1,0:T(8,128)(2,1)S(1)} %fusion.24), channel_id=1, source_target_pairs={{0,16},{2,18},{4,20},{6,22},{8,24},{10,26},{12,28},{14,30},{16,0},... | collective-permute-start | bytes 663560 | tf_op jit(solution)/shard_map/ppermute | solution.py:1062
  325.2 22.2 %collective-permute-start.40 = (bf16[288,768]{1,0:T(8,128)(2,1)S(1)}, bf16[288,768]{1,0:T(8,128)(2,1)S(1)}, u32[]{:S(2)}, u32[]{:S(2)}) collective-permute-start(bf16[288,768]{1,0:T(8,128)(2,1)S(1)} %fusion.10), channel_id=1, source_target_pairs={{0,1},{1,0},{2,3},{3,2},{4,5},{5,4},{6,7},{7,6},{8,9},{9,8},{10,11... | collective-permute-start | bytes 1327112 | tf_op jit(solution)/shard_map/ppermute | solution.py:1066
  (90 other events, 736.2 us)

commit v4 on v3

--- a/solution.py
+++ b/solution.py
@@ -91,6 +91,14 @@
     return (lanes_of(column.shape[0], count) == column).astype(F32).astype(BF16)
 
 
+def reorder(column, rows_of):
+    count = column.shape[0]
+    half = count // 2
+    return jnp.concatenate(
+        [dot(one_hot(column[n * half : (n + 1) * half] - n * half, half), rows_of(n * half, half)) for n in range(2)], 0
+    )
+
+
 def split3(x):
     high = x.astype(BF16).astype(F32)
     rest = x - high
@@ -117,7 +125,7 @@
     return pl.BlockSpec(shape, lambda *_: (0,) * len(shape))
 
 
-def call(kernel, name, out_shape, args, flops, **options):
+def call(kernel, name, out_shape, args, flops, vmem=16, **options):
     size = sum(int(np.prod(a.shape)) * a.dtype.itemsize for a in args)
     outs = jax.tree.leaves(out_shape)
     size += sum(int(np.prod(o.shape)) * o.dtype.itemsize for o in outs)
@@ -126,7 +134,7 @@
         out_shape=out_shape,
         name=name,
         cost_estimate=pl.CostEstimate(flops=1024, bytes_accessed=1024, transcendentals=0),
-        compiler_params=pltpu.CompilerParams(vmem_limit_bytes=30 << 20),
+        compiler_params=pltpu.CompilerParams(vmem_limit_bytes=vmem << 20),
         **options,
     )(*args)
 
@@ -162,7 +170,7 @@
 
     def kernel(v_ref, hl_ref, e_ref, g_ref, t_ref, stream_ref, first_ref, second_ref, mark_ref):
         table = t_ref[...]
-        moved = dot(one_hot(table[:, 0:1], rows), v_ref[...])
+        moved = reorder(table[:, 0:1], lambda start, size: v_ref[start : start + size, :])
         marks = dot(one_hot(table[:, 1:2], page_rows), hl_ref[...].astype(F32).astype(BF16))
         mark = jnp.sum(
             jnp.where(lanes_of(rows, cols) == table[:, 2:3], marks, 0.0), 1, keepdims=True
@@ -179,13 +187,16 @@
         kernel,
         "visual_pre",
         (
-            shape_of(F32, rows, width),
+            hbm_of(F32, rows, width),
+            hbm_of(BF16, half, width),
             shape_of(BF16, half, width),
-            shape_of(BF16, half, width),
-            shape_of(F32, rows, PAIR),
+            hbm_of(F32, rows, PAIR),
         ),
         (visual, highlight, embed, gain, orders),
         2 * rows * rows * width,
+        in_specs=[window(rows, width), whole(page_rows, cols), whole(1, width), whole(1, width), window(*orders.shape)],
+        out_specs=[window(rows, width), window(half, width), whole(half, width), window(rows, PAIR)],
+        grid=(1,),
     )
 
 
@@ -279,12 +290,17 @@
     size = 2 * part
     steps = width // QUAD
 
-    def kernel(n_ref, r_ref, wq_ref, wk_ref, wv_ref, x_ref, q_ref, k_ref, v_ref, lse_ref, top_ref, low_ref, t_sc, l_sc):
+    def kernel(
+        n_ref, r_any, wq_ref, wk_ref, wv_ref, x_ref, q_ref, k_ref, v_ref, lse_ref, top_ref, low_ref, t_sc, l_sc, r_ref, sem
+    ):
         step = pl.program_id(0)
 
         @pl.when(step == 0)
         def _():
+            load = pltpu.make_async_copy(r_any, r_ref, sem)
+            load.start()
             top = n_ref[...].astype(F32)
+            load.wait()
             low = r_ref[...].astype(F32)
             pieces = []
             for k in range(WIN_ROW):
@@ -321,13 +337,13 @@
     grid_spec = pltpu.PrefetchScalarGridSpec(
         num_scalar_prefetch=0,
         grid=(steps,),
-        in_specs=[whole(half, width), whole(half, width)]
+        in_specs=[whole(half, width), pl.BlockSpec(memory_space=pl.ANY)]
         + [pl.BlockSpec((width, QUAD), lambda j, n=n: (0, n * steps + j)) for n in range(3)],
         out_specs=[window(rows, width)]
         + [pl.BlockSpec((rows, QUAD), lambda j: (0, j))] * 3
         + [pl.BlockSpec((1, rows, PAIR), lambda j: (j, 0, 0))]
         + [pl.BlockSpec((half, QUAD), lambda j: (0, j))] * 2,
-        scratch_shapes=[pltpu.VMEM((half, QUAD), F32)] * 2,
+        scratch_shapes=[pltpu.VMEM((half, QUAD), F32)] * 2 + [pltpu.VMEM((half, width), BF16), pltpu.SemaphoreType.DMA],
     )
     return call(
         kernel,
@@ -341,92 +357,100 @@
     )
 
 
-FF_CHUNK = 512
-ROW_BLOCK = 192
-
-
-def visual_forward(received, top, stream, window_out, gain, up, down, pages_gain, keyval_proj, orders):
+FF_CHUNK = 1024
+ROW_BLOCK = 288
+
+
+def visual_forward(
+    h, context, stream, window_out, gain, up, down, pages_gain, keyval_proj, orders, into
+):
     rows, width = stream.shape
     half = rows // 2
     steps = up.shape[1] // FF_CHUNK
-
-    def kernel(
-        r_ref, t_ref, s_ref, wo_ref, g_ref, up_ref, down_ref, pg_ref, kv_ref, o_ref,
-        unshifted_hbm, mid_hbm, normed_hbm, active_ref, slope_ref, final_hbm, pages_hbm, page_kv_ref, out_ref,
-        unshifted_ref, mid_ref, normed_ref, final_ref, pages_ref, sems,
-    ):
+    mine = pl.ds(h * half, half)
+
+    def kernel(c_any, s_hbm, wo_ref, g_ref, up_ref, down_ref, pg_ref, kv_hbm, o_hbm, *refs):
+        (
+            unshifted_ref, normed_ref, active_ref, slope_ref, pages_ref, page_kv_ref, scale_ref, out_ref,
+            final_ref, s_ref, kv_ref, o_ref, in_sems,
+        ) = refs[-13:]
         step = pl.program_id(0)
-        early = [
-            pltpu.make_async_copy(source, target, sems.at[n])
+        lane = lanes_of(half)
+        loads = [
+            pltpu.make_async_copy(source, target, in_sems.at[n])
             for n, (source, target) in enumerate(
-                ((unshifted_ref, unshifted_hbm), (mid_ref, mid_hbm), (normed_ref, normed_hbm))
+                ((c_any, unshifted_ref.at[mine]), (s_hbm.at[mine], s_ref), (kv_hbm, kv_ref), (o_hbm.at[mine], o_ref))
             )
         ]
 
         @pl.when(step == 0)
         def _():
-            unshifted_ref[:half, :] = r_ref[...]
-            unshifted_ref[half:, :] = t_ref[...]
-            mid = s_ref[...] + dot(unshifted_ref[...], wo_ref[...])
-            mid_ref[...] = mid
+            for load in loads:
+                load.start()
+            loads[0].wait()
+            branch = dot(unshifted_ref[mine, :], wo_ref[...])
+            loads[1].wait()
+            mid = s_ref[...] + branch
             final_ref[...] = mid
-            hat, _ = norm_parts(mid)
-            normed_ref[...] = (hat * g_ref[...]).astype(BF16)
-            for copy in early:
-                copy.start()
-
-        for block in range(rows // ROW_BLOCK):
-            at = slice(block * ROW_BLOCK, (block + 1) * ROW_BLOCK)
-            hidden = dot(normed_ref[at, :], up_ref[...])
-            active, slope = gelu_parts(hidden)
-            active = active.astype(BF16)
-            active_ref[at, :] = active
-            slope_ref[at, :] = slope.astype(BF16)
-            final_ref[at, :] += dot(active, down_ref[...])
+            hat, inverse = norm_parts(mid)
+            normed_ref[mine, :] = (hat * g_ref[...]).astype(BF16)
+            scale_ref[mine, :] = jnp.broadcast_to(inverse, (half, PAIR))
+
+        cols = pl.ds(pl.multiple_of(step * FF_CHUNK, FF_CHUNK), FF_CHUNK)
+        hidden = dot(normed_ref[mine, :], up_ref[...])
+        active, slope = gelu_parts(hidden)
+        active = active.astype(BF16)
+        active_ref[mine, cols] = active
+        slope_ref[mine, cols] = slope.astype(BF16)
+        final_ref[...] += dot(active, down_ref[...])
 
         @pl.when(step == steps - 1)
         def _():
+            loads[2].wait()
+            loads[3].wait()
             final = final_ref[...]
-            final_copy = pltpu.make_async_copy(final_ref, final_hbm, sems.at[3])
-            final_copy.start()
-            hat, _ = norm_parts(final)
+            hat, inverse = norm_parts(final)
+            scale_ref[mine, :] = jnp.where(lane == 0, scale_ref[mine, :], inverse)
             pages = (hat * pg_ref[...]).astype(BF16)
-            pages_ref[...] = pages
-            pages_copy = pltpu.make_async_copy(pages_ref, pages_hbm, sems.at[4])
-            pages_copy.start()
-            page_kv_ref[...] = dot(pages, kv_ref[...]).astype(BF16)
-            out_ref[...] = dot(one_hot(o_ref[:, 3:4], rows), final.astype(BF16)).astype(BF16)
-            for copy in early + [final_copy, pages_copy]:
-                copy.wait()
-
+            pages_ref[mine, :] = pages
+            page_kv_ref[mine, :] = dot(pages, kv_ref[...]).astype(BF16)
+            out_ref[...] = dot(one_hot(o_ref[:, 3:4] - h * half, half), final.astype(BF16)).astype(BF16)
+
+    anywhere = pl.BlockSpec(memory_space=pl.ANY)
+    args = (context, stream, window_out, gain, up, down, pages_gain, keyval_proj, orders)
+    in_specs = [
+        anywhere, anywhere, window(*window_out.shape), whole(1, width),
+        pl.BlockSpec((width, FF_CHUNK), lambda j: (0, j)), pl.BlockSpec((FF_CHUNK, width), lambda j: (j, 0)),
+        whole(1, width), anywhere, anywhere,
+    ]
+    extra = {}
+    if into is not None:
+        extra = dict(input_output_aliases={len(args) + n: n for n in range(len(into))})
+        args += tuple(into)
+        in_specs += [whole()] * (len(into) - 1) + [anywhere]
     grid_spec = pltpu.PrefetchScalarGridSpec(
         num_scalar_prefetch=0,
         grid=(steps,),
-        in_specs=[
-            whole(half, width), whole(half, width), whole(rows, width), whole(*window_out.shape), whole(1, width),
-            pl.BlockSpec((width, FF_CHUNK), lambda j: (0, j)), pl.BlockSpec((FF_CHUNK, width), lambda j: (j, 0)),
-            whole(1, width), whole(*keyval_proj.shape), whole(*orders.shape),
-        ],
-        out_specs=[pl.BlockSpec(memory_space=pl.ANY)] * 3
-        + [pl.BlockSpec((rows, FF_CHUNK), lambda j: (0, j))] * 2
-        + [pl.BlockSpec(memory_space=pl.ANY)] * 2
-        + [whole(rows, 2 * width), window(rows, width)],
+        in_specs=in_specs,
+        out_specs=[whole()] * 7 + [pl.BlockSpec((half, width), lambda j: (h, 0))],
         scratch_shapes=[
-            pltpu.VMEM((rows, width), BF16), pltpu.VMEM((rows, width), F32), pltpu.VMEM((rows, width), BF16),
-            pltpu.VMEM((rows, width), F32), pltpu.VMEM((rows, width), BF16), pltpu.SemaphoreType.DMA((5,)),
+            pltpu.VMEM((half, width), F32), pltpu.VMEM((half, width), F32), pltpu.VMEM(keyval_proj.shape, BF16),
+            pltpu.VMEM((half, orders.shape[1]), jnp.int32), pltpu.SemaphoreType.DMA((4,)),
         ],
     )
     return call(
         kernel,
         "visual_forward",
         (
-            hbm_of(BF16, rows, width), hbm_of(F32, rows, width), hbm_of(BF16, rows, width),
-            hbm_of(BF16, rows, up.shape[1]), hbm_of(BF16, rows, up.shape[1]),
-            hbm_of(F32, rows, width), hbm_of(BF16, rows, width), shape_of(BF16, rows, 2 * width), shape_of(BF16, rows, width),
+            shape_of(BF16, rows, width), shape_of(BF16, rows, width), shape_of(BF16, rows, up.shape[1]),
+            shape_of(BF16, rows, up.shape[1]), shape_of(BF16, rows, width), shape_of(BF16, rows, 2 * width),
+            shape_of(F32, rows, PAIR), hbm_of(BF16, rows, width),
         ),
-        (received, top, stream, window_out, gain, up, down, pages_gain, keyval_proj, orders),
-        2 * rows * width * (width + 2 * up.shape[1] + 2 * width + rows),
+        args,
+        0,
+        vmem=24,
         grid_spec=grid_spec,
+        **extra,
     )
 
 
@@ -590,7 +614,7 @@
         num_scalar_prefetch=1,
         grid=(steps,),
         in_specs=[
-            whole(own_count, width + STAT), whole(own_count, width + STAT),
+            whole(own_count, width + STAT), window(own_count, width + STAT),
             pl.BlockSpec((own_count, width), lambda j, w: (w[0], 0)),
             whole(*cross_out.shape), whole(1, width),
             pl.BlockSpec((width, FF_CHUNK), lambda j, w: (0, j)), pl.BlockSpec((FF_CHUNK, width), lambda j, w: (j, 0)),
@@ -757,13 +781,15 @@
     )
 
 
-def visual_backward(kv_grad, keyval_proj, final, upstream, orders, pages_gain, mid, gain, window_out, up, down, slope):
-    rows, width = final.shape
+def visual_backward(
+    kv_grad, keyval_proj, pages, upstream, orders, pages_gain, normed, gain, scales, window_out, up, down, slope
+):
+    rows, width = pages.shape
     half = rows // 2
     steps = up.shape[1] // FF_CHUNK
 
     def kernel(
-        kv_ref, kp_ref, f_ref, u_ref, o_ref, pg_ref, m_ref, g_ref, wo_ref, up_ref, down_ref, s_ref,
+        kv_ref, kp_ref, f_ref, u_ref, o_ref, pg_ref, m_ref, g_ref, i_ref, wo_ref, up_ref, down_ref, s_ref,
         out_grad_ref, grad_ref, mid_grad_ref, branch_ref, first_ref, second_ref, pages_gain_ref, gain_ref, acc_sc,
     ):
         step = pl.program_id(0)
@@ -771,24 +797,25 @@
         @pl.when(step == 0)
         def _():
             pages = dot_t(kv_ref[...], kp_ref[...])
-            hat, inverse = norm_parts(f_ref[...])
+            hat, inverse = f_ref[...].astype(F32) * (1.0 / pg_ref[...]), i_ref[:, 1:2]
             pages_gain_ref[...] = jnp.sum(pages * hat, 0, keepdims=True)
-            upstream_rows = dot(one_hot(o_ref[:, 0:1], rows), u_ref[...])
+            upstream_rows = reorder(o_ref[:, 0:1], lambda start, size: u_ref[start : start + size, :])
             final_grad = upstream_rows + norm_back(hat, inverse, pg_ref[...], pages)
             mid_grad_ref[...] = final_grad
             out_grad_ref[...] = final_grad.astype(BF16)
             acc_sc[...] = jnp.zeros_like(acc_sc)
 
+        cols = pl.ds(pl.multiple_of(step * FF_CHUNK, FF_CHUNK), FF_CHUNK)
         for block in range(rows // ROW_BLOCK):
             at = slice(block * ROW_BLOCK, (block + 1) * ROW_BLOCK)
-            grad = (dot_t(out_grad_ref[at, :], down_ref[...]) * s_ref[at, :].astype(F32)).astype(BF16)
+            grad = (dot_t(out_grad_ref[at, :], down_ref[cols, :]) * s_ref[at, cols].astype(F32)).astype(BF16)
             grad_ref[at, :] = grad
-            acc_sc[at, :] += dot_t(grad, up_ref[...])
+            acc_sc[at, :] += dot_t(grad, up_ref[:, cols])
 
         @pl.when(step == steps - 1)
         def _():
             grad = acc_sc[...]
-            hat, inverse = norm_parts(m_ref[...])
+            hat, inverse = m_ref[...].astype(F32) * (1.0 / g_ref[...]), i_ref[:, 0:1]
             gain_ref[...] = jnp.sum(grad * hat, 0, keepdims=True)
             mid_grad = mid_grad_ref[...] + norm_back(hat, inverse, g_ref[...], grad)
             mid_grad_ref[...] = mid_grad
@@ -803,9 +830,9 @@
         grid=(steps,),
         in_specs=[
             whole(rows, 2 * width), whole(*keyval_proj.shape), whole(rows, width), whole(rows, width),
-            whole(*orders.shape), whole(1, width), whole(rows, width), whole(1, width), whole(*window_out.shape),
-            pl.BlockSpec((width, FF_CHUNK), lambda j: (0, j)), pl.BlockSpec((FF_CHUNK, width), lambda j: (j, 0)),
-            pl.BlockSpec((rows, FF_CHUNK), lambda j: (0, j)),
+            whole(*orders.shape), whole(1, width), whole(rows, width), whole(1, width), whole(), whole(*window_out.shape),
+            whole(), whole(),
+            whole(),
         ],
         out_specs=[
             whole(rows, width), pl.BlockSpec((rows, FF_CHUNK), lambda j: (0, j)), whole(rows, width), whole(rows, width),
@@ -820,8 +847,9 @@
             shape_of(BF16, rows, width), shape_of(BF16, rows, up.shape[1]), shape_of(F32, rows, width), shape_of(BF16, rows, width),
             shape_of(BF16, half, width), shape_of(BF16, half, width), shape_of(F32, 1, width), shape_of(F32, 1, width),
         ),
-        (kv_grad, keyval_proj, final, upstream, orders, pages_gain, mid, gain, window_out, up, down, slope),
+        (kv_grad, keyval_proj, pages, upstream, orders, pages_gain, normed, gain, scales, window_out, up, down, slope),
         2 * rows * width * (3 * width + 2 * up.shape[1] + rows),
+        vmem=16,
         grid_spec=grid_spec,
     )
 
@@ -930,9 +958,11 @@
         gain_ref[...] = jnp.sum(grad * hat, 0, keepdims=True)
         result = m_ref[...] + norm_back(hat, inverse, g_ref[...], grad)
         embed_ref[...] = jnp.sum(mark_ref[:, 0:1] * result, 0, keepdims=True)
-        order = one_hot(o_ref[:, 3:4], rows)
-        high, middle, low = split3(result)
-        out_ref[...] = dot(order, high.astype(BF16)) + dot(order, middle.astype(BF16)) + dot(order, low.astype(BF16))
+        high, middle, low = (part.astype(BF16) for part in split3(result))
+        for n in range(2):
+            at = slice(n * half, (n + 1) * half)
+            place = one_hot(o_ref[at, 3:4] - n * half, half)
+            out_ref[at, :] = dot(place, high[at]) + dot(place, middle[at]) + dot(place, low[at])
 
     return call(
         kernel,
@@ -974,7 +1004,7 @@
             scratch_shapes=scratch,
         ),
         cost_estimate=pl.CostEstimate(flops=1024, bytes_accessed=1024, transcendentals=0),
-        compiler_params=pltpu.CompilerParams(vmem_limit_bytes=30 << 20),
+        compiler_params=pltpu.CompilerParams(vmem_limit_bytes=20 << 20),
         **extra,
     )(*args)
 
@@ -1003,13 +1033,14 @@
                     source = pl.multiple_of((p_ref[0] ^ rel) * block, block)
                     move[place * block : (place + 1) * block, :] = turn[pl.ds(source, block), :]
 
-        kept = sent = None
+        found = None
         for right, move in zip(rights, moved):
             right_side = right[...]
-            one, two = dot(move[: depth // 2, :], right_side), dot(move[depth // 2 :, :], right_side)
-            kept, sent = (one, two) if kept is None else (kept + one, sent + two)
-        keep_ref[...] = kept.astype(BF16).reshape(keep_ref.shape)
-        send_ref[...] = sent.astype(BF16).reshape(send_ref.shape)
+            part = dot(move[...], right_side)
+            found = part if found is None else found + part
+        found = found.astype(BF16)
+        keep_ref[...] = found[: depth // 2].reshape(keep_ref.shape)
+        send_ref[...] = found[depth // 2 :].reshape(send_ref.shape)
 
     if split:
         per = steps // 2
@@ -1042,20 +1073,28 @@
             rel = rel | ((place >> (bits - 1 - bit)) & 1) << (bit - 1)
         return rel
 
-    def kernel(p_ref, w_ref, l_ref, r_ref, *refs):
-        keep_ref, send_ref, turned_sc = refs[-3:]
-        turned_sc[...] = l_ref[...].T
-        right_side = r_ref[...]
-        for out_ref, side in ((keep_ref, p_ref[0] & 1), (send_ref, 1 - (p_ref[0] & 1))):
-            for rel in range(2):
-                source = pl.multiple_of(side * block + (w_ref[0] ^ rel) * piece, piece)
-                out_ref[rel, 0] = dot(turned_sc[pl.ds(source, piece), :], right_side).astype(BF16)
-
-    out_block = pl.BlockSpec((2, 1, piece, D), lambda s, p, w: (0, s, offset // piece, 0))
-    in_specs = [pl.BlockSpec((rows, 2 * block), lambda s, p, w: (0, (p[0] >> 1) ^ other_bits(s))), whole(rows, D)]
-    scratch = [pltpu.VMEM((2 * block, rows), BF16)]
-    args = (page_index, win_index, left, right)
-    return grad_call(kernel, name, at, in_specs, args, into, out_block, count, scratch, 2 * rows * depth * D)
+    def kernel(p_ref, w_ref, a_ref, b_ref, r_ref, keep_ref, send_ref, turned_sc, moved_sc):
+        for n, left_ref in enumerate((a_ref, b_ref)):
+            turned_sc[...] = left_ref[...].T
+            for side in range(2):
+                for rel in range(2):
+                    source = pl.multiple_of(((p_ref[0] & 1) ^ side) * block + (w_ref[0] ^ rel) * piece, piece)
+                    place = (2 * (2 * n + side) + rel) * piece
+                    moved_sc[place : place + piece, :] = turned_sc[pl.ds(source, piece), :]
+        result = dot(moved_sc[...], r_ref[...]).astype(BF16)
+        for n in range(2):
+            for side, out_ref in enumerate((keep_ref, send_ref)):
+                for rel in range(2):
+                    place = (2 * (2 * n + side) + rel) * piece
+                    out_ref[rel, n] = result[place : place + piece]
+
+    out_block = pl.BlockSpec((2, 2, piece, D), lambda s, p, w: (0, s, offset // piece, 0))
+    in_specs = [
+        pl.BlockSpec((rows, 2 * block), lambda s, p, w, n=n: (0, (p[0] >> 1) ^ other_bits(2 * s + n))) for n in range(2)
+    ] + [whole(rows, D)]
+    scratch = [pltpu.VMEM((2 * block, rows), BF16), pltpu.VMEM((4 * block, rows), BF16)]
+    args = (page_index, win_index, left, left, right)
+    return grad_call(kernel, name, at, in_specs, args, into, out_block, count // 2, scratch, 2 * rows * depth * D)
 
 
 def swap_page(x, bit):
@@ -1190,21 +1229,31 @@
     block = D // pages
     tall = FF // pages
 
-    stream, first_normed, normed, mark = visual_pre(visual_in.reshape(rows, D), highlight[0], embed, g_window, orders)
+    stream, first_normed, normed, mark = visual_pre(
+        from_hbm(visual_in.reshape(rows, D)), highlight[0], embed, g_window, from_hbm(orders)
+    )
     ahead = swap_win(first_normed)
     queries, text_normed, text_kv = text_pre(own_index, text, g_text, text_query, keyval_proj, own_count)
     ahead, queries = tie((ahead, queries))
     shifted, win_q, win_k, win_v, win_log, top, low = window_forward(normed, ahead, window_proj_hbm)
     behind = swap_win(low)
-    unshifted, mid, ff_normed, active, slope, final, pages_normed, page_kv, visual_out = visual_forward(
-        behind, top, stream, window_out, g_visual, visual_up_hbm, visual_down_hbm, g_pages, keyval_proj, orders
+    def ahead_of_pages(h, context, into):
+        return visual_forward(
+            h, context, from_hbm(stream), from_hbm(window_out), g_visual, visual_up_hbm, visual_down_hbm, g_pages,
+            from_hbm(keyval_proj), from_hbm(orders), into,
+        )
+
+    halves = ahead_of_pages(1, top, None)
+    behind, first_half = tie((behind, halves[0]))
+    unshifted, ff_normed, active, slope, pages_normed, page_kv, scales, visual_out = ahead_of_pages(
+        0, behind, (first_half, *halves[1:])
     )
     away = cross_forward(other_index, queries, page_kv, text_kv, text_mask)
     theirs = swap_win(away)
     mine = cross_forward(first_index, queries, page_kv, text_kv, text_mask)
     theirs, mine = tie((theirs, mine))
     (text_out, context, reply_normed, text_active, text_hidden_grad, text_mid_grad, branch, pack, reply_gain) = text_block(
-        own_index, mine, theirs, text, cross_out, g_reply, text_up_hbm, text_down_hbm, text_up_stream
+        own_index, mine, from_hbm(theirs), text, cross_out, g_reply, text_up_hbm, text_down_hbm, text_up_stream
     )
     pack_other = swap_win(pack)
     order = Order(pack)
@@ -1216,6 +1265,11 @@
     )
     reply_b = Reduction(*grads, True)
     order.after(grads[0])
+    grads_a = narrow_grad(
+        where, [(context, order.before(branch))], (1, count, 3 * block, D), 2 * block, None, "cross_out_grad"
+    )
+    window_grads = grads_a
+    order.after(grads_a[0])
     pack_other = order.before(pack_other)
     order.after(pack_other)
     order.step(reply_a, reply_b, reply_b)
@@ -1226,14 +1280,16 @@
     order.step(reply_a, reply_b)
     query_theirs = swap_win(query_away)
     (out_grad, hidden_grad, mid_grad, window_branch, context_first, context_second, pages_gain, visual_gain) = visual_backward(
-        order.before(page_kv_grad), keyval_proj, final, visual_upstream.reshape(rows, D), orders, g_pages, mid, g_visual,
-        window_out, visual_up_hbm, visual_down_hbm, from_hbm(slope),
+        order.before(page_kv_grad), keyval_proj, pages_normed, visual_upstream.reshape(rows, D), orders, g_pages, ff_normed,
+        g_visual, scales, window_out, visual_up, visual_down, slope,
     )
     later = swap_win(context_first)
     order.after(out_grad)
+    query_theirs = order.before(query_theirs)
+    order.after(query_theirs)
     order.step(reply_a, reply_b)
     grads = wide_grad(
-        where, from_hbm(order.before(active)), out_grad, (2, count, tall // 2, D), 0, None, "visual_down_grad"
+        where, order.before(active), out_grad, (2, count, tall // 2, D), 0, None, "visual_down_grad"
     )
     visual_b = Reduction(*grads, True)
     order.after(grads[0])
@@ -1245,7 +1301,7 @@
     order.after(later)
     order.step(visual_b, reply_b, reply_a)
     text_grad, query_grad, text_gain = text_tail(
-        own_index, query_mine, order.before(query_theirs), text_kv_grad, text, text_mid_grad, g_text, text_query, keyval_proj
+        own_index, order.before(query_mine), query_theirs, text_kv_grad, text, text_mid_grad, g_text, text_query, keyval_proj
     )
     grads_a = narrow_grad(where, [(text_normed, query_grad)], at, tall, grads_a, "text_query_grad")
     grads_a = narrow_grad(where, [(unshifted, window_branch)], at, tall + block, grads_a, "window_out_grad")
@@ -1257,10 +1313,6 @@
     grads_b = narrow_grad(where, pairs, at_b, 0, None, "keyval_grad", D // 2, split=True)
     order.after(grads_b[0])
     order.step(visual_a)
-    grads_a = narrow_grad(
-        where, [(context, order.before(branch))], (1, count, 3 * block, D), 2 * block, None, "cross_out_grad"
-    )
-    order.after(grads_a[0])
     order.hold(reply_a)
     order.step(reply_b)
     packed_grad, top_grad, low_grad = window_backward(
@@ -1268,9 +1320,8 @@
     )
     earlier = swap_win(low_grad)
     order.after(packed_grad)
-    order.hold(reply_b)
     grads_a = narrow_grad(
-        where, [(shifted, order.before(packed_grad))], (1, count, 3 * block, D), 0, grads_a, "window_proj_grad", steps=2
+        where, [(shifted, order.before(packed_grad))], (1, count, 3 * block, D), 0, window_grads, "window_proj_grad", steps=2
     )
     window_a = Reduction(*grads_a, False)
     order.after(grads_a[0])
@@ -1286,8 +1337,9 @@
     )
     sums = SmallSum([window_gain, visual_gain, text_gain, pages_gain, reply_gain, embed_grad])
     order.after(window_gain)
-    order.step(sums, visual_b, window_b, sums, visual_a, window_a, visual_b, window_b, sums, visual_a, window_a)
-    order.step(visual_b, window_b, sums, window_a, sums, window_b)
+    order.step(sums, visual_b, window_b, sums, visual_a, window_a, visual_b)
+    order.hold(reply_b)
+    order.step(window_b, sums, window_a, visual_b, visual_a, window_b, sums, window_a, sums, window_b)
     left = [one for one in (reply_a, reply_b, visual_a, visual_b, window_a, window_b, sums) if one.todo]
     assert not left
     reply_a, reply_b, visual_a, visual_b, window_a, window_b, sums = (

time: 357 us -> 337 us (0.944)
  local copies, waits for them, and re-layouts: 29.6 us -> 18.1 us
  Pallas kernels: 155 us -> 151 us
    unnamed x155 -> x139, local copies, waits for them, and re-layouts: 22.6 us -> 11.9 us
    pallas_call x10, Pallas kernels: 36.1 us -> 32.2 us  [grad_call(): pl.pallas_call(kernel, out_shape=(shape_of(BF16, *at),) * 2, name=name, g...]
    pallas_call x12 -> x13, Pallas kernels: 119 us -> 118 us  [call(): pl.pallas_call(kernel, out_shape=out_shape, name=name, cost_estimate=pl.C...]
  transfers between devices with their start and end apart: 45 -> 45, of which waited for: 22 -> 18; matrix products, arithmetic and copies ran while one was open for 13% -> 12% of each run, Pallas kernels for 24% -> 27%
where the time goes in v4:
time: 337 us; the launch traced here: 333 us
  Pallas kernels  151 us (45%)
  waiting for transfers between devices  71.4 us (21%)
  starting transfers between devices  48.8 us (14%)
  other arithmetic  42.7 us (13%)
  local copies, waits for them, and re-layouts  18.1 us (5%)
    pallas_call x13, Pallas kernels, call(): pl.pallas_call(kernel, out_shape=out_shape, name=name, cost_estimate=pl.C...  118 us
    ppermute x28, waiting for transfers between devices, swap_page(): lax.ppermute(x, 'page', [(i, i ^ 1 << bit) for i in range(lax.axis_size('...  37.3 us
    convert_element_type x27, other arithmetic, total(): return result.astype(BF16)  35.1 us
    ppermute x17, waiting for transfers between devices, swap_win(): return lax.ppermute(x, 'win', [(0, 1), (1, 0)])  34.1 us
    pallas_call x10, Pallas kernels, grad_call(): pl.pallas_call(kernel, out_shape=(shape_of(BF16, *at),) * 2, name=name, g...  32.2 us
    ppermute x28, starting transfers between devices, swap_page(): lax.ppermute(x, 'page', [(i, i ^ 1 << bit) for i in range(lax.axis_size('...  30.2 us
    ppermute x17, starting transfers between devices, swap_win(): return lax.ppermute(x, 'win', [(0, 1), (1, 0)])  18.6 us
    unnamed x139, local copies, waits for them, and re-layouts  11.9 us
  transfers between devices with their start and end apart: 45, of which 18 were waited for; matrix products, arithmetic and copies ran while one was open for 12% of the time, Pallas kernels for 27%

profile of v4, /device:TPU:0, one launch (start us, length us, event | category | flops | bytes accessed | tf_op | source)
XLA Modules:
  0.0 333.4 jit_solution(6451640015311312232)
XLA Ops:
  2.8 3.6 %visual_pre.1 = (f32[576,768]{1,0:T(8,128)}, bf16[288,768]{1,0:T(8,128)(2,1)}, bf16[288,768]{1,0:T(8,128)(2,1)S(1)}, f32[576,128]{1,0:T(8,128)}) custom-call(bf16[576,768]{1,0:T(8,128)(2,1)} %bitcast.237, s32[12,48]{1,0:T(8,128)S(1)} %bitcast.236, f32[1,768]{1,0:T(1,128)S(1)} %reshape.456.e_ref, f32[1,768]{1,0:T(1,128)S(1)} %reshape.457.g_ref, ...), custom_call_target="tpu_custom_call" | custom-call | flops 1024 | bytes 1024 | tf_op jit(solution)/shard_map/visual_pre/pallas_call | solution.py:132
  6.4 2.9 collective-permute-start
  14.9 4.8 %collective-permute-done.r_any = bf16[288,768]{1,0:T(8,128)(2,1)S(1)} collective-permute-done((bf16[288,768]{1,0:T(8,128)(2,1)}, bf16[288,768]{1,0:T(8,128)(2,1)S(1)}, u32[]{:S(2)}, u32[]{:S(2)}) %collective-permute-start) | collective-permute-done | bytes 442400 | tf_op jit(solution)/shard_map/ppermute | solution.py:1105
  19.8 11.4 %window_forward.1 = (bf16[576,768]{1,0:T(8,128)(2,1)}, bf16[576,768]{1,0:T(8,128)(2,1)}, bf16[576,768]{1,0:T(8,128)(2,1)}, bf16[576,768]{1,0:T(8,128)(2,1)}, f32...) custom-call(bf16[288,768]{1,0:T(8,128)(2,1)S(1)} %get-tuple-element.168.n_ref, ...), custom_call_target="tpu_custom_call" | custom-call | flops 1024 | bytes 1024 | tf_op jit(solution)/shard_map/window_forward/pallas_call | solution.py:132
  33.1 11.8 %visual_forward.2 = (bf16[576,768]{1,0:T(8,128)(2,1)S(1)}, bf16[576,768]{1,0:T(8,128)(2,1)S(1)}, bf16[576,3072]{1,0:T(8,128)(2,1)S(1)}, bf16[576,3072]{1,0:T(8,1...) custom-call(bf16[288,768]{1,0:T(8,128)(2,1)S(1)} %get-tuple-element., ...), custom_call_target="tpu_custom_call" | custom-call | flops 1024 | bytes 1024 | tf_op jit(solution)/shard_map/visual_forward/pallas_call | solution.py:132
  45.0 12.1 %visual_forward.3 = (bf16[576,768]{1,0:T(8,128)(2,1)S(1)}, bf16[576,768]{1,0:T(8,128)(2,1)S(1)}, bf16[576,3072]{1,0:T(8,128)(2,1)S(1)}, bf16[576,3072]{1,0:T(8,1...) custom-call(bf16[288,768]{1,0:T(8,128)(2,1)} %collective-permute-don, ...), custom_call_target="tpu_custom_call", output_to_operand_aliasing={{0}: (9, {}), {1}: (10, {}), {2}: (11, {}), {3}: (12, {}), ... | custom-call | flops 1024 | bytes 1024 | tf_op jit(solution)/shard_map/visual_forward/pallas_call | solution.py:132
  59.9 7.8 %cross_forward.2 = bf16[200,896]{1,0:T(8,128)(2,1)} custom-call(s32[2]{0:T(128)S(1)} %pad_add_fusion.i_ref, bf16[400,768]{1,0:T(8,128)(2,1)S(1)} %copy-done.10, bf16[576,1536]{1,0:T(8,128)(2,1)S(1)} %get-tuple-element.187.pk_ref.pv_ref, bf16[576,1536]{1,0:T(8,128)(2,1)S(1)} %get-tuple-element.187.pk_ref.pv_ref, ...), custom_call_target="tpu_custom_call" | custom-call | flops 1024 | bytes 1024 | tf_op jit(solution)/shard_map/cross_forward/pallas_call | solution.py:132
  68.1 7.3 %cross_forward.3.a_ref = bf16[200,896]{1,0:T(8,128)(2,1)S(1)} custom-call(s32[2]{0:T(128)S(1)} %pad_add_fusion.1.i_ref, bf16[400,768]{1,0:T(8,128)(2,1)S(1)} %copy-done.10, bf16[576,1536]{1,0:T(8,128)(2,1)S(1)} %get-tuple-element.187.pk_ref.pv_ref, bf16[576,1536]{1,0:T(8,128)(2,1)S(1)} %get-tuple-element.187.pk_ref.pv_ref, ...), custom_call_target="tpu_custom_call" | custom-call | flops 1024 | bytes 1024 | tf_op jit(solution)/shard_map/cross_forward/pallas_call | solution.py:132
  77.0 12.0 %text_block.1 = (bf16[200,768]{1,0:T(8,128)(2,1)}, bf16[200,768]{1,0:T(8,128)(2,1)S(1)}, bf16[200,768]{1,0:T(8,128)(2,1)S(1)}, bf16[200,3072]{1,0:T(8,128)(2,1)S...) custom-call(s32[1]{0:T(128)} %bitcast.1.w_ref, ...), custom_call_target="tpu_custom_call" | custom-call | flops 1024 | bytes 1024 | tf_op jit(solution)/shard_map/text_block/pallas_call | solution.py:132
  92.2 2.9 text_down_grad.1
  96.6 5.7 %collective-permute-done.3.b_ref = bf16[200,896]{1,0:T(8,128)(2,1)S(1)} collective-permute-done((bf16[200,896]{1,0:T(8,128)(2,1)S(1)}, bf16[200,896]{1,0:T(8,128)(2,1)S(1)}, u32[]{:S(2)}, u32[]{:S(2)}) %collective-permute-start.3) | collective-permute-done | bytes 358432 | tf_op jit(solution)/shard_map/ppermute | solution.py:1105
  104.4 2.9 collective-permute-done.5
  108.3 19.1 %cross_backward.1 = (bf16[576,1536]{1,0:T(8,128)(2,1)S(1)}, bf16[200,1536]{1,0:T(8,128)(2,1)S(1)}, f32[200,768]{1,0:T(8,128)S(1)}, bf16[200,768]{1,0:T(8,128)(2,1)S(1)}) custom-call(s32[2]{0:T(128)S(1)} %pad_add_fusion.i_ref, bf16[400,768]{1,0:T(8,128)(2,1)S(1)} %copy-done.10, bf16[400,768]{1,0:T(8,128)(2,1)S(1)} %copy-done.10, ...), custom_call_target="tpu_custom_call" | custom-call | flops 1024 | bytes 1024 | tf_op jit(solution)/shard_map/cross_backward/pallas_call | solution.py:132
  127.4 3.7 %collective-permute-done.7 = bf16[4,192,768]{2,1,0:T(8,128)(2,1)S(1)} collective-permute-done((bf16[4,192,768]{2,1,0:T(8,128)(2,1)S(1)}, bf16[4,192,768]{2,1,0:T(8,128)(2,1)S(1)}, u32[]{:S(2)}, u32[]{:S(2)}) %collective-permute-start.7) | collective-permute-done | bytes 1179680 | tf_op jit(solution)/shard_map/ppermute | solution.py:1101
  133.1 2.6 collective-permute-done.6
  138.2 11.3 %visual_backward.1 = (bf16[576,768]{1,0:T(8,128)(2,1)S(1)}, bf16[576,3072]{1,0:T(8,128)(2,1)S(1)}, f32[576,768]{1,0:T(8,128)S(1)}, bf16[576,768]{1,0:T(8,128)(2,...) custom-call(bf16[576,1536]{1,0:T(8,128)(2,1)S(1)} %get-tuple-element, ...), custom_call_target="tpu_custom_call" | custom-call | flops 1024 | bytes 1024 | tf_op jit(solution)/shard_map/visual_backward/pallas_call | solution.py:132
  152.4 6.1 %visual_down_grad.1 = (bf16[2,8,96,768]{3,2,1,0:T(8,128)(2,1)S(1)}, bf16[2,8,96,768]{3,2,1,0:T(8,128)(2,1)S(1)}) custom-call(s32[1]{0:T(128)} %bitcast.7.p_ref, s32[1]{0:T(128)} %bitcast.1.w_ref, bf16[576,3072]{1,0:T(8,128)(2,1)S(1)} %copy-done.3, bf16[576,3072]{1,0:T(8,128)(2,1)S(1)} %copy-done.3, bf16[576,768]{1,0:T(8,128)(2,1)S(1)} %get-tuple-element.231.r_ref), custom_call_target="tpu_custom_call" | custom-call | flops 1024 | bytes 1024 | tf_op jit(solution)/shard_map/visual_down_grad/pallas_call | solution.py:995
  164.4 5.3 %visual_up_grad.1 = (bf16[1,8,288,768]{3,2,1,0:T(8,128)(2,1)S(1)}, bf16[1,8,288,768]{3,2,1,0:T(8,128)(2,1)S(1)}) custom-call(s32[1]{0:T(128)} %bitcast.7.p_ref, s32[1]{0:T(128)} %bitcast.1.w_ref, bf16[576,768]{1,0:T(8,128)(2,1)S(1)} %copy-done.12, bf16[576,3072]{1,0:T(8,128)(2,1)S(1)} %get-tuple-element.240.refs_1_), custom_call_target="tpu_custom_call" | custom-call | flops 1024 | bytes 1024 | tf_op jit(solution)/shard_map/visual_up_grad/pallas_call | solution.py:995
  171.5 5.3 %collective-permute-done.12 = bf16[2,96,768]{2,1,0:T(8,128)(2,1)S(1)} collective-permute-done((bf16[2,96,768]{2,1,0:T(8,128)(2,1)S(1)}, bf16[2,96,768]{2,1,0:T(8,128)(2,1)S(1)}, u32[]{:S(2)}, u32[]{:S(2)}) %collective-permute-start.12) | collective-permute-done | bytes 294944 | tf_op jit(solution)/shard_map/ppermute | solution.py:1101
  186.8 5.5 %keyval_grad.1 = (bf16[2,8,144,384]{3,2,1,0:T(8,128)(2,1)S(1)}, bf16[2,8,144,384]{3,2,1,0:T(8,128)(2,1)}) custom-call(s32[1]{0:T(128)} %bitcast.7.p_ref, s32[1]{0:T(128)} %bitcast.1.w_ref, bf16[200,768]{1,0:T(8,128)(2,1)S(1)} %copy-done.32, bf16[576,768]{1,0:T(8,128)(2,1)S(1)} %copy-done.14, bf16[200,1536]{1,0:T(8,128)(2,1)S(1)} %get-tuple-element.261.kv_ref.refs_2_, ...), custom_call_target="tpu_custom_call" | custom-call | flops 1024 | bytes 1024 | tf_op jit(solution)/shard_map/keyval_grad/pallas_call | solution.py:995
  192.3 3.2 collective-permute-done.14
  201.1 13.2 %window_backward.1 = (bf16[576,2304]{1,0:T(8,128)(2,1)S(1)}, bf16[288,768]{1,0:T(8,128)(2,1)S(1)}, bf16[288,768]{1,0:T(8,128)(2,1)S(1)}) custom-call(bf16[576,768]{1,0:T(8,128)(2,1)S(1)} %copy-done.36, bf16[576,768]{1,0:T(8,128)(2,1)S(1)} %copy-done.37, bf16[576,768]{1,0:T(8,128)(2,1)S(1)} %copy-done.38, f32[3,576,128]{2,1,0:T(8,128)S(1)} %copy-done.39, ...), custom_call_target="tpu_custom_call" | custom-call | flops 1024 | bytes 1024 | tf_op jit(solution)/shard_map/window_backward/pallas_call | solution.py:132
  215.8 3.6 %window_proj_grad.1 = (bf16[1,8,144,768]{3,2,1,0:T(8,128)(2,1)S(1)}, bf16[1,8,144,768]{3,2,1,0:T(8,128)(2,1)}) custom-call(s32[1]{0:T(128)} %bitcast.7.p_ref, s32[1]{0:T(128)} %bitcast.1.w_ref, bf16[576,768]{1,0:T(8,128)(2,1)S(1)} %copy-done.26, bf16[576,2304]{1,0:T(8,128)(2,1)S(1)} %get-tuple-element.254.refs_1_, ...), custom_call_target="tpu_custom_call", output_to_operand_aliasing={{0}: (4, {}), {1}: (5, {})} | custom-call | flops 1024 | bytes 1024 | tf_op jit(solution)/shard_map/window_proj_grad/pallas_call | solution.py:995
  220.8 2.9 window_value_grad.1
  227.5 8.2 %collective-permute-done.42 = bf16[192,768]{1,0:T(8,128)(2,1)} collective-permute-done((bf16[192,768]{1,0:T(8,128)(2,1)}, bf16[192,768]{1,0:T(8,128)(2,1)}, u32[]{:S(2)}, u32[]{:S(2)}) %collective-permute-start.42) | collective-permute-done | bytes 294944 | tf_op jit(solution)/shard_map/ppermute | solution.py:1105
  239.7 2.7 fusion.1
  251.8 4.3 %visual_tail.1 = (f32[576,768]{1,0:T(8,128)}, f32[1,768]{1,0:T(1,128)S(1)}, f32[1,768]{1,0:T(1,128)S(1)}) custom-call(bf16[288,768]{1,0:T(8,128)(2,1)S(1)} %collective-permute-done.15.r_ref, bf16[288,768]{1,0:T(8,128)(2,1)S(1)} %copy-done.41, f32[576,768]{1,0:T(8,128)S(1)} %copy-done.4, f32[576,768]{1,0:T(8,128)S(1)} %copy-done.29, ...), custom_call_target="tpu_custom_call" | custom-call | flops 1024 | bytes 1024 | tf_op jit(solution)/shard_map/visual_tail/pallas_call | solution.py:132
  260.6 4.9 %collective-permute-done.25 = bf16[8,144,384]{2,1,0:T(8,128)(2,1)} collective-permute-done((bf16[8,144,384]{2,1,0:T(8,128)(2,1)}, bf16[8,144,384]{2,1,0:T(8,128)(2,1)}, u32[]{:S(2)}, u32[]{:S(2)}) %collective-permute-start.25) | collective-permute-done | bytes 884768 | tf_op jit(solution)/shard_map/ppermute | solution.py:1105
  283.4 15.9 %collective-permute-done.27 = bf16[2,144,768]{2,1,0:T(8,128)(2,1)S(1)} collective-permute-done((bf16[2,144,768]{2,1,0:T(8,128)(2,1)S(1)}, bf16[2,144,768]{2,1,0:T(8,128)(2,1)S(1)}, u32[]{:S(2)}, u32[]{:S(2)}) %collective-permute-start.27) | collective-permute-done | bytes 442400 | tf_op jit(solution)/shard_map/ppermute | solution.py:1101
  310.2 2.9 collective-permute-start.38
  318.0 2.9 collective-permute-start.37
  321.5 3.3 collective-permute-done.37
  (280 shorter events, 119.4 us)
Async XLA Ops:
  6.4 13.3 %collective-permute-start = (bf16[288,768]{1,0:T(8,128)(2,1)}, bf16[288,768]{1,0:T(8,128)(2,1)S(1)}, u32[]{:S(2)}, u32[]{:S(2)}) collective-permute-start(bf16[288,768]{1,0:T(8,128)(2,1)} %get-tuple-element.169), channel_id=1, source_target_pairs={{0,1},{1,0},{2,3},{3,2},{4,5},{5,4},{6,7},{7,6},{8,9},{9,8},{10,11... | collective-permute-start | bytes 1327112 | tf_op jit(solution)/shard_map/ppermute | solution.py:1105
  31.2 13.8 %collective-permute-start.1 = (bf16[288,768]{1,0:T(8,128)(2,1)}, bf16[288,768]{1,0:T(8,128)(2,1)}, u32[]{:S(2)}, u32[]{:S(2)}) collective-permute-start(bf16[288,768]{1,0:T(8,128)(2,1)} %get-tuple-element.172.lc_ref), channel_id=1, source_target_pairs={{0,1},{1,0},{2,3},{3,2},{4,5},{5,4},{6,7},{7,6},{8,9},{9,8},{10,11... | collective-permute-start | bytes 1327112 | tf_op jit(solution)/shard_map/ppermute | solution.py:1105
  91.5 10.9 %collective-permute-start.4 = (bf16[1,8,192,768]{3,2,1,0:T(8,128)(2,1)S(1)}, bf16[1,8,192,768]{3,2,1,0:T(8,128)(2,1)S(1)}, u32[]{:S(2)}, u32[]{:S(2)}) collective-permute-start(bf16[1,8,192,768]{3,2,1,0:T(8,128)(2,1)S(1)} %get-tuple-element.205), channel_id=1, source_target_pairs={{0,2},{2,0},{4,6},{6,4},{8,10},{10,8},{12,14},{14,12},{16,18},{18,... | collective-permute-start | bytes 7077896 | tf_op jit(solution)/shard_map/ppermute | solution.py:1101
  91.6 10.8 %collective-permute-start.3 = (bf16[200,896]{1,0:T(8,128)(2,1)S(1)}, bf16[200,896]{1,0:T(8,128)(2,1)S(1)}, u32[]{:S(2)}, u32[]{:S(2)}) collective-permute-start(bf16[200,896]{1,0:T(8,128)(2,1)S(1)} %get-tuple-element.196.a_ref), channel_id=1, source_target_pairs={{0,1},{1,0},{2,3},{3,2},{4,5},{5,4},{6,7},{7,6},{8,9},{9,8},{10,11... | collective-permute-start | bytes 1075208 | tf_op jit(solution)/shard_map/ppermute | solution.py:1105
  102.8 28.4 %collective-permute-start.7 = (bf16[4,192,768]{2,1,0:T(8,128)(2,1)S(1)}, bf16[4,192,768]{2,1,0:T(8,128)(2,1)S(1)}, u32[]{:S(2)}, u32[]{:S(2)}) collective-permute-start(bf16[4,192,768]{2,1,0:T(8,128)(2,1)S(1)} %fusion.2), channel_id=1, source_target_pairs={{0,4},{2,6},{4,0},{6,2},{8,12},{10,14},{12,8},{14,10},{16,20},{18,... | collective-permute-start | bytes 3538952 | tf_op jit(solution)/shard_map/ppermute | solution.py:1101
  107.6 28.1 %collective-permute-start.6 = (bf16[8,96,768]{2,1,0:T(8,128)(2,1)S(1)}, bf16[8,96,768]{2,1,0:T(8,128)(2,1)S(1)}, u32[]{:S(2)}, u32[]{:S(2)}) collective-permute-start(bf16[8,96,768]{2,1,0:T(8,128)(2,1)S(1)} %fusion.3), channel_id=1, source_target_pairs={{0,1},{1,0},{2,3},{3,2},{4,5},{5,4},{6,7},{7,6},{8,9},{9,8},{10,11... | collective-permute-start | bytes 3538952 | tf_op jit(solution)/shard_map/ppermute | solution.py:1105
  131.4 18.1 %collective-permute-start.10 = (bf16[2,192,768]{2,1,0:T(8,128)(2,1)S(1)}, bf16[2,192,768]{2,1,0:T(8,128)(2,1)S(1)}, u32[]{:S(2)}, u32[]{:S(2)}) collective-permute-start(bf16[2,192,768]{2,1,0:T(8,128)(2,1)S(1)} %fusion.6), channel_id=1, source_target_pairs={{0,8},{2,10},{4,12},{6,14},{8,0},{10,2},{12,4},{14,6},{16,24},{18,... | collective-permute-start | bytes 1769480 | tf_op jit(solution)/shard_map/ppermute | solution.py:1101
  135.9 15.0 %collective-permute-start.9 = (bf16[4,96,768]{2,1,0:T(8,128)(2,1)S(1)}, bf16[4,96,768]{2,1,0:T(8,128)(2,1)S(1)}, u32[]{:S(2)}, u32[]{:S(2)}) collective-permute-start(bf16[4,96,768]{2,1,0:T(8,128)(2,1)S(1)} %fusion.7), channel_id=1, source_target_pairs={{0,4},{2,6},{4,0},{6,2},{8,12},{10,14},{12,8},{14,10},{16,20},{18,... | collective-permute-start | bytes 1769480 | tf_op jit(solution)/shard_map/ppermute | solution.py:1101
  137.5 12.0 %collective-permute-start.11 = (bf16[200,768]{1,0:T(8,128)(2,1)S(1)}, bf16[200,768]{1,0:T(8,128)(2,1)S(1)}, u32[]{:S(2)}, u32[]{:S(2)}) collective-permute-start(bf16[200,768]{1,0:T(8,128)(2,1)S(1)} %get-tuple-element.230), channel_id=1, source_target_pairs={{0,1},{1,0},{2,3},{3,2},{4,5},{5,4},{6,7},{7,6},{8,9},{9,8},{10,11... | collective-permute-start | bytes 921608 | tf_op jit(solution)/shard_map/ppermute | solution.py:1105
  158.5 12.7 %collective-permute-start.13 = (bf16[2,8,96,768]{3,2,1,0:T(8,128)(2,1)S(1)}, bf16[2,8,96,768]{3,2,1,0:T(8,128)(2,1)S(1)}, u32[]{:S(2)}, u32[]{:S(2)}) collective-permute-start(bf16[2,8,96,768]{3,2,1,0:T(8,128)(2,1)S(1)} %get-tuple-element.238), channel_id=1, source_target_pairs={{0,2},{2,0},{4,6},{6,4},{8,10},{10,8},{12,14},{14,12},{16,18},{18,... | collective-permute-start | bytes 7077896 | tf_op jit(solution)/shard_map/ppermute | solution.py:1101
  158.6 12.6 %collective-permute-start.8 = (bf16[288,768]{1,0:T(8,128)(2,1)S(1)}, bf16[288,768]{1,0:T(8,128)(2,1)S(1)}, u32[]{:S(2)}, u32[]{:S(2)}) collective-permute-start(bf16[288,768]{1,0:T(8,128)(2,1)S(1)} %get-tuple-element.228), channel_id=1, source_target_pairs={{0,1},{1,0},{2,3},{3,2},{4,5},{5,4},{6,7},{7,6},{8,9},{9,8},{10,11... | collective-permute-start | bytes 1327112 | tf_op jit(solution)/shard_map/ppermute | solution.py:1105
  160.2 17.7 %collective-permute-start.17 = (bf16[1,192,768]{2,1,0:T(8,128)(2,1)S(1)}, bf16[1,192,768]{2,1,0:T(8,128)(2,1)S(1)}, u32[]{:S(2)}, u32[]{:S(2)}) collective-permute-start(bf16[1,192,768]{2,1,0:T(8,128)(2,1)S(1)} %fusion.19), channel_id=1, source_target_pairs={{0,16},{2,18},{4,20},{6,22},{8,24},{10,26},{12,28},{14,30},{16,0},... | collective-permute-start | bytes 884744 | tf_op jit(solution)/shard_map/ppermute | solution.py:1101
  162.8 14.0 %collective-permute-start.12 = (bf16[2,96,768]{2,1,0:T(8,128)(2,1)S(1)}, bf16[2,96,768]{2,1,0:T(8,128)(2,1)S(1)}, u32[]{:S(2)}, u32[]{:S(2)}) collective-permute-start(bf16[2,96,768]{2,1,0:T(8,128)(2,1)S(1)} %fusion.21), channel_id=1, source_target_pairs={{0,8},{2,10},{4,12},{6,14},{8,0},{10,2},{12,4},{14,6},{16,24},{18,... | collective-permute-start | bytes 884744 | tf_op jit(solution)/shard_map/ppermute | solution.py:1101
  184.9 34.5 %collective-permute-start.16 = (bf16[8,96,768]{2,1,0:T(8,128)(2,1)S(1)}, bf16[8,96,768]{2,1,0:T(8,128)(2,1)S(1)}, u32[]{:S(2)}, u32[]{:S(2)}) collective-permute-start(bf16[8,96,768]{2,1,0:T(8,128)(2,1)S(1)} %fusion.4), channel_id=1, source_target_pairs={{0,1},{1,0},{2,3},{3,2},{4,5},{5,4},{6,7},{7,6},{8,9},{9,8},{10,11... | collective-permute-start | bytes 3538952 | tf_op jit(solution)/shard_map/ppermute | solution.py:1105
  198.1 41.6 %collective-permute-start.21 = (bf16[4,288,768]{2,1,0:T(8,128)(2,1)}, bf16[4,288,768]{2,1,0:T(8,128)(2,1)}, u32[]{:S(2)}, u32[]{:S(2)}) collective-permute-start(bf16[4,288,768]{2,1,0:T(8,128)(2,1)} %fusion), channel_id=1, source_target_pairs={{0,4},{2,6},{4,0},{6,2},{8,12},{10,14},{12,8},{14,10},{16,20},{18,... | collective-permute-start | bytes 5308424 | tf_op jit(solution)/shard_map/ppermute | solution.py:1101
  225.0 17.5 %collective-permute-start.19 = (bf16[2,8,144,384]{3,2,1,0:T(8,128)(2,1)}, bf16[2,8,144,384]{3,2,1,0:T(8,128)(2,1)}, u32[]{:S(2)}, u32[]{:S(2)}) collective-permute-start(bf16[2,8,144,384]{3,2,1,0:T(8,128)(2,1)} %get-tuple-element.281), channel_id=1, source_target_pairs={{0,2},{2,0},{4,6},{6,4},{8,10},{10,8},{12,14},{14,12},{16,18},{18,... | collective-permute-start | bytes 5308424 | tf_op jit(solution)/shard_map/ppermute | solution.py:1101
  225.0 21.8 %collective-permute-start.18 = (bf16[1,8,144,768]{3,2,1,0:T(8,128)(2,1)}, bf16[1,8,144,768]{3,2,1,0:T(8,128)(2,1)}, u32[]{:S(2)}, u32[]{:S(2)}) collective-permute-start(bf16[1,8,144,768]{3,2,1,0:T(8,128)(2,1)} %get-tuple-element.277), channel_id=1, source_target_pairs={{0,2},{2,0},{4,6},{6,4},{8,10},{10,8},{12,14},{14,12},{16,18},{18,... | collective-permute-start | bytes 5308424 | tf_op jit(solution)/shard_map/ppermute | solution.py:1101
  226.4 23.8 %collective-permute-start.15 = (bf16[288,768]{1,0:T(8,128)(2,1)}, bf16[288,768]{1,0:T(8,128)(2,1)S(1)}, u32[]{:S(2)}, u32[]{:S(2)}) collective-permute-start(bf16[288,768]{1,0:T(8,128)(2,1)} %copy-done.49), channel_id=1, source_target_pairs={{0,1},{1,0},{2,3},{3,2},{4,5},{5,4},{6,7},{7,6},{8,9},{9,8},{10,11... | collective-permute-start | bytes 1327112 | tf_op jit(solution)/shard_map/ppermute | solution.py:1105
  235.7 23.5 %collective-permute-start.26 = (bf16[4,96,768]{2,1,0:T(8,128)(2,1)}, bf16[4,96,768]{2,1,0:T(8,128)(2,1)}, u32[]{:S(2)}, u32[]{:S(2)}) collective-permute-start(bf16[4,96,768]{2,1,0:T(8,128)(2,1)} %fusion.5), channel_id=1, source_target_pairs={{0,4},{2,6},{4,0},{6,2},{8,12},{10,14},{12,8},{14,10},{16,20},{18,... | collective-permute-start | bytes 1769480 | tf_op jit(solution)/shard_map/ppermute | solution.py:1101
  242.4 27.3 %collective-permute-start.23 = (bf16[2,288,768]{2,1,0:T(8,128)(2,1)}, bf16[2,288,768]{2,1,0:T(8,128)(2,1)}, u32[]{:S(2)}, u32[]{:S(2)}) collective-permute-start(bf16[2,288,768]{2,1,0:T(8,128)(2,1)} %fusion.1), channel_id=1, source_target_pairs={{0,8},{2,10},{4,12},{6,14},{8,0},{10,2},{12,4},{14,6},{16,24},{18,... | collective-permute-start | bytes 2654216 | tf_op jit(solution)/shard_map/ppermute | solution.py:1101
  245.0 20.5 %collective-permute-start.25 = (bf16[8,144,384]{2,1,0:T(8,128)(2,1)}, bf16[8,144,384]{2,1,0:T(8,128)(2,1)}, u32[]{:S(2)}, u32[]{:S(2)}) collective-permute-start(bf16[8,144,384]{2,1,0:T(8,128)(2,1)} %fusion.8), channel_id=1, source_target_pairs={{0,1},{1,0},{2,3},{3,2},{4,5},{5,4},{6,7},{7,6},{8,9},{9,8},{10,11... | collective-permute-start | bytes 2654216 | tf_op jit(solution)/shard_map/ppermute | solution.py:1105
  249.3 22.9 %collective-permute-start.22 = (bf16[4,144,768]{2,1,0:T(8,128)(2,1)}, bf16[4,144,768]{2,1,0:T(8,128)(2,1)}, u32[]{:S(2)}, u32[]{:S(2)}) collective-permute-start(bf16[4,144,768]{2,1,0:T(8,128)(2,1)} %fusion.9), channel_id=1, source_target_pairs={{0,4},{2,6},{4,0},{6,2},{8,12},{10,14},{12,8},{14,10},{16,20},{18,... | collective-permute-start | bytes 2654216 | tf_op jit(solution)/shard_map/ppermute | solution.py:1101
  250.1 28.5 %collective-permute-start.43 = (bf16[96,768]{1,0:T(8,128)(2,1)}, bf16[96,768]{1,0:T(8,128)(2,1)}, u32[]{:S(2)}, u32[]{:S(2)}) collective-permute-start(bf16[96,768]{1,0:T(8,128)(2,1)} %fusion.32), channel_id=1, source_target_pairs={{0,1},{1,0},{2,3},{3,2},{4,5},{5,4},{6,7},{7,6},{8,9},{9,8},{10,11... | collective-permute-start | bytes 442376 | tf_op jit(solution)/shard_map/ppermute | solution.py:1105
  268.5 11.5 %collective-permute-start.29 = (bf16[4,144,384]{2,1,0:T(8,128)(2,1)S(1)}, bf16[4,144,384]{2,1,0:T(8,128)(2,1)S(1)}, u32[]{:S(2)}, u32[]{:S(2)}) collective-permute-start(bf16[4,144,384]{2,1,0:T(8,128)(2,1)S(1)} %fusion.12), channel_id=1, source_target_pairs={{0,4},{2,6},{4,0},{6,2},{8,12},{10,14},{12,8},{14,10},{16,20},{18,... | collective-permute-start | bytes 1327112 | tf_op jit(solution)/shard_map/ppermute | solution.py:1101
  269.7 13.6 %collective-permute-start.28 = (f32[8,768]{1,0:T(8,128)S(1)}, f32[8,768]{1,0:T(8,128)S(1)}, u32[]{:S(2)}, u32[]{:S(2)}) collective-permute-start(f32[8,768]{1,0:T(8,128)S(1)} %add.423), channel_id=1, source_target_pairs={{0,4},{2,6},{4,0},{6,2},{8,12},{10,14},{12,8},{14,10},{16,20},{18,... | collective-permute-start | bytes 73736 | tf_op jit(solution)/shard_map/ppermute | solution.py:1101
  272.2 31.7 %collective-permute-start.33 = (bf16[1,288,768]{2,1,0:T(8,128)(2,1)S(1)}, bf16[1,288,768]{2,1,0:T(8,128)(2,1)S(1)}, u32[]{:S(2)}, u32[]{:S(2)}) collective-permute-start(bf16[1,288,768]{2,1,0:T(8,128)(2,1)S(1)} %fusion.14), channel_id=1, source_target_pairs={{0,16},{2,18},{4,20},{6,22},{8,24},{10,26},{12,28},{14,30},{16,0},... | collective-permute-start | bytes 1327112 | tf_op jit(solution)/shard_map/ppermute | solution.py:1101
  275.7 23.6 %collective-permute-start.27 = (bf16[2,144,768]{2,1,0:T(8,128)(2,1)S(1)}, bf16[2,144,768]{2,1,0:T(8,128)(2,1)S(1)}, u32[]{:S(2)}, u32[]{:S(2)}) collective-permute-start(bf16[2,144,768]{2,1,0:T(8,128)(2,1)S(1)} %fusion.11), channel_id=1, source_target_pairs={{0,8},{2,10},{4,12},{6,14},{8,0},{10,2},{12,4},{14,6},{16,24},{18,... | collective-permute-start | bytes 1327112 | tf_op jit(solution)/shard_map/ppermute | solution.py:1101
  278.6 22.1 %collective-permute-start.35 = (bf16[1,96,768]{2,1,0:T(8,128)(2,1)S(1)}, bf16[1,96,768]{2,1,0:T(8,128)(2,1)S(1)}, u32[]{:S(2)}, u32[]{:S(2)}) collective-permute-start(bf16[1,96,768]{2,1,0:T(8,128)(2,1)S(1)} %fusion.35), channel_id=1, source_target_pairs={{0,16},{2,18},{4,20},{6,22},{8,24},{10,26},{12,28},{14,30},{16,0},... | collective-permute-start | bytes 442376 | tf_op jit(solution)/shard_map/ppermute | solution.py:1101
  281.2 27.9 %collective-permute-start.32 = (bf16[2,144,384]{2,1,0:T(8,128)(2,1)S(1)}, bf16[2,144,384]{2,1,0:T(8,128)(2,1)S(1)}, u32[]{:S(2)}, u32[]{:S(2)}) collective-permute-start(bf16[2,144,384]{2,1,0:T(8,128)(2,1)S(1)} %fusion.26), channel_id=1, source_target_pairs={{0,8},{2,10},{4,12},{6,14},{8,0},{10,2},{12,4},{14,6},{16,24},{18,... | collective-permute-start | bytes 663560 | tf_op jit(solution)/shard_map/ppermute | solution.py:1101
  283.3 26.8 %collective-permute-start.31 = (f32[8,768]{1,0:T(8,128)S(1)}, f32[8,768]{1,0:T(8,128)S(1)}, u32[]{:S(2)}, u32[]{:S(2)}) collective-permute-start(f32[8,768]{1,0:T(8,128)S(1)} %add.433), channel_id=1, source_target_pairs={{0,8},{2,10},{4,12},{6,14},{8,0},{10,2},{12,4},{14,6},{16,24},{18,... | collective-permute-start | bytes 73736 | tf_op jit(solution)/shard_map/ppermute | solution.py:1101
  300.5 12.6 %collective-permute-start.30 = (bf16[1,144,768]{2,1,0:T(8,128)(2,1)S(1)}, bf16[1,144,768]{2,1,0:T(8,128)(2,1)S(1)}, u32[]{:S(2)}, u32[]{:S(2)}) collective-permute-start(bf16[1,144,768]{2,1,0:T(8,128)(2,1)S(1)} %fusion.24), channel_id=1, source_target_pairs={{0,16},{2,18},{4,20},{6,22},{8,24},{10,26},{12,28},{14,30},{16,0},... | collective-permute-start | bytes 663560 | tf_op jit(solution)/shard_map/ppermute | solution.py:1101
  305.4 22.1 %collective-permute-start.40 = (bf16[288,768]{1,0:T(8,128)(2,1)S(1)}, bf16[288,768]{1,0:T(8,128)(2,1)S(1)}, u32[]{:S(2)}, u32[]{:S(2)}) collective-permute-start(bf16[288,768]{1,0:T(8,128)(2,1)S(1)} %fusion.10), channel_id=1, source_target_pairs={{0,1},{1,0},{2,3},{3,2},{4,5},{5,4},{6,7},{7,6},{8,9},{9,8},{10,11... | collective-permute-start | bytes 1327112 | tf_op jit(solution)/shard_map/ppermute | solution.py:1105
  (82 other events, 915.4 us)
